TPU v7x, 32 devices: a whole 2x2x4 slice. The times are simulated.
32 devices in a mesh: dp: 4 (over z), seq: 8 (over y, x, core).
Axes of the slice: x: 2, y: 2, z: 4, core: 2. Of those that a mesh axis runs over, the one named last changes fastest.
Arguments:
- streams: bfloat16 [4, 1024, 4, 2048], P('dp', 'seq'), may hold values from -6 to 6
- segments: int32 [4, 1024], P('dp', 'seq'), may hold values from 0 to 3, as said below
- positions: int32 [4, 1024], P('dp', 'seq'), may hold values from 0 to 1023, as said below
- att_proj: bfloat16 [2048, 6144], P(('dp', 'seq')), may hold values from -0.125 to 0.125
- attn_out: bfloat16 [2048, 2048], P(('dp', 'seq')), may hold values from -1 to 1
- ff_proj: bfloat16 [2048, 16384], P(('dp', 'seq')), may hold values from -0.125 to 0.125
- ff_out: bfloat16 [8192, 2048], P(('dp', 'seq')), may hold values from -0.0625 to 0.0625
- mix_in: float32 [2, 4], replicated, may hold values from 0.25 to 0.75
- mix_res: float32 [2, 4, 4], replicated, may hold values from -0.45 to 1.45
- depth: float32 [2, 4], replicated, may hold values from 0.5 to 1.5
- cotangent: bfloat16 [4, 1024, 4, 2048], P('dp', 'seq'), may hold values from -6 to 6
Outputs:
- streams_out: bfloat16 [4, 1024, 4, 2048], P('dp', 'seq')
- grad_streams: float32 [4, 1024, 4, 2048], P('dp', 'seq')
- grad_att_proj: float32 [2048, 6144], P(('dp', 'seq'))
- grad_attn_out: float32 [2048, 2048], P(('dp', 'seq'))
- grad_ff_proj: float32 [2048, 16384], P(('dp', 'seq'))
- grad_ff_out: float32 [8192, 2048], P(('dp', 'seq'))
- grad_mix_in: float32 [2, 4], replicated
- grad_mix_res: float32 [2, 4, 4], replicated
- grad_depth: float32 [2, 4], replicated
Inputs may be any that keep to these rules, and one draw needn't show every extreme that they name: `segments`: 0 marks text; each sequence holds 3 picture pieces numbered 1 to 3, each 256 consecutive tokens; the last token of each sequence is text. `positions`: a text token's position is its index in its sequence; every token of a picture piece has the index of the piece's first token; the last token of each sequence is text.
All inputs are finite; a program needn't handle non-finite values.
Results may differ from a plain program's by a relative error of at most 0.035.
Values may be sent and summed in bfloat16 or wider, within the bound.
A program may use at most 512 MiB of HBM per device.

v0:
```python
import jax
import jax.numpy as jnp
from jax import lax
from jax.sharding import PartitionSpec as P

HEADS = 16
HEAD_DIM = 128
FF = 8192


ln_eps = 1e-05
rope_base = 10000.0
neg_big = -1e30
group_count = 4
highest = lax.Precision.HIGHEST


def layer_norm(values):
    row_mean = jnp.mean(values, axis=-1, keepdims=True)
    centered = values - row_mean
    row_var = jnp.mean(centered * centered, axis=-1, keepdims=True)
    return centered * lax.rsqrt(row_var + ln_eps)


def rope_tables(positions, head_dim):
    half_dim = head_dim // 2
    inv_freq = rope_base ** (-(jnp.arange(half_dim, dtype=jnp.float32) * 2.0 / head_dim))
    angles = positions.astype(jnp.float32)[..., None] * inv_freq
    angles = jnp.concatenate([angles, angles], axis=-1)
    return (jnp.cos(angles), jnp.sin(angles))


def rotate(values, cosine, sine_table):
    half_dim = values.shape[-1] // 2
    turned = jnp.concatenate([-values[..., half_dim:], values[..., :half_dim]], axis=-1)
    return values * cosine + turned * sine_table


def mix_streams(streams_in, weights):
    return jnp.sum(streams_in * weights[None, :, None], axis=1)


def cross_streams(streams_in, matrix):
    return jnp.einsum("rid,ij->rjd", streams_in, matrix, precision=highest)


def to_groups(values):
    seq_count, tok_count, head_count, head_dim = values.shape
    return values.reshape(
        seq_count, tok_count, group_count, head_count // group_count, head_dim
    ).transpose(2, 0, 1, 3, 4)


def from_groups(values):
    group_total, seq_count, tok_count, per_group, head_dim = values.shape
    return values.transpose(1, 2, 0, 3, 4).reshape(
        seq_count, tok_count, group_total * per_group, head_dim
    )


def project(inputs, weight):
    return jnp.dot(
        inputs,
        lax.all_gather(weight, ("dp", "seq"), axis=0, tiled=True),
        preferred_element_type=jnp.float32,
    )


def project_back(grad_rows, weight):
    contract = (((1,), (1,)), ((), ()))
    return lax.dot_general(
        grad_rows,
        lax.all_gather(weight, ("dp", "seq"), axis=0, tiled=True),
        contract,
        preferred_element_type=jnp.float32,
    )


def weight_grad(inputs, grad_rows):
    return lax.psum_scatter(
        lax.dot_general(
            inputs, grad_rows, (((0,), (0,)), ((), ())), preferred_element_type=jnp.float32
        ),
        ("dp", "seq"),
        scatter_dimension=0,
        tiled=True,
    )


def body(
    streams,
    segments,
    positions,
    att_proj,
    attn_out,
    ff_proj,
    ff_out,
    mix_in,
    mix_res,
    depth,
    cotangent,
):
    seq_count, tok_count, stream_count, width = streams.shape
    row_count = seq_count * tok_count
    score_scale = HEAD_DIM ** (-0.5)
    query_index = lax.axis_index("seq") * tok_count + jnp.arange(tok_count, dtype=jnp.int32)
    seg_query = segments.astype(jnp.float32)
    cosine, sine_table = rope_tables(positions, HEAD_DIM)
    cosine = cosine[:, :, None, :]
    sine_table = sine_table[:, :, None, :]

    def allowed_mask(seg_keys):
        key_index = jnp.arange(seg_keys.shape[1], dtype=jnp.int32)
        causal = key_index[None, None, :] <= query_index[None, :, None]
        same_piece = (seg_keys.astype(jnp.float32)[:, None, :] == seg_query[:, :, None]) & (
            seg_query[:, :, None] > 0.5
        )
        return (causal | same_piece)[:, None]

    def roped(projected):
        pieces = projected.reshape(seq_count, tok_count, 3, HEADS, HEAD_DIM)
        queries = rotate(pieces[:, :, 0], cosine, sine_table)
        keys_rot = rotate(pieces[:, :, 1], cosine, sine_table)
        return (queries, keys_rot, pieces[:, :, 2])

    def swiglu(upgate):
        return jax.nn.silu(upgate[:, FF:]) * upgate[:, :FF]

    state_in = streams.astype(jnp.float32).reshape(row_count, stream_count, width)
    mixed_att = mix_streams(state_in, mix_in[0])
    normed_att, norm_back_att = jax.vjp(layer_norm, mixed_att)
    normed_att = normed_att.astype(jnp.bfloat16)
    projected = project(normed_att, att_proj)
    (queries, keys_rot, values_in), rope_back = jax.vjp(roped, projected)
    query_low = to_groups(queries.astype(jnp.bfloat16))
    key_low = to_groups(keys_rot.astype(jnp.bfloat16))
    value_low = to_groups(values_in.astype(jnp.bfloat16))
    seg_send = segments.astype(jnp.bfloat16)[None]
    group_shape = (group_count, seq_count, HEADS // group_count, tok_count)
    initial = (
        jnp.full(group_shape, neg_big, jnp.float32),
        jnp.zeros(group_shape, jnp.float32),
        jnp.zeros(group_shape + (HEAD_DIM,), jnp.float32),
    )
    keys_part = lax.all_gather(key_low, "seq", axis=2, tiled=True)
    values_part = lax.all_gather(value_low, "seq", axis=2, tiled=True)
    seg_part = lax.all_gather(seg_send, "seq", axis=2, tiled=True)
    allowed = allowed_mask(seg_part[0])

    def group_step(group_args):
        query_group, key_group, value_group, top_score, weight_sum, out_sum = group_args
        scores = (
            jnp.einsum(
                "sqhd,skhd->shqk", query_group, key_group, preferred_element_type=jnp.float32
            )
            * score_scale
        )
        scores = jnp.where(allowed, scores, neg_big)
        top_new = jnp.maximum(top_score, jnp.max(scores, axis=-1))
        weights_exp = jnp.where(allowed, jnp.exp(scores - top_new[..., None]), 0.0)
        shrink = jnp.exp(top_score - top_new)
        sum_new = weight_sum * shrink + jnp.sum(weights_exp, axis=-1)
        out_new = out_sum * shrink[..., None] + jnp.einsum(
            "shqk,skhd->shqd",
            weights_exp.astype(jnp.bfloat16),
            value_group,
            preferred_element_type=jnp.float32,
        )
        return (top_new, sum_new, out_new)

    top_score, weight_sum, out_sum = lax.map(
        group_step, (query_low, keys_part, values_part) + tuple(initial)
    )
    attended = from_groups(jnp.swapaxes(out_sum / weight_sum[..., None], 2, 3))
    attended_low = attended.reshape(row_count, width).astype(jnp.bfloat16)
    log_total = top_score + jnp.log(weight_sum)
    branch_att = project(attended_low, attn_out)
    state_mid = (
        cross_streams(state_in, mix_res[0]) + depth[0][None, :, None] * branch_att[:, None, :]
    )
    mixed_ff = mix_streams(state_mid, mix_in[1])
    normed_ff, norm_back_ff = jax.vjp(layer_norm, mixed_ff)
    normed_ff = normed_ff.astype(jnp.bfloat16)
    upgate = project(normed_ff, ff_proj)
    hidden, swiglu_back = jax.vjp(swiglu, upgate)
    hidden = hidden.astype(jnp.bfloat16)
    branch_ff = project(hidden, ff_out)
    state_out = (
        cross_streams(state_mid, mix_res[1]) + depth[1][None, :, None] * branch_ff[:, None, :]
    )
    streams_out = state_out.astype(jnp.bfloat16).reshape(streams.shape)
    grad_out = cotangent.astype(jnp.float32).reshape(row_count, stream_count, width)
    grad_depth_ff = jnp.sum(branch_ff[:, None, :] * grad_out, axis=(0, 2))
    grad_res_ff = jnp.einsum("rid,rjd->ij", state_mid, grad_out, precision=highest)
    grad_mid = jnp.einsum("rjd,ij->rid", grad_out, mix_res[1], precision=highest)
    grad_branch_ff = mix_streams(grad_out, depth[1]).astype(jnp.bfloat16)
    grad_hidden = project_back(grad_branch_ff, ff_out)
    grad_ff_out = weight_grad(hidden, grad_branch_ff)
    grad_upgate = swiglu_back(grad_hidden)[0].astype(jnp.bfloat16)
    grad_normed_ff = project_back(grad_upgate, ff_proj)
    grad_ff_proj = weight_grad(normed_ff, grad_upgate)
    grad_mixed_ff = norm_back_ff(grad_normed_ff)[0]
    grad_mid = grad_mid + mix_in[1][None, :, None] * grad_mixed_ff[:, None, :]
    grad_in_ff = jnp.sum(state_mid * grad_mixed_ff[:, None, :], axis=(0, 2))
    grad_depth_att = jnp.sum(branch_att[:, None, :] * grad_mid, axis=(0, 2))
    grad_res_att = jnp.einsum("rid,rjd->ij", state_in, grad_mid, precision=highest)
    grad_in_streams = jnp.einsum("rjd,ij->rid", grad_mid, mix_res[0], precision=highest)
    grad_branch_att = mix_streams(grad_mid, depth[0]).astype(jnp.bfloat16)
    grad_attended = project_back(grad_branch_att, attn_out)
    grad_attn_out = weight_grad(attended_low, grad_branch_att)
    grad_att_low = to_groups(
        grad_attended.reshape(seq_count, tok_count, HEADS, HEAD_DIM).astype(jnp.bfloat16)
    )
    key_source = (
        lax.all_gather(key_low, "seq", axis=2, tiled=True),
        lax.all_gather(value_low, "seq", axis=2, tiled=True),
        lax.all_gather(seg_send, "seq", axis=2, tiled=True),
    )
    keys_again, values_again, seg_again = key_source
    allowed_all = allowed_mask(seg_again[0])

    def back_group(group_args):
        query_group, key_group, value_group, grad_group, log_group = group_args
        scores = (
            jnp.einsum(
                "sqhd,skhd->shqk", query_group, key_group, preferred_element_type=jnp.float32
            )
            * score_scale
        )
        scores = jnp.where(allowed_all, scores, neg_big)
        attn_probs = jnp.exp(scores - log_group[..., None])
        grad_value = jnp.einsum(
            "shqk,sqhd->skhd",
            attn_probs.astype(jnp.bfloat16),
            grad_group,
            preferred_element_type=jnp.float32,
        )
        grad_probs = jnp.einsum(
            "sqhd,skhd->shqk", grad_group, value_group, preferred_element_type=jnp.float32
        )
        row_dot = jnp.sum(attn_probs * grad_probs, axis=-1, keepdims=True)
        grad_scores = (attn_probs * (grad_probs - row_dot)).astype(jnp.bfloat16)
        grad_query = (
            jnp.einsum(
                "shqk,skhd->sqhd", grad_scores, key_group, preferred_element_type=jnp.float32
            )
            * score_scale
        )
        grad_key = (
            jnp.einsum(
                "shqk,sqhd->skhd", grad_scores, query_group, preferred_element_type=jnp.float32
            )
            * score_scale
        )
        return (grad_query, grad_key, grad_value)

    grad_query, grad_key, grad_value = lax.map(
        back_group, (query_low, keys_again, values_again, grad_att_low, log_total)
    )
    grad_key, grad_value = (
        lax.psum_scatter(
            grad_key.astype(jnp.bfloat16), "seq", scatter_dimension=2, tiled=True
        ).astype(jnp.float32),
        lax.psum_scatter(
            grad_value.astype(jnp.bfloat16), "seq", scatter_dimension=2, tiled=True
        ).astype(jnp.float32),
    )
    grad_projected = rope_back(
        (from_groups(grad_query), from_groups(grad_key), from_groups(grad_value))
    )[0].astype(jnp.bfloat16)
    grad_normed_att = project_back(grad_projected, att_proj)
    grad_att_proj = weight_grad(normed_att, grad_projected)
    grad_mixed_att = norm_back_att(grad_normed_att)[0]
    grad_in_streams = grad_in_streams + mix_in[0][None, :, None] * grad_mixed_att[:, None, :]
    grad_in_att = jnp.sum(state_in * grad_mixed_att[:, None, :], axis=(0, 2))
    grad_mix_in, grad_mix_res, grad_depth = lax.psum(
        (
            jnp.stack([grad_in_att, grad_in_ff]),
            jnp.stack([grad_res_att, grad_res_ff]),
            jnp.stack([grad_depth_att, grad_depth_ff]),
        ),
        ("dp", "seq"),
    )
    return (
        streams_out,
        grad_in_streams.reshape(streams.shape),
        grad_att_proj,
        grad_attn_out,
        grad_ff_proj,
        grad_ff_out,
        grad_mix_in,
        grad_mix_res,
        grad_depth,
    )


def solution(mesh):
    placed = (
        P("dp", "seq", None, None),
        P("dp", "seq"),
        P("dp", "seq"),
        P(("dp", "seq"), None),
        P(("dp", "seq"), None),
        P(("dp", "seq"), None),
        P(("dp", "seq"), None),
        P(),
        P(),
        P(),
        P("dp", "seq", None, None),
    )
    return jax.shard_map(
        body,
        mesh=mesh,
        in_specs=placed,
        out_specs=(
            P("dp", "seq", None, None),
            P("dp", "seq", None, None),
            P(("dp", "seq"), None),
            P(("dp", "seq"), None),
            P(("dp", "seq"), None),
            P(("dp", "seq"), None),
            P(),
            P(),
            P(),
        ),
        check_vma=False,
    )
```

profile of v0, /device:TPU:14, one launch (start us, length us, event | category | flops | bytes accessed | tf_op | source)
XLA Modules:
  0.0 3919.1 jit_solution(8692249105864490426)
XLA Ops:
  9.8 5.0 fusion.57
  15.2 148.2 %all-gather.8.cloned.1.call-done = bf16[2048,6144]{1,0:T(8,128)(2,1)} async-done(((bf16[64,6144]{1,0:T(8,128)(2,1)}), bf16[2048,6144]{1,0:T(8,128)(2,1)}) %all-gather.8.cloned.1.call-update) | async-done | bytes 25165840 | tf_op jit(solution)/shard_map/all_gather | solution.py:64
  163.4 16.3 fusion.111
  179.7 3.0 fusion.115
  185.6 2.4 copy.87
  187.9 2.4 copy.88
  190.3 2.5 copy.83
  194.1 3.6 fusion.86
  197.7 9.3 all-gather.12.cloned.1.call-start
  211.3 8.6 all-gather
  220.0 14.3 all-gather.10.cloned.1.call-done
  234.3 39.1 all-gather.12.cloned.1.call-done
  273.4 22.6 while.30
  297.4 55.9 %all-gather.14.cloned.1.call-done = bf16[2048,2048]{1,0:T(8,128)(2,1)} async-done(((bf16[64,2048]{1,0:T(8,128)(2,1)}), bf16[2048,2048]{1,0:T(8,128)(2,1)}) %all-gather.14.cloned.1.call-update) | async-done | bytes 8388624 | tf_op jit(solution)/shard_map/all_gather | solution.py:64
  353.3 4.8 fusion.119
  358.2 10.0 multiply_reduce_fusion.4
  368.5 339.9 %all-gather.16.cloned.1.call-done = bf16[2048,16384]{1,0:T(8,128)(2,1)} async-done(((bf16[64,16384]{1,0:T(8,128)(2,1)}), bf16[2048,16384]{1,0:T(8,128)(2,1)}) %all-gather.16.cloned.1.call-update) | async-done | bytes 67108880 | tf_op jit(solution)/shard_map/all_gather | solution.py:64
  708.4 27.2 fusion.112
  735.7 6.0 multiply_convert_fusion.1
  741.6 161.9 %all-gather.18.cloned.1.call-done = bf16[8192,2048]{1,0:T(8,128)(2,1)} async-done(((bf16[256,2048]{1,0:T(8,128)(2,1)}), bf16[8192,2048]{1,0:T(8,128)(2,1)}) %all-gather.18.cloned.1.call-update) | async-done | bytes 33554448 | tf_op jit(solution)/shard_map/all_gather | solution.py:64
  903.5 13.8 fusion.120
  918.3 5.3 fusion.61
  923.6 21.9 fusion.88
  945.5 30.7 multiply_reduce_fusion.7
  978.4 10.0 multiply_reduce_fusion.1
  988.4 2.9 convolution_convert_fusion
  993.7 50.2 %while.31 = (s32[]{:T(128)}, f32[4,1,128,4,128]{2,4,3,1,0:T(8,128)}, bf16[4,1,1024,4,128]{2,4,3,1,0:T(8,128)(2,1)}, bf16[4,1,1024,4,128]{2,4,3,1,0:T(8,128)(2,1)...) while((s32[]{:T(128)}, ...), condition=%wide.region_16.17_spmd.clone, body=%wide.region_14.16_spmd.clone.sunk | while | flops 676920832 | bytes 91246960 | solution.py:257
  995.6 2.3 multiply_reduce_fusion.11
  998.7 2.5 copy-done.11
  1001.7 2.0 copy-done.12
  1003.8 2.5 fusion.184
  1008.2 2.3 multiply_reduce_fusion.11
  1011.2 2.5 copy-done.11
  1014.3 2.0 copy-done.12
  1016.3 2.5 fusion.184
  1020.7 2.3 multiply_reduce_fusion.11
  1023.8 2.5 copy-done.11
  1026.8 2.0 copy-done.12
  1028.9 2.5 fusion.184
  1033.3 2.3 multiply_reduce_fusion.11
  1036.3 2.5 copy-done.11
  1039.4 2.0 copy-done.12
  1041.4 2.5 fusion.184
  1043.9 7.9 copy.106
  1051.8 7.8 reshape.754
  1059.7 7.9 copy.104
  1067.6 8.1 reshape.752
  1075.9 8.6 fusion.121
  1085.5 25.4 reduce-scatter.22.cloned.1.call-done
  1112.9 52.5 %reduce-scatter.20.cloned.1.call-done = bf16[128,2048]{1,0:T(8,128)(2,1)} async-done(((bf16[1024,2048]{1,0:T(8,128)(2,1)}), bf16[128,2048]{1,0:T(8,128)(2,1)}) %reduce-scatter.20.cloned.1.call-update) | async-done | bytes 524304
  1172.9 21.3 fusion.110
  1195.2 25.5 fusion.122
  1220.8 48.6 %fusion.84 = f32[2048,16384]{1,0:T(8,128)} fusion(f32[128,8192]{1,0:T(8,128)} %get-tuple-element.245, f32[128,8192]{1,0:T(8,128)} %get-tuple-element.244, f32[128,2048]{1,0:T(8,128)S(1)} %get-tuple-element.174, f32[128]{0:T(128)S(1)} %fusion.107, f32[128]{0:T(128)S(1)} %broadcast_multiply_fusion.3), kind=kOutput, calls=%fused_computation.128 | convolution fusion | flops 8594915328 | bytes 143655936 | tf_op jit(solution)/shard_map/dot_general | solution.py:81
  1271.0 12.0 fusion.77
  1283.0 9.1 fusion.74
  1292.2 4.9 multiply_reduce_fusion.2
  1297.2 14.7 multiply_reduce_fusion.6
  1313.9 2.3 fusion.59
  1316.3 9.4 fusion.67
  1325.7 43.1 %all-reduce.10 = (f32[2,4]{1,0:T(2,128)}, f32[2,4,4]{2,1,0:T(4,128)}, f32[2,4]{1,0:T(2,128)}) all-reduce(f32[2,4]{1,0:T(2,128)S(1)} %pad_maximum_fusion.2, f32[2,4,4]{2,1,0:T(4,128)S(1)} %pad_maximum_fusion.1, f32[2,4]{1,0:T(2,128)S(1)} %pad_maximum_fusion.3), channel_id=1, replica_groups=mesh['dp'=4,'seq'=8] {'dp','seq'}, use_global_device_ids=true, to_apply=%region_27.28 | all-reduce | flops 48 | bytes 384 | tf_op jit(solution)/shard_map/psum | solution.py:276
  1368.8 11.0 fusion.64
  1379.8 409.9 %reduce-scatter.14.cloned.1.call-done = f32[64,6144]{1,0:T(8,128)} async-done(((f32[2048,6144]{1,0:T(8,128)}), f32[64,6144]{1,0:T(8,128)}) %reduce-scatter.14.cloned.1.call-update) | async-done | bytes 1572880 | tf_op jit(solution)/shard_map/reduce_scatter | solution.py:80
  1789.7 712.6 %reduce-scatter.18.cloned.1.call-done = f32[256,2048]{1,0:T(8,128)} async-done(((f32[8192,2048]{1,0:T(8,128)}), f32[256,2048]{1,0:T(8,128)}) %reduce-scatter.18.cloned.1.call-update) | async-done | bytes 2097168 | tf_op jit(solution)/shard_map/reduce_scatter | solution.py:80
  2502.2 1409.8 %reduce-scatter.24.cloned.1.call-done = f32[64,16384]{1,0:T(8,128)} async-done(((f32[2048,16384]{1,0:T(8,128)}), f32[64,16384]{1,0:T(8,128)}) %reduce-scatter.24.cloned.1.call-update) | async-done | bytes 4194320
  (261 shorter events, 68.7 us)
Async XLA Ops:
  7.2 156.2 %all-gather.8.cloned.1.call-start = ((), (), s32[]{:S(2)}) async-start(), calls=%async_computation.6 | async-start | bytes 25952256 | tf_op jit(solution)/shard_map/all_gather | solution.py:64
  7.9 226.4 %all-gather.10.cloned.1.call-start = ((), (), s32[]{:S(2)}) async-start(), calls=%async_computation.7 | async-start | bytes 4718592 | tf_op jit(solution)/shard_map/all_gather | solution.py:145
  9.0 185.1 %copy-start.23 = (f32[128,128]{1,0:T(8,128)}, f32[128,128]{1,0:T(8,128)S(1)}, u32[]{:S(2)}) copy-start(f32[128,128]{1,0:T(8,128)S(1)} %get-tuple-element.264) | copy-start | bytes 196612
  9.0 185.1 %copy-start.25 = (f32[128,128]{1,0:T(8,128)}, f32[128,128]{1,0:T(8,128)S(1)}, u32[]{:S(2)}) copy-start(f32[128,128]{1,0:T(8,128)S(1)} %get-tuple-element.265) | copy-start | bytes 196612
  9.8 5.1 copy-start.38
  9.8 348.3 %copy-start.46 = (f32[4]{0:T(128)}, f32[4]{0:T(128)S(1)}, u32[]{:S(2)}) copy-start(f32[4]{0:T(128)S(1)} %get-tuple-element.268) | copy-start | bytes 52
  14.9 164.8 %copy-start = (f32[128,2048]{1,0:T(8,128)}, f32[128,2048]{1,0:T(8,128)S(1)}, u32[]{:S(2)}) copy-start(f32[128,2048]{1,0:T(8,128)S(1)} %get-tuple-element.178) | copy-start | bytes 3145732
  14.9 164.8 %copy-start.31 = (f32[128]{0:T(128)}, f32[128]{0:T(128)S(1)}, u32[]{:S(2)}) copy-start(f32[128]{0:T(128)S(1)} %broadcast_multiply_fusion.4) | copy-start | bytes 1540
  15.2 164.6 %copy-start.44 = (f32[128]{0:T(128)}, f32[128]{0:T(128)S(1)}, u32[]{:S(2)}) copy-start(f32[128]{0:T(128)S(1)} %multiply_reduce_fusion.9) | copy-start | bytes 1540
  15.2 164.5 %copy-start.33 = (f32[128]{0:T(128)}, f32[128]{0:T(128)S(1)}, u32[]{:S(2)}) copy-start(f32[128]{0:T(128)S(1)} %fusion.106) | copy-start | bytes 1540
  197.7 13.6 copy-start.51
  197.7 22.3 copy-start.43
  197.7 75.7 %all-gather.12.cloned.1.call-start = ((), (), s32[]{:S(2)}) async-start(), calls=%async_computation.8 | async-start | bytes 4718592 | tf_op jit(solution)/shard_map/all_gather | solution.py:146
  209.5 143.8 %all-gather.14.cloned.1.call-start = ((), (), s32[]{:S(2)}) async-start(), calls=%async_computation.9 | async-start | bytes 8650752 | tf_op jit(solution)/shard_map/all_gather | solution.py:64
  210.0 498.4 %all-gather.16.cloned.1.call-start = ((), (), s32[]{:S(2)}) async-start(), calls=%async_computation.10 | async-start | bytes 69206016 | tf_op jit(solution)/shard_map/all_gather | solution.py:64
  210.6 692.9 %all-gather.18.cloned.1.call-start = ((), (), s32[]{:S(2)}) async-start(), calls=%async_computation.11 | async-start | bytes 34603008 | tf_op jit(solution)/shard_map/all_gather | solution.py:64
  211.2 899.7 %reduce-scatter.22.cloned.1.call-start = ((), (), s32[]{:S(2)}) async-start(), calls=%async_computation.16 | async-start | bytes 4718592
  220.0 138.1 %copy-start.49 = (f32[4]{0:T(128)}, f32[4]{0:T(128)S(1)}, u32[]{:S(2)}) copy-start(f32[4]{0:T(128)S(1)} %get-tuple-element.267) | copy-start | bytes 52
  220.0 697.3 %copy-start.36 = (f32[4]{0:T(128)}, f32[4]{0:T(128)S(1)}, u32[]{:S(2)}) copy-start(f32[4]{0:T(128)S(1)} %get-tuple-element.266) | copy-start | bytes 52
  296.0 62.1 %copy-start.27 = (s32[128]{0:T(128)}, s32[128]{0:T(128)S(1)}, u32[]{:S(2)}) copy-start(s32[128]{0:T(128)S(1)} %get-tuple-element.564) | copy-start | bytes 1540
  296.0 62.1 %copy-start.29 = (pred[128]{0:T(512)(128)(4,1)}, pred[128]{0:T(512)(128)(4,1)S(1)}, u32[]{:S(2)}) copy-start(pred[128]{0:T(512)(128)(4,1)S(1)} %get-tuple-element.565) | copy-start | bytes 388
  353.3 4.9 copy-start.6
  353.3 4.9 copy-start.40
  358.1 10.1 copy-start.21
  903.5 14.8 copy-start.17
  923.6 21.9 copy-start.15
  976.2 2.2 copy-start.47
  976.3 12.1 slice-start
  978.4 10.0 copy-start.13
  978.4 10.0 slice-start.1
  988.4 5.2 copy-start.28
  988.4 5.2 copy-start.30
  995.6 2.6 copy-start.9
  997.9 3.3 copy-start.11
  998.7 3.0 copy-start.10
  1008.1 2.6 copy-start.9
  1010.5 3.3 copy-start.11
  1011.2 3.0 copy-start.10
  1020.7 2.6 copy-start.9
  1023.0 3.3 copy-start.11
  1023.8 3.0 copy-start.10
  1033.2 2.6 copy-start.9
  1035.6 3.3 copy-start.11
  1036.3 3.0 copy-start.10
  1059.6 105.9 %reduce-scatter.20.cloned.1.call-start = ((), (), s32[]{:S(2)}) async-start(), calls=%async_computation.15 | async-start | bytes 4718592
  1075.7 304.1 %reduce-scatter.16.cloned.1.call-start = ((), (), s32[]{:S(2)}) async-start(), calls=%async_computation.13 | async-start | bytes 17301504 | tf_op jit(solution)/shard_map/reduce_scatter | solution.py:80
  1084.5 705.2 %reduce-scatter.14.cloned.1.call-start = ((), (), s32[]{:S(2)}) async-start(), calls=%async_computation.12 | async-start | bytes 51904512 | tf_op jit(solution)/shard_map/reduce_scatter | solution.py:80
  1169.7 3.2 copy-start.1
  1169.7 3.2 copy-start.32
  1169.7 3.2 copy-start.34
  1194.2 1308.1 %reduce-scatter.18.cloned.1.call-start = ((), (), s32[]{:S(2)}) async-start(), calls=%async_computation.14 | async-start | bytes 69206016 | tf_op jit(solution)/shard_map/reduce_scatter | solution.py:80
  1220.7 2691.3 %reduce-scatter.24.cloned.1.call-start = ((), (), s32[]{:S(2)}) async-start(), calls=%async_computation.17 | async-start | bytes 138412032
  1269.4 13.6 copy-start.7
  1269.4 13.6 copy-start.14
  1283.0 9.2 copy-start.42
  1283.0 9.2 copy-start.48
  1292.1 5.1 copy-start.2
  1297.1 14.8 copy-start.45
  1297.1 14.8 copy-start.35
  1311.9 4.3 copy-start.3
  1311.9 4.3 copy-start.5
  1312.0 4.3 copy-start.37
  1312.0 4.3 copy-start.41
  1316.2 52.6 %copy-start.39 = (f32[4]{0:T(128)S(1)}, f32[4]{0:T(128)}, u32[]{:S(2)}) copy-start(f32[4]{0:T(128)} %copy-done.38) | copy-start | bytes 52
  (14 other events, 23.7 us)
Sparse Core Ops, SparseCore 0:
  10.8 152.4 all-gather.7
  197.8 36.4 all-gather.9
  236.8 36.5 all-gather.11
  276.2 77.0 all-gather.13
  356.0 352.3 all-gather.15
  711.1 192.3 all-gather.17
  1059.7 51.1 reduce-scatter.21
  1114.3 51.1 reduce-scatter.19
  1168.3 186.2 reduce-scatter.15
  1361.5 428.1 reduce-scatter.13
  1792.6 709.6 reduce-scatter.17
  2505.0 1406.9 reduce-scatter.23
where the time goes:
time: 3930 us; the launch traced here: 3920 us
  waiting for transfers between devices  3370 us (86%)
  matrix products  343 us (9%)
  local copies, waits for them, and re-layouts  81.6 us (2%)
  blocking collectives  51.8 us (1%)
  other arithmetic  45.5 us (1%)
    unnamed x15, waiting for transfers between devices  1490 us
    reduce_scatter x3, waiting for transfers between devices, weight_grad(): lax.psum_scatter(lax.dot_general(inputs, grad_rows, (((0,), (0,)), ((), (...  1120 us
    all_gather x4, waiting for transfers between devices, project(): lax.all_gather(weight, ('dp', 'seq'), axis=0, tiled=True)  706 us
    dot_general x4, matrix products, weight_grad(): lax.dot_general(inputs, grad_rows, (((0,), (0,)), ((), ())), preferred_el...  104 us
  transfers between devices with their start and end apart: 12, of which 11 were waited for; matrix products, arithmetic and copies ran while one was open for 7% of the time, Pallas kernels for 0%

commit v1 on v0

v1 whole, which is shorter than its diff:
```python
import jax
import jax.numpy as jnp
from jax import lax
from jax.sharding import PartitionSpec as P

HEADS = 16
HEAD_DIM = 128

ln_eps = 1e-05
rope_base = 10000.0
neg_big = -1e30
f32 = jnp.float32
bf16 = jnp.bfloat16


def dot(a, b, dims):
    return lax.dot_general(a, b, (dims, ((), ())), preferred_element_type=f32)


def norm_stats(values):
    mean = jnp.mean(values, axis=-1, keepdims=True)
    centered = values - mean
    inv = lax.rsqrt(jnp.mean(centered * centered, axis=-1, keepdims=True) + ln_eps)
    return centered * inv, inv


def norm_back(grad, unit, inv):
    mean = jnp.mean(grad, axis=-1, keepdims=True)
    proj = jnp.mean(grad * unit, axis=-1, keepdims=True)
    return (grad - mean - unit * proj) * inv


def rope_tables(positions):
    half = HEAD_DIM // 2
    inv_freq = rope_base ** (-(jnp.arange(half, dtype=f32) * 2.0 / HEAD_DIM))
    angles = positions.astype(f32)[..., None] * inv_freq
    angles = jnp.concatenate([angles, angles], axis=-1)
    return jnp.cos(angles), jnp.sin(angles)


def turn(values):
    half = HEAD_DIM // 2
    return jnp.concatenate([-values[..., half:], values[..., :half]], axis=-1)


def turn_back(values):
    half = HEAD_DIM // 2
    return jnp.concatenate([values[..., half:], -values[..., :half]], axis=-1)


def body(n_dp, n_seq, streams, segments, positions, att_proj, attn_out, ff_proj, ff_out,
         mix_in, mix_res, depth, cotangent):
    seq_count, toks, n_str, width = streams.shape
    assert seq_count == 1
    n_all = n_dp * n_seq
    both = ("dp", "seq")
    rows = att_proj.shape[0]
    ffl = ff_out.shape[0]
    hp = HEADS // n_seq
    hw = hp * HEAD_DIM
    length = toks * n_seq
    scale = HEAD_DIM ** -0.5
    seq_id = lax.axis_index("seq")

    def mix(parts, weights):
        total = parts[0] * weights[0]
        for i in range(1, n_str):
            total = total + parts[i] * weights[i]
        return total

    wq = att_proj.reshape(rows, 3, n_seq, hw)
    wq = lax.all_to_all(wq, "seq", 2, 0, tiled=True).reshape(n_seq * rows, 3 * hw)
    wq = lax.all_gather(wq, "dp", axis=0, tiled=True)
    wf = ff_proj.reshape(rows, 2, n_all, ffl)
    wf = lax.all_to_all(wf, both, 2, 0, tiled=True).reshape(n_all * rows, 2 * ffl)
    wo = lax.all_gather(attn_out, both, axis=0, tiled=True)
    wo = lax.dynamic_slice_in_dim(wo, seq_id * hw, hw, 0)
    seg_all = lax.all_gather(segments[0], "seq", axis=0, tiled=True)
    pos_all = lax.all_gather(positions[0], "seq", axis=0, tiled=True)

    s_in = [streams[0, :, i].astype(f32) for i in range(n_str)]
    cot = [cotangent[0, :, i].astype(f32) for i in range(n_str)]
    d_branch_ff = mix(cot, depth[1]).astype(bf16)
    dbf = lax.all_gather(d_branch_ff, both, axis=0, tiled=True)

    unit_att, inv_att = norm_stats(mix(s_in, mix_in[0]))
    xa = lax.all_gather(unit_att.astype(bf16), "seq", axis=0, tiled=True)
    proj = dot(xa, wq, ((1,), (0,))).reshape(length, 3, hp, HEAD_DIM)
    cosine, sine = rope_tables(pos_all)
    cosine, sine = cosine[:, None], sine[:, None]
    q = (proj[:, 0] * cosine + turn(proj[:, 0]) * sine).astype(bf16)
    k = (proj[:, 1] * cosine + turn(proj[:, 1]) * sine).astype(bf16)
    v = proj[:, 2].astype(bf16)
    idx = jnp.arange(length, dtype=jnp.int32)
    allowed = (idx[None, :] <= idx[:, None]) | (
        (seg_all[None, :] == seg_all[:, None]) & (seg_all[:, None] > 0))
    scores = jnp.einsum("qhd,khd->hqk", q, k, preferred_element_type=f32) * scale
    scores = jnp.where(allowed[None], scores, neg_big)
    top = jnp.max(scores, axis=-1, keepdims=True)
    p = jnp.exp(scores - top)
    p = p / jnp.sum(p, axis=-1, keepdims=True)
    p_low = p.astype(bf16)
    att = jnp.einsum("hqk,khd->qhd", p_low, v, preferred_element_type=f32)
    att = att.reshape(length, hw).astype(bf16)
    branch_att = lax.psum_scatter(dot(att, wo, ((1,), (0,))).astype(bf16), "seq",
                                  scatter_dimension=0, tiled=True).astype(f32)

    mid = [mix(s_in, mix_res[0, :, j]) + depth[0, j] * branch_att for j in range(n_str)]
    unit_ff, inv_ff = norm_stats(mix(mid, mix_in[1]))
    xf = lax.all_gather(unit_ff.astype(bf16), both, axis=0, tiled=True)
    upgate = dot(xf, wf, ((1,), (0,)))
    up, gate = upgate[:, :ffl], upgate[:, ffl:]
    sig = 1.0 / (1.0 + jnp.exp(-gate))
    hidden = (gate * sig * up).astype(bf16)
    branch_ff = lax.psum_scatter(dot(hidden, ff_out, ((1,), (0,))).astype(bf16), both,
                                 scatter_dimension=0, tiled=True).astype(f32)

    d_hidden = dot(dbf, ff_out, ((1,), (1,)))
    g_ff_out = dot(hidden, dbf, ((0,), (0,)))
    d_up = d_hidden * gate * sig
    d_gate = d_hidden * up * (sig * (1.0 + gate * (1.0 - sig)))
    d_ug = jnp.concatenate([d_up, d_gate], axis=1).astype(bf16)
    d_unit = lax.psum_scatter(dot(d_ug, wf, ((1,), (1,))).astype(bf16), both,
                              scatter_dimension=0, tiled=True).astype(f32)
    g_wf = dot(xf, d_ug, ((0,), (0,))).astype(bf16).reshape(n_all, rows, 2 * ffl)
    g_wf = lax.all_to_all(g_wf, both, 0, 0, tiled=True)
    g_ff_proj = g_wf.reshape(n_all, rows, 2, ffl).transpose(1, 2, 0, 3).reshape(ff_proj.shape).astype(f32)
    d_mix_ff = norm_back(d_unit, unit_ff, inv_ff)

    d_mid = [mix(cot, mix_res[1, i]) + mix_in[1, i] * d_mix_ff for i in range(n_str)]
    d_branch_att = mix(d_mid, depth[0]).astype(bf16)
    dba = lax.all_gather(d_branch_att, "seq", axis=0, tiled=True)
    d_att = dot(dba, wo, ((1,), (1,))).astype(bf16).reshape(length, hp, HEAD_DIM)
    g_wo = dot(att, dba, ((0,), (0,))).astype(bf16)
    g_wo = lax.all_gather(g_wo, "seq", axis=0, tiled=True)
    g_attn_out = lax.psum_scatter(g_wo, "dp", scatter_dimension=0, tiled=True)
    g_attn_out = lax.dynamic_slice_in_dim(g_attn_out, seq_id * rows, rows, 0).astype(f32)

    d_v = jnp.einsum("hqk,qhd->khd", p_low, d_att, preferred_element_type=f32)
    d_p = jnp.einsum("qhd,khd->hqk", d_att, v, preferred_element_type=f32)
    d_s = (p * (d_p - jnp.sum(p * d_p, axis=-1, keepdims=True))).astype(bf16)
    d_q = jnp.einsum("hqk,khd->qhd", d_s, k, preferred_element_type=f32) * scale
    d_k = jnp.einsum("hqk,qhd->khd", d_s, q, preferred_element_type=f32) * scale
    d_q = d_q * cosine + turn_back(d_q * sine)
    d_k = d_k * cosine + turn_back(d_k * sine)
    d_proj = jnp.stack([d_q, d_k, d_v], axis=1).reshape(length, 3 * hw).astype(bf16)
    d_unit_att = lax.psum_scatter(dot(d_proj, wq, ((1,), (1,))).astype(bf16), "seq",
                                  scatter_dimension=0, tiled=True).astype(f32)
    g_wq = dot(xa, d_proj, ((0,), (0,))).astype(bf16)
    g_wq = lax.psum_scatter(g_wq, "dp", scatter_dimension=0, tiled=True)
    g_wq = lax.all_to_all(g_wq.reshape(n_seq, rows, 3 * hw), "seq", 0, 0, tiled=True)
    g_att_proj = g_wq.reshape(n_seq, rows, 3, hw).transpose(1, 2, 0, 3).reshape(att_proj.shape).astype(f32)
    d_mix_att = norm_back(d_unit_att, unit_att, inv_att)

    g_in = [mix(d_mid, mix_res[0, i]) + mix_in[0, i] * d_mix_att for i in range(n_str)]
    out = [mix(mid, mix_res[1, :, j]) + depth[1, j] * branch_ff for j in range(n_str)]

    def inner(a, b):
        return jnp.sum(a * b)

    g_mix_in = jnp.stack([
        jnp.stack([inner(s, d_mix_att) for s in s_in]),
        jnp.stack([inner(m, d_mix_ff) for m in mid])])
    g_mix_res = jnp.stack([
        jnp.stack([jnp.stack([inner(s, d) for d in d_mid]) for s in s_in]),
        jnp.stack([jnp.stack([inner(m, c) for c in cot]) for m in mid])])
    g_depth = jnp.stack([
        jnp.stack([inner(branch_att, d) for d in d_mid]),
        jnp.stack([inner(branch_ff, c) for c in cot])])
    g_mix_in, g_mix_res, g_depth = lax.psum((g_mix_in, g_mix_res, g_depth), both)
    return (jnp.stack(out, axis=1).astype(bf16)[None], jnp.stack(g_in, axis=1)[None],
            g_att_proj, g_attn_out, g_ff_proj, g_ff_out, g_mix_in, g_mix_res, g_depth)


def solution(mesh):
    n_dp, n_seq = mesh.shape["dp"], mesh.shape["seq"]
    tok = P("dp", "seq", None, None)
    ids = P("dp", "seq")
    mat = P(("dp", "seq"), None)

    def run(*args):
        return body(n_dp, n_seq, *args)

    return jax.shard_map(
        run, mesh=mesh,
        in_specs=(tok, ids, ids, mat, mat, mat, mat, P(), P(), P(), tok),
        out_specs=(tok, tok, mat, mat, mat, mat, P(), P(), P()),
        check_vma=False)
```

time: 3930 us -> 1370 us (0.35)
  waiting for transfers between devices: 3370 us -> 833 us
  matrix products: 343 us -> 140 us
  blocking collectives: 51.8 us -> 161 us
  other arithmetic: 45.5 us -> 137 us
    unnamed x15 -> x13, waiting for transfers between devices: 1490 us -> 0.88 us
    reduce_scatter x3 -> x6, waiting for transfers between devices: 1120 us -> 473 us  [the longest x1 186 us: body(): lax.psum_scatter(dot(hidden, ff_out, ((1,), (0,))).astype(bf16), both, sc...]
    all_gather x6 -> x7, waiting for transfers between devices: 759 us -> 326 us  [the longest x1 101 us: body(): dbf = lax.all_gather(d_branch_ff, both, axis=0, tiled=True)]
    dot_general x46 -> x17, matrix products: 343 us -> 132 us  [the longest x12 119 us: dot(): return lax.dot_general(a, b, (dims, ((), ())), preferred_element_type=f32)]
    all_to_all x0 -> x2, blocking collectives: none -> 93.6 us  [the longest x1 79.3 us: body(): lax.all_to_all(wf, both, 2, 0, tiled=True).reshape(n_all * rows, 2 * ffl)]
    another operation x8 -> x24, other arithmetic: 0.05 us -> 61.6 us  [the longest x2 15.6 us: body(): jnp.stack(g_in, axis=1)[None]]
  transfers between devices with their start and end apart: 12 -> 15, of which waited for: 11 -> 12; matrix products, arithmetic and copies ran while one was open for 7% -> 17% of each run, Pallas kernels for 0% -> 0%
where the time goes in v1:
time: 1370 us; the launch traced here: 1360 us
  waiting for transfers between devices  833 us (61%)
  blocking collectives  161 us (12%)
  matrix products  140 us (10%)
  other arithmetic  137 us (10%)
  local copies, waits for them, and re-layouts  58.5 us (4%)
  between operations  15 us (1%)
    reduce_scatter x1, waiting for transfers between devices, body(): lax.psum_scatter(dot(hidden, ff_out, ((1,), (0,))).astype(bf16), both, sc...  186 us
    reduce_scatter x1, waiting for transfers between devices, body(): lax.psum_scatter(dot(d_ug, wf, ((1,), (1,))).astype(bf16), both, scatter_...  175 us
    dot_general x12, matrix products, dot(): return lax.dot_general(a, b, (dims, ((), ())), preferred_element_type=f32)  119 us
    all_gather x1, waiting for transfers between devices, body(): dbf = lax.all_gather(d_branch_ff, both, axis=0, tiled=True)  101 us
    all_to_all x1, blocking collectives, body(): lax.all_to_all(wf, both, 2, 0, tiled=True).reshape(n_all * rows, 2 * ffl)  79.3 us
    reduce_scatter x1, waiting for transfers between devices, body(): g_attn_out = lax.psum_scatter(g_wo, 'dp', scatter_dimension=0, tiled=True)  64.5 us
    all_gather x1, waiting for transfers between devices, body(): wo = lax.all_gather(attn_out, both, axis=0, tiled=True)  59.8 us
    psum x1, blocking collectives, body(): lax.psum((g_mix_in, g_mix_res, g_depth), both)  49.6 us
  transfers between devices with their start and end apart: 15, of which 12 were waited for; matrix products, arithmetic and copies ran while one was open for 17% of the time, Pallas kernels for 0%

profile of v1, /device:TPU:14, one launch (start us, length us, event | category | flops | bytes accessed | tf_op | source)
XLA Modules:
  0.0 1357.4 jit_solution(10905882169217803883)
XLA Ops:
  8.8 14.3 %all_to_all.40 = bf16[64,3,8,256]{3,0,1,2:T(8,128)(2,1)S(1)} all-to-all(bf16[64,3,8,256]{3,0,1,2:T(8,128)(2,1)S(1)} %copy.109), channel_id=1, replica_groups=mesh['dp'=4,'seq'=8] {'seq'}, dimensions={2} | all-to-all | bytes 1572864 | tf_op jit(solution)/shard_map/all_to_all | solution.py:72
  25.6 3.0 fusion.160
  28.7 5.9 fusion.157
  37.8 8.7 all-gather.1
  46.6 9.0 all-gather
  55.7 2.7 broadcast_multiply_fusion.3
  60.2 27.1 %all-gather.12.cloned.1.call-done = bf16[2048,768]{1,0:T(8,128)(2,1)} async-done(((bf16[512,768]{1,0:T(8,128)(2,1)}), bf16[2048,768]{1,0:T(8,128)(2,1)}) %all-gather.12.cloned.1.call-update) | async-done | bytes 3145744 | tf_op jit(solution)/shard_map/all_gather | solution.py:73
  87.4 39.0 %all-gather.10.cloned.1.call-done = bf16[1024,2048]{1,0:T(8,128)(2,1)} async-done(((bf16[128,2048]{1,0:T(8,128)(2,1)}), bf16[1024,2048]{1,0:T(8,128)(2,1)}) %all-gather.10.cloned.1.call-update) | async-done | bytes 4194320 | tf_op jit(solution)/shard_map/all_gather | solution.py:87
  126.3 6.2 fusion.168
  134.9 7.2 fusion.167
  142.1 4.5 fusion.10
  146.6 59.8 %all-gather.14.cloned.1.call-done = bf16[2048,2048]{1,0:T(8,128)(2,1)} async-done(((bf16[64,2048]{1,0:T(8,128)(2,1)}), bf16[2048,2048]{1,0:T(8,128)(2,1)}) %all-gather.14.cloned.1.call-update) | async-done | bytes 8388624 | tf_op jit(solution)/shard_map/all_gather | solution.py:76
  206.3 4.6 convolution_convert_fusion.2
  213.1 47.7 %reduce-scatter.7.cloned.1.call-done = bf16[128,2048]{1,0:T(8,128)(2,1)} async-done(((bf16[1024,2048]{1,0:T(8,128)(2,1)}), bf16[128,2048]{1,0:T(8,128)(2,1)}) %reduce-scatter.7.cloned.1.call-update) | async-done | bytes 524304 | tf_op jit(solution)/shard_map/reduce_scatter | solution.py:105
  260.8 20.2 %fusion.152 = (f32[128]{0:T(128)S(1)}, f32[128,2048]{1,0:T(8,128)S(1)}, f32[128,2048]{1,0:T(8,128)S(1)}, f32[128,2048]{1,0:T(8,128)}, f32[128,2048]{1,0:T(8,128)}, /*index=5*/f32[128,2048]{1,0:T(8,128)}) fusion(f32[]{:T(128)} %bitcast.50, f32[]{:T(128)} %bitcast.49, f32[]{:T(128)} %bitcast.48, f32[]{:T(128)} %bitcast.47, ...), kind=kLoop, calls=%fused_computation.326 | loop fusion | flops 12844928 | bytes 7864928 | tf_op jit(solution)/shard_map/reduce_sum | solution.py:21
  282.8 8.1 fusion.159
  290.9 5.4 fusion.83
  300.7 79.3 %all_to_all.41 = bf16[64,2,32,256]{3,1,0,2:T(2,128)(2,1)S(1)} all-to-all(bf16[64,2,32,256]{3,1,0,2:T(2,128)(2,1)S(1)} %copy.114), channel_id=1, replica_groups=mesh['dp'=4,'seq'=8] {'dp','seq'}, dimensions={2} | all-to-all | bytes 4194304 | tf_op jit(solution)/shard_map/all_to_all | solution.py:75
  381.8 42.9 %all-gather.16.cloned.1.call-done = bf16[4096,2048]{1,0:T(8,128)(2,1)} async-done(((bf16[128,2048]{1,0:T(8,128)(2,1)}), bf16[4096,2048]{1,0:T(8,128)(2,1)}) %all-gather.16.cloned.1.call-update) | async-done | bytes 16777232 | tf_op jit(solution)/shard_map/all_gather | solution.py:110
  424.7 15.1 %fusion.169 = f32[4096,512]{0,1:T(8,128)} fusion(bf16[4096,2048]{1,0:T(8,128)(2,1)} %all-gather.16.cloned.1.call-done, bf16[2048,512]{1,0:T(8,128)(2,1)} %bitcast.286), kind=kOutput, calls=%fused_computation.338 | convolution fusion | flops 8589934592 | bytes 27262976 | tf_op jit(solution)/shard_map/dot_general | solution.py:17
  439.8 101.1 %all-gather.18.cloned.1.call-done = bf16[4096,2048]{1,0:T(8,128)(2,1)} async-done(((bf16[128,2048]{1,0:T(8,128)(2,1)}), bf16[4096,2048]{1,0:T(8,128)(2,1)}) %all-gather.18.cloned.1.call-update) | async-done | bytes 16777232 | tf_op jit(solution)/shard_map/all_gather | solution.py:84
  540.9 20.5 %multiply_convert_fusion.2 = (bf16[4096,256]{0,1:T(8,128)(2,1)S(1)}, bf16[4096,256]{0,1:T(8,128)(2,1)}, bf16[4096,256]{0,1:T(8,128)(2,1)}) fusion(f32[4096,512]{0,1:T(8,128)} %fusion.169, bf16[4096,2048]{1,0:T(8,128)(2,1)} %all-gather.18.cloned.1.call-done, bf16[256,2048]{1,0:T(8,128)(2,1)S(1)} %copy-done), kind=kOutput, calls=%fused_computation.11 | convolution fusion | flops 4311744512 | bytes 32505856 | tf_op jit(solution)/shard_map/dot_general | solution.py:17
  562.8 14.3 %convolution_convert_fusion = bf16[4096,2048]{1,0:T(8,128)(2,1)} fusion(bf16[2048,512]{1,0:T(8,128)(2,1)S(1)} %bitcast.287, bf16[4096,256]{0,1:T(8,128)(2,1)} %get-tuple-element.168, bf16[4096,256]{0,1:T(8,128)(2,1)S(1)} %get-tuple-element.167), kind=kOutput, calls=%fused_computation.1 | convolution fusion | flops 8606711808 | bytes 23068672 | tf_op jit(solution)/shard_map/dot_general | solution.py:17
  577.2 9.9 convolution_convert_fusion.1
  587.1 174.7 %reduce-scatter.11.cloned.1.call-done = bf16[128,2048]{1,0:T(8,128)(2,1)} async-done(((bf16[4096,2048]{1,0:T(8,128)(2,1)}), bf16[128,2048]{1,0:T(8,128)(2,1)}) %reduce-scatter.11.cloned.1.call-update) | async-done | bytes 524304 | tf_op jit(solution)/shard_map/reduce_scatter | solution.py:123
  763.2 185.6 %reduce-scatter.9.cloned.1.call-done = bf16[128,2048]{1,0:T(8,128)(2,1)} async-done(((bf16[4096,2048]{1,0:T(8,128)(2,1)}), bf16[128,2048]{1,0:T(8,128)(2,1)}) %reduce-scatter.9.cloned.1.call-update) | async-done | bytes 524304 | tf_op jit(solution)/shard_map/reduce_scatter | solution.py:115
  948.8 4.8 fusion.96
  953.6 18.3 %add_convert_fusion = (bf16[128,2048]{1,0:T(8,128)(2,1)}, f32[128,2048]{1,0:T(8,128)S(1)}, f32[128,2048]{1,0:T(8,128)S(1)}, f32[128,2048]{1,0:T(8,128)}, f32[128,2048]{1,0:T(8,128)}) fusion(f32[]{:T(128)} %bitcast.44, f32[]{:T(128)} %bitcast.38, f32[]{:T(128)} %bitcast.32, f32[]{:T(128)} %bitcast.8, f32[128,2048]{1,0:T(8,128)S(1)} %get-tuple-element.144, ...), kind=kLoop, calls=%fused_computation.253 | loop fusion | flops 12582912 | bytes 7864416 | tf_op jit(solution)/shard_map/convert_element_type | solution.py:131
  972.0 35.7 %all-gather.20.cloned.1.call-done = bf16[1024,2048]{1,0:T(8,128)(2,1)} async-done(((bf16[128,2048]{1,0:T(8,128)(2,1)}), bf16[1024,2048]{1,0:T(8,128)(2,1)}) %all-gather.20.cloned.1.call-update) | async-done | bytes 4194320 | tf_op jit(solution)/shard_map/all_gather | solution.py:132
  1007.7 4.6 convolution_convert_fusion.6
  1012.8 3.8 convolution_convert_fusion.7
  1016.6 5.3 multiply_reduce_fusion
  1033.1 5.0 convolution_convert_fusion.3
  1038.4 7.9 convolution_convert_fusion.4
  1046.4 20.4 %all-gather.22.cloned.1.call-done = bf16[2048,2048]{1,0:T(8,128)(2,1)} async-done(((bf16[256,2048]{1,0:T(8,128)(2,1)}), bf16[2048,2048]{1,0:T(8,128)(2,1)}) %all-gather.22.cloned.1.call-update) | async-done | bytes 8388624 | tf_op jit(solution)/shard_map/all_gather | solution.py:135
  1066.8 14.7 %convolution_convert_fusion.5 = bf16[2048,512]{1,0:T(8,128)(2,1)} fusion(bf16[4096,2048]{1,0:T(8,128)(2,1)} %all-gather.16.cloned.1.call-done, bf16[4096,256]{0,1:T(8,128)(2,1)} %get-tuple-element.168, bf16[4096,256]{0,1:T(8,128)(2,1)} %copy-done.37), kind=kOutput, calls=%fused_computation.103 | convolution fusion | flops 8599371776 | bytes 23068672 | tf_op jit(solution)/shard_map/dot_general | solution.py:17
  1081.5 5.8 all-to-all-start.3
  1087.3 12.2 fusion.170
  1099.5 33.9 %all-to-all-done.3 = bf16[32,64,512]{2,1,0:T(8,128)(2,1)} async-done(((bf16[32,64,512]{2,1,0:T(8,128)(2,1)}), bf16[32,64,512]{2,1,0:T(8,128)(2,1)}, u32[]{:S(2)}, u32[]{:S(2)}) %all-to-all-start.3) | async-done | bytes 2097184 | tf_op jit(solution)/shard_map/all_to_all | solution.py:126
  1133.4 5.6 reshape.472
  1139.0 4.6 copy.125
  1143.7 4.4 copy.149
  1148.1 7.1 fusion.135
  1155.2 6.9 fusion.136
  1162.4 2.9 copy.126
  1165.4 2.6 maximum_bitcast_fusion.9
  1168.0 2.7 maximum_bitcast_fusion.4
  1170.7 2.6 maximum_bitcast_fusion.12
  1173.3 2.5 maximum_bitcast_fusion.11
  1175.8 2.5 maximum_bitcast_fusion.10
  1178.3 2.7 maximum_bitcast_fusion.14
  1182.5 5.4 fusion.32
  1187.9 2.5 maximum_bitcast_fusion.13
  1192.9 2.8 maximum_bitcast_fusion.5
  1195.6 2.5 maximum_bitcast_fusion.6
  1198.1 2.6 maximum_bitcast_fusion.7
  1200.7 2.5 maximum_bitcast_fusion.3
  1203.4 5.4 all-to-all-start.2
  1208.7 49.6 %all-reduce = (f32[2,4]{1,0:T(2,128)}, f32[2,4,4]{2,1,0:T(4,128)}, f32[2,4]{1,0:T(2,128)}) all-reduce(f32[2,4]{1,0:T(2,128)S(1)} %pad_maximum_fusion.7, f32[2,4,4]{2,1,0:T(4,128)S(1)} %pad_maximum_fusion.6, f32[2,4]{1,0:T(2,128)S(1)} %pad_maximum_fusion.8), channel_id=1, replica_groups=mesh['dp'=4,'seq'=8] {'dp','seq'}, use_global_device_ids=true, to_apply=%region_25.26 | all-reduce | flops 48 | bytes 384 | tf_op jit(solution)/shard_map/psum | solution.py:170
  1258.3 8.9 add_bitcast_fusion.2
  1267.2 6.7 add_bitcast_fusion.3
  1274.2 4.7 copy.127
  1278.9 2.6 reshape.471
  1284.1 64.5 %reduce-scatter.17.cloned.1.call-done = bf16[512,2048]{1,0:T(8,128)(2,1)} async-done(((bf16[2048,2048]{1,0:T(8,128)(2,1)}), bf16[512,2048]{1,0:T(8,128)(2,1)}) %reduce-scatter.17.cloned.1.call-update) | async-done | bytes 2097168 | tf_op jit(solution)/shard_map/reduce_scatter | solution.py:136
  (162 shorter events, 45.3 us)
Async XLA Ops:
  7.2 533.7 %copy-start = (bf16[256,2048]{1,0:T(8,128)(2,1)S(1)}, bf16[256,2048]{1,0:T(8,128)(2,1)}, u32[]{:S(2)}) copy-start(bf16[256,2048]{1,0:T(8,128)(2,1)} %param.17) | copy-start | bytes 3145732
  7.2 80.2 %all-gather.12.cloned.1.call-start = ((), (), s32[]{:S(2)}) async-start(), calls=%async_computation.11 | async-start | bytes 3932160 | tf_op jit(solution)/shard_map/all_gather | solution.py:73
  8.6 16.3 %copy-start.28 = (f32[2,4]{1,0:T(2,128)S(1)}, f32[2,4]{1,0:T(2,128)}, u32[]{:S(2)}) copy-start(f32[2,4]{1,0:T(2,128)} %param.18) | copy-start | bytes 100
  8.6 17.0 %copy-start.11 = (bf16[1,128,4,2048]{3,2,1,0:T(4,128)(2,1)S(1)}, bf16[1,128,4,2048]{3,2,1,0:T(4,128)(2,1)}, u32[]{:S(2)}) copy-start(bf16[1,128,4,2048]{3,2,1,0:T(4,128)(2,1)} %param.11) | copy-start | bytes 6291460
  24.9 101.5 %all-gather.10.cloned.1.call-start = ((), (), s32[]{:S(2)}) async-start(), calls=%async_computation.10 | async-start | bytes 4718592 | tf_op jit(solution)/shard_map/all_gather | solution.py:87
  28.6 9.2 copy-start.34
  28.7 17.9 %copy-start.35 = (s32[1,128]{1,0:T(1,128)S(1)}, s32[1,128]{1,0:T(1,128)}, u32[]{:S(2)}) copy-start(s32[1,128]{1,0:T(1,128)} %param.12) | copy-start | bytes 1540
  34.5 1.0 copy-start.2
  34.5 1.0 copy-start.30
  35.5 0.5 copy-start.32
  37.0 169.3 %all-gather.14.cloned.1.call-start = ((), (), s32[]{:S(2)}) async-start(), calls=%async_computation.12 | async-start | bytes 8650752 | tf_op jit(solution)/shard_map/all_gather | solution.py:76
  37.8 223.0 %reduce-scatter.7.cloned.1.call-start = ((), (), s32[]{:S(2)}) async-start(), calls=%async_computation.13 | async-start | bytes 4718592 | tf_op jit(solution)/shard_map/reduce_scatter | solution.py:105
  132.6 1.7 copy-start.12
  134.9 7.2 copy-start.19
  134.9 7.2 copy-start.22
  146.5 64.4 %copy-start.26 = (bf16[2,128,1024]{2,1,0:T(8,128)(2,1)}, bf16[2,128,1024]{2,1,0:T(8,128)(2,1)S(1)}, u32[]{:S(2)}) copy-start(bf16[2,128,1024]{2,1,0:T(8,128)(2,1)S(1)} %fusion.10) | copy-start | bytes 1572868
  206.3 4.6 copy-start.29
  206.3 5.3 copy-start.27
  210.9 213.8 %all-gather.16.cloned.1.call-start = ((), (), s32[]{:S(2)}) async-start(), calls=%async_computation.14 | async-start | bytes 17301504 | tf_op jit(solution)/shard_map/all_gather | solution.py:110
  282.2 258.6 %all-gather.18.cloned.1.call-start = ((), (), s32[]{:S(2)}) async-start(), calls=%async_computation.16 | async-start | bytes 17301504 | tf_op jit(solution)/shard_map/all_gather | solution.py:84
  296.4 465.5 %reduce-scatter.11.cloned.1.call-start = ((), (), s32[]{:S(2)}) async-start(), calls=%async_computation.17 | async-start | bytes 17301504 | tf_op jit(solution)/shard_map/reduce_scatter | solution.py:123
  540.9 21.9 %copy-start.21 = (bf16[256,8,2,256]{3,1,2,0:T(8,128)(2,1)S(1)}, bf16[256,8,2,256]{3,1,2,0:T(8,128)(2,1)}, u32[]{:S(2)}) copy-start(bf16[256,8,2,256]{3,1,2,0:T(8,128)(2,1)} %copy.147) | copy-start | bytes 6291460
  561.4 1.4 copy-start.37
  577.1 371.7 %reduce-scatter.9.cloned.1.call-start = ((), (), s32[]{:S(2)}) async-start(), calls=%async_computation.15 | async-start | bytes 17301504 | tf_op jit(solution)/shard_map/reduce_scatter | solution.py:115
  587.0 361.8 %copy-start.6 = (f32[128,2048]{1,0:T(8,128)S(1)}, f32[128,2048]{1,0:T(8,128)}, u32[]{:S(2)}) copy-start(f32[128,2048]{1,0:T(8,128)} %get-tuple-element.158) | copy-start | bytes 3145732
  587.1 420.7 %all-gather.20.cloned.1.call-start = ((), (), s32[]{:S(2)}) async-start(), calls=%async_computation.18 | async-start | bytes 4718592 | tf_op jit(solution)/shard_map/all_gather | solution.py:132
  948.8 4.8 copy-start.13
  948.8 4.8 copy-start.14
  948.8 4.8 copy-start.15
  948.8 4.8 copy-start.16
  971.9 94.8 %all-gather.22.cloned.1.call-start = ((), (), s32[]{:S(2)}) async-start(), calls=%async_computation.21 | async-start | bytes 9437184 | tf_op jit(solution)/shard_map/all_gather | solution.py:135
  1012.3 168.7 %reduce-scatter.13.cloned.1.call-start = ((), (), s32[]{:S(2)}) async-start(), calls=%async_computation.19 | async-start | bytes 4718592 | tf_op jit(solution)/shard_map/reduce_scatter | solution.py:147
  1016.6 5.4 slice-start
  1016.6 7.1 slice-start.1
  1023.6 2.5 copy-start.23
  1026.1 1.6 copy-start.17
  1026.1 1.6 copy-start.20
  1028.6 1.0 copy-start.24
  1030.2 2.9 copy-start.36
  1032.0 1.1 copy-start.25
  1038.2 165.2 %reduce-scatter.15.cloned.1.call-start = ((), (), s32[]{:S(2)}) async-start(), calls=%async_computation.20 | async-start | bytes 3932160 | tf_op jit(solution)/shard_map/reduce_scatter | solution.py:150
  1046.3 302.3 %reduce-scatter.17.cloned.1.call-start = ((), (), s32[]{:S(2)}) async-start(), calls=%async_computation.22 | async-start | bytes 10485760 | tf_op jit(solution)/shard_map/reduce_scatter | solution.py:136
  1081.5 52.0 %all-to-all-start.3 = ((bf16[32,64,512]{2,1,0:T(8,128)(2,1)}), bf16[32,64,512]{2,1,0:T(8,128)(2,1)}, u32[]{:S(2)}, u32[]{:S(2)}) async-start(bf16[32,64,512]{2,1,0:T(8,128)(2,1)} %bitcast.285), calls=%async_computation.9 | async-start | bytes 4194304 | tf_op jit(solution)/shard_map/all_to_all | solution.py:126
  1143.7 4.4 copy-start.7
  1143.7 4.4 copy-start.8
  1143.7 4.4 copy-start.9
  1143.7 4.4 copy-start.18
  1162.1 18.9 %copy-start.3 = (f32[128,2048]{1,0:T(8,128)S(1)}, f32[128,2048]{1,0:T(8,128)}, u32[]{:S(2)}) copy-start(f32[128,2048]{1,0:T(8,128)} %copy-done.2) | copy-start | bytes 3145732
  1162.1 18.9 %copy-start.31 = (f32[128]{0:T(128)S(1)}, f32[128]{0:T(128)}, u32[]{:S(2)}) copy-start(f32[128]{0:T(128)} %copy-done.30) | copy-start | bytes 1540
  1162.1 18.9 %copy-start.33 = (f32[128]{0:T(128)S(1)}, f32[128]{0:T(128)}, u32[]{:S(2)}) copy-start(f32[128]{0:T(128)} %copy-done.32) | copy-start | bytes 1540
  1203.4 63.8 %copy-start.4 = (f32[128,2048]{1,0:T(8,128)S(1)}, f32[128,2048]{1,0:T(8,128)}, u32[]{:S(2)}) copy-start(f32[128,2048]{1,0:T(8,128)} %get-tuple-element.148) | copy-start | bytes 3145732
  1203.4 75.5 %all-to-all-start.2 = ((bf16[8,64,768]{2,1,0:T(8,128)(2,1)}), bf16[8,64,768]{2,1,0:T(8,128)(2,1)}, u32[]{:S(2)}, u32[]{:S(2)}) async-start(bf16[8,64,768]{2,1,0:T(8,128)(2,1)} %bitcast.294), calls=%async_computation.7 | async-start | bytes 1572864 | tf_op jit(solution)/shard_map/all_to_all | solution.py:151
  1258.3 8.9 copy-start.5
  1258.3 8.9 copy-start.10
  1278.9 71.5 %copy-start.1 = (bf16[256,2048]{1,0:T(8,128)(2,1)S(1)}, bf16[256,2048]{1,0:T(8,128)(2,1)}, u32[]{:S(2)}) copy-start(bf16[256,2048]{1,0:T(8,128)(2,1)} %param.17) | copy-start | bytes 3145732
Sparse Core Ops, SparseCore 0:
  25.0 62.3 all-gather.11
  89.8 36.4 all-gather.9
  129.2 77.0 all-gather.13
  211.0 49.7 reduce-scatter.6
  282.4 142.3 all-gather.15
  428.0 112.8 all-gather.17
  577.2 184.5 reduce-scatter.10
  764.1 184.6 reduce-scatter.8
  972.1 35.6 all-gather.19
  1012.5 54.2 all-gather.21
  1070.7 67.5 reduce-scatter.12
  1140.4 59.9 reduce-scatter.14
  1202.8 145.7 reduce-scatter.16

commit v2 on v1

--- a/solution.py
+++ b/solution.py
@@ -1,6 +1,10 @@
+import functools
+
 import jax
 import jax.numpy as jnp
 from jax import lax
+from jax.experimental import pallas as pl
+from jax.experimental.pallas import tpu as pltpu
 from jax.sharding import PartitionSpec as P
 
 HEADS = 16
@@ -11,6 +15,512 @@
 neg_big = -1e30
 f32 = jnp.float32
 bf16 = jnp.bfloat16
+
+
+MESH = pl.DeviceIdType.MESH
+DMA = pltpu.SemaphoreType.DMA
+ANY = pl.BlockSpec(memory_space=pl.ANY)
+VM = pl.BlockSpec(memory_space=pltpu.VMEM)
+
+def greet(peers):
+    bar = pltpu.get_barrier_semaphore()
+    for p in peers:
+        pl.semaphore_signal(bar, inc=1, device_id=p, device_id_type=MESH)
+    pl.semaphore_wait(bar, len(peers))
+
+def remote(src, dst, ss, rs, dev):
+    return pltpu.make_async_remote_copy(src_ref=src, dst_ref=dst, send_sem=ss, recv_sem=rs, device_id=dev, device_id_type=MESH)
+
+def place():
+    z = lax.axis_index("dp"); s = lax.axis_index("seq")
+    c = s // 2; k = lax.rem(s, 2)
+    xc = c + 1 - 2 * lax.rem(c, 2)
+    yc = lax.rem(c + 2, 4)
+    dc = lax.rem(xc + 2, 4)
+    return z, s, c, k, xc, yc, dc
+
+def add_rows(dst, srcs, first, count, step=16):
+    def one(i, _):
+        rows = pl.ds(pl.multiple_of(first + i * step, step), step)
+        total = srcs[0][rows, :].astype(f32)
+        for src in srcs[1:]:
+            total = total + src[rows, :].astype(f32)
+        dst[rows, :] = total.astype(dst.dtype)
+        return 0
+    lax.fori_loop(0, count // step, one, 0)
+
+def rs_kernel(nz, trans, a, b, out, pp, po, ra, rd, fx, fy, fz, p_s, p_r, d_s, d_r, x_s, x_r, y_s, y_r, z_s, z_r):
+    z, s, c, k, xc, yc, dc = place()
+    rows = out.shape[0]; half = rows // 2
+    partner = (z, s + 1 - 2 * k)
+    dev_x = (z, 2 * xc + k); dev_y = (z, 2 * yc + k)
+    zt = [lax.rem(z + i, nz) for i in range(1, nz)]
+    greet([partner, dev_x, dev_y] + [(t, s) for t in zt])
+    dims = (((1,), (1,)), ((), ())) if trans else (((1,), (0,)), ((), ()))
+    cx = lax.rem(c, 2); cy = c // 2
+    def produce(i, _):
+        j = lax.rem(i, 4)
+        rx = jnp.where(j < 2, 1, 0); ry = jnp.where(lax.rem(j, 2) == 0, 1, 0) * jnp.where(j < 3, 1, 0)
+        px = cx + rx - 2 * cx * rx; py = cy + ry - 2 * cy * ry
+        blk = px + 2 * py
+        if nz > 1:
+            blk = blk + lax.rem(z + 1 + i // 4, nz) * 4
+        at = pl.ds(pl.multiple_of(blk * 2 * rows, 2 * rows), 2 * rows)
+        both = lax.dot_general(a[at, :], b[...], dims, preferred_element_type=f32).astype(bf16)
+        pp[i, 0] = both[:rows]
+        pp[i, 1] = both[rows:]
+        remote(pp.at[i, 1 - k], ra.at[i], p_s.at[i], p_r.at[i], partner).start()
+        return 0
+    lo, hi = pl.ds(0, half), pl.ds(half, half)
+    def first(zi):
+        for j in range(4):
+            q = zi * 4 + j
+            remote(ra.at[q], ra.at[q], p_s.at[q], p_r.at[q], partner).wait_recv()
+            add_rows(po.at[q], [pp.at[q, k], ra.at[q]], 0, rows)
+            if j == 0:
+                remote(po.at[q, lo], rd.at[zi, lo], d_s.at[zi, 0], d_r.at[zi, 0], dev_x).start()
+                remote(po.at[q, hi], rd.at[zi, hi], d_s.at[zi, 1], d_r.at[zi, 1], dev_y).start()
+            if j == 1:
+                remote(po.at[q, lo], fx.at[zi, lo], x_s.at[zi, 0], x_r.at[zi, 0], dev_x).start()
+            if j == 2:
+                remote(po.at[q, hi], fy.at[zi, hi], y_s.at[zi, 1], y_r.at[zi, 1], dev_y).start()
+    def second(zi):
+        qx, qy = zi * 4 + 1, zi * 4 + 2
+        remote(rd.at[zi, lo], rd.at[zi, lo], d_s.at[zi, 0], d_r.at[zi, 0], dev_x).wait_recv()
+        add_rows(po.at[qy], [po.at[qy], rd.at[zi]], 0, half)
+        remote(po.at[qy, lo], fy.at[zi, lo], y_s.at[zi, 0], y_r.at[zi, 0], dev_y).start()
+        remote(rd.at[zi, hi], rd.at[zi, hi], d_s.at[zi, 1], d_r.at[zi, 1], dev_y).wait_recv()
+        add_rows(po.at[qx], [po.at[qx], rd.at[zi]], half, half)
+        remote(po.at[qx, hi], fx.at[zi, hi], x_s.at[zi, 1], x_r.at[zi, 1], dev_x).start()
+    def third(zi):
+        q = zi * 4 + 3
+        for h, part in ((0, lo), (1, hi)):
+            remote(fx.at[zi, part], fx.at[zi, part], x_s.at[zi, h], x_r.at[zi, h], dev_x).wait_recv()
+            remote(fy.at[zi, part], fy.at[zi, part], y_s.at[zi, h], y_r.at[zi, h], dev_y).wait_recv()
+        if zi < nz - 1:
+            add_rows(po.at[q], [po.at[q], fx.at[zi], fy.at[zi]], 0, rows)
+            remote(po.at[q], fz.at[zi], z_s.at[zi], z_r.at[zi], (zt[zi], s)).start()
+        else:
+            for i in range(nz - 1):
+                remote(fz.at[i], fz.at[i], z_s.at[i], z_r.at[i], (zt[i], s)).wait_recv()
+            add_rows(out, [po.at[q], fx.at[zi], fy.at[zi]] + [fz.at[i] for i in range(nz - 1)], 0, rows)
+    lax.fori_loop(0, 4, produce, 0)
+    for t in range(nz + 2):
+        if t + 1 < nz: lax.fori_loop(4 * t + 4, 4 * t + 8, produce, 0)
+        if t < nz: first(t)
+        if 0 <= t - 1 < nz: second(t - 1)
+        if 0 <= t - 2 < nz: third(t - 2)
+    for q in range(4 * nz):
+        remote(ra.at[q], ra.at[q], p_s.at[q], p_r.at[q], partner).wait_send()
+    for zi in range(nz):
+        for h, part in ((0, lo), (1, hi)):
+            remote(rd.at[zi, part], rd.at[zi, part], d_s.at[zi, h], d_r.at[zi, h], dev_x).wait_send()
+            remote(fx.at[zi, part], fx.at[zi, part], x_s.at[zi, h], x_r.at[zi, h], dev_x).wait_send()
+            remote(fy.at[zi, part], fy.at[zi, part], y_s.at[zi, h], y_r.at[zi, h], dev_y).wait_send()
+    for i in range(nz - 1):
+        remote(fz.at[i], fz.at[i], z_s.at[i], z_r.at[i], (zt[i], s)).wait_send()
+
+def dot_scatter(a, b, nz, trans, cid):
+    rows = a.shape[0] // (8 * nz); width = b.shape[0] if trans else b.shape[1]
+    m = max(nz - 1, 1)
+    blk = lambda n: pltpu.VMEM((n, rows, width), bf16)
+    return pl.pallas_call(
+        functools.partial(rs_kernel, nz, trans),
+        out_shape=jax.ShapeDtypeStruct((rows, width), f32),
+        in_specs=[VM, VM], out_specs=VM,
+        scratch_shapes=[pltpu.VMEM((4*nz, 2, rows, width), bf16), blk(4*nz), blk(4*nz), blk(nz), blk(nz), blk(nz), blk(m),
+                        DMA((4*nz,)), DMA((4*nz,)), DMA((nz,2)), DMA((nz,2)), DMA((nz,2)), DMA((nz,2)), DMA((nz,2)), DMA((nz,2)), DMA((m,)), DMA((m,))],
+        compiler_params=pltpu.CompilerParams(collective_id=cid, has_side_effects=True, vmem_limit_bytes=60*1024*1024),
+    )(a, b)
+
+
+class Gather:
+    def __init__(self, nz, x, out, sems):
+        self.zs, self.zr, self.cs, self.cr, self.ds, self.dr, self.ps, self.pr, self.ls = sems
+        self.nz, self.x, self.out = nz, x, out
+        self.z, self.s, self.c, self.k, self.xc, self.yc, self.dc = place()
+        z, s, k = self.z, self.s, self.k
+        self.half = x.shape[0] // 2
+        self.zt = [(lax.rem(z + i, nz), s) for i in range(1, nz)]
+        self.dev = [(z, 2 * self.xc + k), (z, 2 * self.yc + k)]
+        self.partner = (z, s + 1 - 2 * k)
+        self.src = [z] + [lax.rem(z + nz - i, nz) for i in range(1, nz)]
+        self.sends = []
+        self.np = 0
+        self.nw = 0
+
+    def peers(self):
+        return self.zt + self.dev + [self.partner]
+
+    def at(self, zi, chip, core, part=None):
+        idx = (chip, core) if self.nz == 1 else (self.src[zi], chip, core)
+        if part is not None:
+            idx = idx + (pl.ds(part * self.half, self.half),)
+        return self.out.at[idx]
+
+    def go(self, *args):
+        d = remote(*args)
+        d.start()
+        self.sends.append(d)
+
+    def pair(self, src, dst):
+        self.go(src, dst, self.ps.at[self.np], self.pr.at[self.np], self.partner)
+        self.np += 1
+
+    def plane(self, zi, src, dst):
+        for j in range(2):
+            self.go(src, dst, self.cs.at[zi, j], self.cr.at[zi, j], self.dev[j])
+
+    def begin(self):
+        own = self.at(0, self.c, self.k)
+        self.local = pltpu.make_async_copy(self.x, own, self.ls)
+        self.local.start()
+        self.plane(0, self.x, own)
+        for i in range(1, self.nz):
+            self.go(self.x, own, self.zs.at[i - 1], self.zr.at[i - 1], self.zt[i - 1])
+        self.pair(self.x, own)
+
+    def line(self, zi):
+        blk = self.at(zi, self.c, self.k)
+        remote(blk, blk, self.zs.at[zi - 1], self.zr.at[zi - 1], self.zt[zi - 1]).wait_recv()
+        self.plane(zi, blk, blk)
+        self.pair(blk, blk)
+
+    def near(self, zi, j):
+        chip = (self.xc, self.yc)[j]
+        blk = self.at(zi, chip, self.k)
+        remote(blk, blk, self.cs.at[zi, j], self.cr.at[zi, j], self.dev[j]).wait_recv()
+        part = self.at(zi, chip, self.k, j)
+        self.go(part, part, self.ds.at[zi, j], self.dr.at[zi, j], self.dev[1 - j])
+        self.pair(blk, blk)
+
+    def far(self, zi, h):
+        part = self.at(zi, self.dc, self.k, h)
+        remote(part, part, self.ds.at[zi, h], self.dr.at[zi, h], self.dev[1 - h]).wait_recv()
+        self.pair(part, part)
+
+    def wait_pair(self, blk):
+        remote(blk, blk, self.ps.at[self.nw], self.pr.at[self.nw], self.partner).wait_recv()
+        self.nw += 1
+
+    def steps(self):
+        nz = self.nz
+        other = 1 - self.k
+        todo = []
+        for t in range(nz + 2):
+            if 1 <= t < nz:
+                todo.append((lambda t=t: self.line(t), lambda t=t: self.at(t, self.c, other)))
+            u = t - 1 if nz > 1 else t
+            if 0 <= u < nz:
+                for j in range(2):
+                    todo.append((lambda u=u, j=j: self.near(u, j), lambda u=u, j=j: self.at(u, (self.xc, self.yc)[j], other)))
+            u = u - 1
+            if 0 <= u < nz:
+                for h in range(2):
+                    todo.append((lambda u=u, h=h: self.far(u, h), lambda u=u, h=h: self.at(u, self.dc, other, h)))
+        return todo
+
+    def finish(self, todo):
+        self.wait_pair(self.at(0, self.c, 1 - self.k))
+        for _, blk in todo:
+            self.wait_pair(blk())
+        for d in self.sends:
+            d.wait_send()
+        self.local.wait()
+
+
+def gather_sems(nz):
+    m = max(nz - 1, 1)
+    return [DMA((m,)), DMA((m,)), DMA((nz, 2)), DMA((nz, 2)), DMA((nz, 2)), DMA((nz, 2)),
+            DMA((nz * 5,)), DMA((nz * 5,)), DMA]
+
+
+def gather_kernel(nz, x, out, *sems):
+    g = Gather(nz, x, out, sems)
+    greet(g.peers())
+    g.begin()
+    todo = g.steps()
+    for act, _ in todo:
+        act()
+    g.finish(todo)
+
+
+def all_gather(x, nz, cid):
+    rows, width = x.shape
+    shape = (4, 2, rows, width) if nz == 1 else (nz, 4, 2, rows, width)
+    out = pl.pallas_call(
+        functools.partial(gather_kernel, nz),
+        out_shape=jax.ShapeDtypeStruct(shape, x.dtype), in_specs=[ANY], out_specs=ANY,
+        scratch_shapes=gather_sems(nz),
+        compiler_params=pltpu.CompilerParams(collective_id=cid, has_side_effects=True))(x)
+    return out.reshape(8 * nz * rows, width)
+
+
+def head_kernel(n_dp, x, ids, wp, wo, xa, ids_all, wq, wo_mine, *sems):
+    gs = sems[:9]
+    i_s, i_r, q_s, q_r, u_s, u_r, v_s, v_r, o_s, o_r, l_s = sems[9:]
+    z, s, c, k, xc, yc, dc = place()
+    n_seq = 8
+    rows = wp.shape[0]
+    w = wp.shape[1] // (3 * n_seq)
+    me = z * n_seq + s
+    g = Gather(1, x, xa, gs)
+    everyone = []
+    for i in range(1, n_dp * n_seq):
+        t = lax.rem(me + i, n_dp * n_seq)
+        everyone.append((t // n_seq, lax.rem(t, n_seq)))
+    greet(everyone)
+    sends = []
+    locals_ = []
+
+    def go(*args):
+        d = remote(*args)
+        d.start()
+        sends.append(d)
+
+    def piece(plane, t):
+        return wq.at[pl.ds(pl.multiple_of((plane * n_seq + t) * rows, rows), rows)]
+
+    def cols(t, j):
+        return wp.at[:, pl.ds(pl.multiple_of(j * n_seq * w + t * w, w), w)]
+    seqs = [lax.rem(s + i, n_seq) for i in range(n_seq)]
+    back = [lax.rem(s + n_seq - i, n_seq) for i in range(n_seq)]
+    mine = piece(z, s)
+    for j in range(3):
+        d = pltpu.make_async_copy(cols(s, j), mine.at[:, pl.ds(j * w, w)], l_s.at[j])
+        d.start()
+        locals_.append(d)
+    for i in range(1, n_seq):
+        for j in range(3):
+            go(cols(seqs[i], j), mine.at[:, pl.ds(j * w, w)], q_s.at[i], q_r.at[i], (z, seqs[i]))
+    for i in range(1, n_seq):
+        own = ids_all.at[s]
+        go(ids, own, i_s.at[i], i_r.at[i], (z, seqs[i]))
+    d = pltpu.make_async_copy(ids, ids_all.at[s], l_s.at[3])
+    d.start()
+    locals_.append(d)
+    g.begin()
+    up, down = z < n_dp - 1, z > 0
+    chain = []
+
+    def send_up(h, plane, t):
+        p = piece(plane, t)
+        return remote(p, p, u_s.at[h, t], u_r.at[h, t], (z + 1, s))
+
+    def send_down(h, plane, t):
+        p = piece(plane, t)
+        return remote(p, p, v_s.at[h, t], v_r.at[h, t], (z - 1, s))
+
+    def first(i):
+        if i == 0:
+            for d in locals_[:3]:
+                d.wait()
+        else:
+            p = piece(z, back[i])
+            remote(p, p, q_s.at[i], q_r.at[i], (z, back[i])).wait_recv()
+        t = back[i]
+
+        @pl.when(up)
+        def _():
+            send_up(0, z, t).start()
+
+        @pl.when(down)
+        def _():
+            send_down(0, z, t).start()
+
+    def hop(h, i):
+        t = lax.rem(s + n_seq - i, n_seq)
+
+        @pl.when(z >= h)
+        def _():
+            send_up(h - 1, z - h, t).wait_recv()
+
+            @pl.when(up)
+            def _():
+                send_up(h, z - h, t).start()
+
+        @pl.when(z + h < n_dp)
+        def _():
+            send_down(h - 1, z + h, t).wait_recv()
+
+            @pl.when(down)
+            def _():
+                send_down(h, z + h, t).start()
+    for i in range(n_seq):
+        first(i)
+    dest = me // 4
+    for i in range(n_dp):
+        zt = lax.rem(z + i, n_dp)
+        part = wo_mine.at[pl.ds(pl.multiple_of(lax.rem(me, 4) * rows, rows), rows)]
+        if i == 0:
+            @pl.when(dest != s)
+            def _():
+                remote(wo, part, o_s.at[0], o_r.at[lax.rem(me, 4)], (z, dest)).start()
+
+            @pl.when(dest == s)
+            def _():
+                pltpu.make_async_copy(wo, part, l_s.at[4]).start()
+        else:
+            go(wo, part, o_s.at[i], o_r.at[lax.rem(me, 4)], (zt, dest))
+    todo = g.steps()
+    pending = [lambda h=h, i=i: hop(h, i) for h in range(1, n_dp) for i in range(n_seq)]
+    for act, _ in todo:
+        act()
+        for p in pending[:2]:
+            p()
+        pending = pending[2:]
+    for p in pending:
+        p()
+    for i in range(1, n_seq):
+        own = ids_all.at[back[i]]
+        remote(own, own, i_s.at[i], i_r.at[i], (z, back[i])).wait_recv()
+    for t in range(4):
+        src = s * 4 + t
+        part = wo_mine.at[pl.ds(t * rows, rows)]
+
+        @pl.when(src != me)
+        def _():
+            remote(part, part, o_s.at[0], o_r.at[t], (src // n_seq, lax.rem(src, n_seq))).wait_recv()
+
+        @pl.when(src == me)
+        def _():
+            pltpu.make_async_copy(wo, part, l_s.at[4]).wait()
+    g.finish(todo)
+    for d in sends:
+        d.wait_send()
+    for d in locals_[3:]:
+        d.wait()
+
+    @pl.when(dest != s)
+    def _():
+        remote(wo, wo, o_s.at[0], o_r.at[0], (z, dest)).wait_send()
+    for h in range(n_dp - 1):
+        for i in range(n_seq):
+            @pl.when((z >= h) & up)
+            def _():
+                send_up(h, z - h, back[i]).wait_send()
+
+            @pl.when((z + h < n_dp) & down)
+            def _():
+                send_down(h, z + h, back[i]).wait_send()
+
+
+def head_exchange(x, ids, wp, wo, n_dp, cid):
+    rows, width = x.shape
+    w = wp.shape[1] // 24
+    n = n_dp * 8
+    return pl.pallas_call(
+        functools.partial(head_kernel, n_dp),
+        out_shape=(jax.ShapeDtypeStruct((4, 2, rows, width), x.dtype),
+                   jax.ShapeDtypeStruct((8,) + ids.shape, ids.dtype),
+                   jax.ShapeDtypeStruct((n * wp.shape[0], 3 * w), wp.dtype),
+                   jax.ShapeDtypeStruct((4 * wo.shape[0], wo.shape[1]), wo.dtype)),
+        in_specs=[ANY] * 4, out_specs=(ANY,) * 4,
+        scratch_shapes=gather_sems(1) + [DMA((8,)), DMA((8,)), DMA((8,)), DMA((8,)),
+                                         DMA((n_dp, 8)), DMA((n_dp, 8)), DMA((n_dp, 8)), DMA((n_dp, 8)),
+                                         DMA((n_dp,)), DMA((4,)), DMA((5,))],
+        compiler_params=pltpu.CompilerParams(collective_id=cid, has_side_effects=True))(x, ids, wp, wo)
+
+
+def tail_kernel(n_dp, gq, go_, small, out_q, out_o, out_s, rz, st, rq, ro, rs, z_s, z_r, q_s, q_r, o_s, o_r, m_s, m_r, l_s):
+    z, s, c, k, xc, yc, dc = place()
+    n_seq = 8
+    rows = out_q.shape[0]
+    w = out_q.shape[1] // (3 * n_seq)
+    me = z * n_seq + s
+    n = n_dp * n_seq
+    everyone = []
+    for i in range(1, n):
+        t = lax.rem(me + i, n)
+        everyone.append((t // n_seq, lax.rem(t, n_seq)))
+    greet(everyone)
+    sends = []
+
+    def go(*args):
+        d = remote(*args)
+        d.start()
+        sends.append(d)
+    for i in range(1, n):
+        go(small, rs.at[i], m_s.at[i], m_r.at[i], everyone[i - 1])
+    seqs = [lax.rem(s + i, n_seq) for i in range(n_seq)]
+    order = list(range(1, n_seq)) + [0]
+
+    def part(plane, t):
+        return pl.ds(pl.multiple_of((plane * n_seq + t) * rows, rows), rows)
+    for i in order:
+        for h in range(1, n_dp):
+            zt = lax.rem(z + h, n_dp)
+            go(gq.at[part(zt, seqs[i])], rz.at[h, i], z_s.at[h, i], z_r.at[h, i], (zt, s))
+    for t in range(4):
+        d = s * 4 + t
+        src = go_.at[pl.ds(t * rows, rows)]
+
+        @pl.when(d != me)
+        def _():
+            remote(src, ro.at[z], o_s.at[t], o_r.at[z], (d // n_seq, lax.rem(d, n_seq))).start()
+
+        @pl.when(d == me)
+        def _():
+            pltpu.make_async_copy(src, ro.at[z], l_s).start()
+    for i in order:
+        for h in range(1, n_dp):
+            remote(rz.at[h, i], rz.at[h, i], z_s.at[h, i], z_r.at[h, i], (z, s + 1 - 2 * k)).wait_recv()
+        own = gq.at[part(z, seqs[i])]
+        if i == 0:
+            add_rows(rq.at[0], [own] + [rz.at[h, i] for h in range(1, n_dp)], 0, rows)
+        else:
+            add_rows(st.at[i], [own] + [rz.at[h, i] for h in range(1, n_dp)], 0, rows)
+            go(st.at[i], rq.at[i], q_s.at[i], q_r.at[i], (z, seqs[i]))
+    total = small[...]
+    for i in range(1, n):
+        remote(rs.at[i], rs.at[i], m_s.at[i], m_r.at[i], everyone[0]).wait_recv()
+        total = total + rs[i]
+    out_s[...] = total
+    for t in range(n_dp):
+        from_s = me // 4
+
+        @pl.when((z != t) | (s != from_s))
+        def _():
+            remote(ro.at[t], ro.at[t], o_s.at[0], o_r.at[t], (t, from_s)).wait_recv()
+
+        @pl.when((z == t) & (s == from_s))
+        def _():
+            pltpu.make_async_copy(ro.at[t], ro.at[t], l_s).wait()
+    add_rows(out_o, [ro.at[t] for t in range(n_dp)], 0, rows)
+    for i in range(n_seq):
+        src = lax.rem(s + n_seq - i, n_seq)
+        if i:
+            remote(rq.at[i], rq.at[i], q_s.at[i], q_r.at[i], (z, src)).wait_recv()
+        for j in range(3):
+            at = pl.ds(pl.multiple_of(j * n_seq * w + src * w, w), w)
+            out_q[:, at] = rq[i, :, j * w:(j + 1) * w].astype(f32)
+    for d in sends:
+        d.wait_send()
+    for t in range(4):
+        d = s * 4 + t
+        src = go_.at[pl.ds(t * rows, rows)]
+
+        @pl.when(d != me)
+        def _():
+            remote(src, ro.at[z], o_s.at[t], o_r.at[z], (d // n_seq, lax.rem(d, n_seq))).wait_send()
+
+
+def tail_exchange(gq, gwo, small, n_dp, cid):
+    n = n_dp * 8
+    rows, w3 = gq.shape[0] // n, gq.shape[1]
+    return pl.pallas_call(
+        functools.partial(tail_kernel, n_dp),
+        out_shape=(jax.ShapeDtypeStruct((rows, w3 * 8), f32),
+                   jax.ShapeDtypeStruct((rows, gwo.shape[1]), f32),
+                   jax.ShapeDtypeStruct(small.shape, f32)),
+        in_specs=[VM] * 3, out_specs=(VM,) * 3,
+        scratch_shapes=[pltpu.VMEM((n_dp, 8, rows, w3), bf16), pltpu.VMEM((8, rows, w3), bf16),
+                        pltpu.VMEM((8, rows, w3), bf16), pltpu.VMEM((n_dp, rows, gwo.shape[1]), bf16),
+                        pltpu.VMEM((n,) + small.shape, f32),
+                        DMA((n_dp, 8)), DMA((n_dp, 8)), DMA((8,)), DMA((8,)), DMA((4,)), DMA((n_dp,)),
+                        DMA((n,)), DMA((n,)), DMA],
+        compiler_params=pltpu.CompilerParams(collective_id=cid, has_side_effects=True,
+                                             vmem_limit_bytes=48 * 1024 * 1024))(gq, gwo, small)
 
 
 def dot(a, b, dims):
@@ -48,7 +558,7 @@
     return jnp.concatenate([values[..., half:], -values[..., :half]], axis=-1)
 
 
-def body(n_dp, n_seq, streams, segments, positions, att_proj, attn_out, ff_proj, ff_out,
+def plain_body(n_dp, n_seq, streams, segments, positions, att_proj, attn_out, ff_proj, ff_out,
          mix_in, mix_res, depth, cotangent):
     seq_count, toks, n_str, width = streams.shape
     assert seq_count == 1
@@ -172,12 +682,124 @@
             g_att_proj, g_attn_out, g_ff_proj, g_ff_out, g_mix_in, g_mix_res, g_depth)
 
 
+def fast_body(n_dp, n_seq, streams, segments, positions, att_proj, attn_out, ff_proj, ff_out,
+         mix_in, mix_res, depth, cotangent):
+    seq_count, toks, n_str, width = streams.shape
+    assert seq_count == 1
+    n_all = n_dp * n_seq
+    both = ("dp", "seq")
+    rows = att_proj.shape[0]
+    ffl = ff_out.shape[0]
+    hp = HEADS // n_seq
+    hw = hp * HEAD_DIM
+    length = toks * n_seq
+    scale = HEAD_DIM ** -0.5
+    seq_id = lax.axis_index("seq")
+
+    def mix(parts, weights):
+        total = parts[0] * weights[0]
+        for i in range(1, n_str):
+            total = total + parts[i] * weights[i]
+        return total
+
+    wf = ff_proj.reshape(rows, 2, n_all, ffl).transpose(2, 0, 1, 3).reshape(n_all, rows, 2 * ffl)
+    wf = lax.all_to_all(wf, both, 0, 0, tiled=True).reshape(n_all * rows, 2 * ffl)
+    s_in = [streams[0, :, i].astype(f32) for i in range(n_str)]
+    cot = [cotangent[0, :, i].astype(f32) for i in range(n_str)]
+    d_branch_ff = mix(cot, depth[1]).astype(bf16)
+    dbf = lax.all_gather(d_branch_ff, both, axis=0, tiled=True)
+
+    unit_att, inv_att = norm_stats(mix(s_in, mix_in[0]))
+    ids = jnp.concatenate([segments, positions, jnp.zeros((6, toks), jnp.int32)], axis=0)
+    xa, ids_all, wq, wo = head_exchange(unit_att.astype(bf16), ids, att_proj, attn_out, n_dp, 0)
+    xa = xa.reshape(length, width)
+    seg_all = ids_all[:, 0].reshape(length)
+    pos_all = ids_all[:, 1].reshape(length)
+    proj = dot(xa, wq, ((1,), (0,))).reshape(length, 3, hp, HEAD_DIM)
+    cosine, sine = rope_tables(pos_all)
+    cosine, sine = cosine[:, None], sine[:, None]
+    q = (proj[:, 0] * cosine + turn(proj[:, 0]) * sine).astype(bf16)
+    k = (proj[:, 1] * cosine + turn(proj[:, 1]) * sine).astype(bf16)
+    v = proj[:, 2].astype(bf16)
+    idx = jnp.arange(length, dtype=jnp.int32)
+    allowed = (idx[None, :] <= idx[:, None]) | (
+        (seg_all[None, :] == seg_all[:, None]) & (seg_all[:, None] > 0))
+    scores = jnp.einsum("qhd,khd->hqk", q, k, preferred_element_type=f32) * scale
+    scores = jnp.where(allowed[None], scores, neg_big)
+    top = jnp.max(scores, axis=-1, keepdims=True)
+    p = jnp.exp(scores - top)
+    p = p / jnp.sum(p, axis=-1, keepdims=True)
+    p_low = p.astype(bf16)
+    att = jnp.einsum("hqk,khd->qhd", p_low, v, preferred_element_type=f32)
+    att = att.reshape(length, hw).astype(bf16)
+    branch_att = dot_scatter(att, wo, 1, False, 1)
+
+    mid = [mix(s_in, mix_res[0, :, j]) + depth[0, j] * branch_att for j in range(n_str)]
+    unit_ff, inv_ff = norm_stats(mix(mid, mix_in[1]))
+    xf = all_gather(unit_ff.astype(bf16), n_dp, 2)
+    upgate = dot(xf, wf, ((1,), (0,)))
+    up, gate = upgate[:, :ffl], upgate[:, ffl:]
+    sig = 1.0 / (1.0 + jnp.exp(-gate))
+    hidden = (gate * sig * up).astype(bf16)
+    branch_ff = lax.psum_scatter(dot(hidden, ff_out, ((1,), (0,))).astype(bf16), both,
+                                 scatter_dimension=0, tiled=True).astype(f32)
+
+    d_hidden = dot(dbf, ff_out, ((1,), (1,)))
+    g_ff_out = dot(hidden, dbf, ((0,), (0,)))
+    d_up = d_hidden * gate * sig
+    d_gate = d_hidden * up * (sig * (1.0 + gate * (1.0 - sig)))
+    d_ug = jnp.concatenate([d_up, d_gate], axis=1).astype(bf16)
+    d_unit = dot_scatter(d_ug, wf, n_dp, True, 3)
+    g_wf = dot(xf, d_ug, ((0,), (0,))).astype(bf16).reshape(n_all, rows, 2 * ffl)
+    g_wf = lax.all_to_all(g_wf, both, 0, 0, tiled=True)
+    g_ff_proj = g_wf.reshape(n_all, rows, 2, ffl).transpose(1, 2, 0, 3).reshape(ff_proj.shape).astype(f32)
+    d_mix_ff = norm_back(d_unit, unit_ff, inv_ff)
+
+    d_mid = [mix(cot, mix_res[1, i]) + mix_in[1, i] * d_mix_ff for i in range(n_str)]
+    d_branch_att = mix(d_mid, depth[0]).astype(bf16)
+    dba = all_gather(d_branch_att, 1, 4)
+    d_att = dot(dba, wo, ((1,), (1,))).astype(bf16).reshape(length, hp, HEAD_DIM)
+    g_wo = dot(att, dba, ((0,), (0,))).astype(bf16)
+
+    d_v = jnp.einsum("hqk,qhd->khd", p_low, d_att, preferred_element_type=f32)
+    d_p = jnp.einsum("qhd,khd->hqk", d_att, v, preferred_element_type=f32)
+    d_s = (p * (d_p - jnp.sum(p * d_p, axis=-1, keepdims=True))).astype(bf16)
+    d_q = jnp.einsum("hqk,khd->qhd", d_s, k, preferred_element_type=f32) * scale
+    d_k = jnp.einsum("hqk,qhd->khd", d_s, q, preferred_element_type=f32) * scale
+    d_q = d_q * cosine + turn_back(d_q * sine)
+    d_k = d_k * cosine + turn_back(d_k * sine)
+    d_proj = jnp.stack([d_q, d_k, d_v], axis=1).reshape(length, 3 * hw).astype(bf16)
+    d_unit_att = dot_scatter(d_proj, wq, 1, True, 5)
+    g_wq = dot(xa, d_proj, ((0,), (0,))).astype(bf16)
+    d_mix_att = norm_back(d_unit_att, unit_att, inv_att)
+
+    g_in = [mix(d_mid, mix_res[0, i]) + mix_in[0, i] * d_mix_att for i in range(n_str)]
+    out = [mix(mid, mix_res[1, :, j]) + depth[1, j] * branch_ff for j in range(n_str)]
+
+    def inner(a, b):
+        return jnp.sum(a * b)
+
+    sums = [inner(s, d_mix_att) for s in s_in] + [inner(m, d_mix_ff) for m in mid]
+    sums += [inner(s, d) for s in s_in for d in d_mid] + [inner(m, c) for m in mid for c in cot]
+    sums += [inner(branch_att, d) for d in d_mid] + [inner(branch_ff, c) for c in cot]
+    small = jnp.pad(jnp.stack(sums), (0, 1024 - len(sums))).reshape(8, 128)
+    g_att_proj, g_attn_out, small = tail_exchange(g_wq, g_wo, small, n_dp, 6)
+    small = small.reshape(-1)
+    g_mix_in = small[:8].reshape(2, 4)
+    g_mix_res = small[8:40].reshape(2, 4, 4)
+    g_depth = small[40:48].reshape(2, 4)
+    return (jnp.stack(out, axis=1).astype(bf16)[None], jnp.stack(g_in, axis=1)[None],
+            g_att_proj, g_attn_out, g_ff_proj, g_ff_out, g_mix_in, g_mix_res, g_depth)
+
+
 def solution(mesh):
     n_dp, n_seq = mesh.shape["dp"], mesh.shape["seq"]
     tok = P("dp", "seq", None, None)
     ids = P("dp", "seq")
     mat = P(("dp", "seq"), None)
 
+    body = fast_body if (n_dp, n_seq) == (4, 8) else plain_body
+
     def run(*args):
         return body(n_dp, n_seq, *args)
 

time: 1370 us -> 1040 us (0.76)
  waiting for transfers between devices: 833 us -> 54.4 us
  Pallas kernels: 0 us -> 614 us
  blocking collectives: 161 us -> 0 us
  matrix products: 140 us -> 102 us
  local copies, waits for them, and re-layouts: 58.5 us -> 91.2 us
  other arithmetic: 137 us -> 115 us
  starting transfers between devices: 12.8 us -> 28.5 us
    pallas_call x0 -> x7, Pallas kernels: none -> 614 us  [the longest x3 221 us: dot_scatter(): pl.pallas_call(functools.partial(rs_kernel, nz, trans), out_shape=jax.Sha...]
    reduce_scatter x6 -> x1, waiting for transfers between devices: 473 us -> 54.4 us  [fast_body(): lax.psum_scatter(dot(hidden, ff_out, ((1,), (0,))).astype(bf16), both, sc...]
    all_gather x7 -> x1, waiting for transfers between devices: 326 us -> 0.01 us  [fast_body(): dbf = lax.all_gather(d_branch_ff, both, axis=0, tiled=True)]
    all_to_all x2 -> x0, blocking collectives: 93.6 us -> none  [the longest x1 79.3 us: body(): lax.all_to_all(wf, both, 2, 0, tiled=True).reshape(n_all * rows, 2 * ffl)]
    psum x1 -> x0, blocking collectives: 49.6 us -> none  [body(): lax.psum((g_mix_in, g_mix_res, g_depth), both)]
    dot_general x12 -> x9, matrix products: 119 us -> 81.1 us  [dot(): return lax.dot_general(a, b, (dims, ((), ())), preferred_element_type=f32)]
    all_to_all x2, waiting for transfers between devices: 33.9 us -> 0.01 us  [the longest x1 0.01 us: fast_body(): lax.all_to_all(wf, both, 0, 0, tiled=True).reshape(n_all * rows, 2 * ffl)]
    another operation x0 -> x1, local copies, waits for them, and re-layouts: none -> 31.1 us  [fast_body(): small = jnp.pad(jnp.stack(sums), (0, 1024 - len(sums))).reshape(8, 128)]
  transfers between devices with their start and end apart: 15 -> 4, of which waited for: 12 -> 1; matrix products, arithmetic and copies ran while one was open for 17% -> 13% of each run, Pallas kernels for 0% -> 43%
where the time goes in v2:
time: 1040 us; the launch traced here: 1020 us
  Pallas kernels  614 us (59%)
  other arithmetic  115 us (11%)
  matrix products  102 us (10%)
  local copies, waits for them, and re-layouts  91.2 us (9%)
  waiting for transfers between devices  54.4 us (5%)
  starting transfers between devices  28.5 us (3%)
  between operations  15.1 us (1%)
    pallas_call x3, Pallas kernels, dot_scatter(): pl.pallas_call(functools.partial(rs_kernel, nz, trans), out_shape=jax.Sha...  221 us
    pallas_call x1, Pallas kernels, head_exchange(): pl.pallas_call(functools.partial(head_kernel, n_dp), out_shape=(jax.Shape...  171 us
    pallas_call x1, Pallas kernels, tail_exchange(): pl.pallas_call(functools.partial(tail_kernel, n_dp), out_shape=(jax.Shape...  121 us
    pallas_call x2, Pallas kernels, all_gather(): pl.pallas_call(functools.partial(gather_kernel, nz), out_shape=jax.ShapeD...  100 us
    dot_general x9, matrix products, dot(): return lax.dot_general(a, b, (dims, ((), ())), preferred_element_type=f32)  81.1 us
    reduce_scatter x1, waiting for transfers between devices, fast_body(): lax.psum_scatter(dot(hidden, ff_out, ((1,), (0,))).astype(bf16), both, sc...  54.4 us
    another operation x1, local copies, waits for them, and re-layouts, fast_body(): small = jnp.pad(jnp.stack(sums), (0, 1024 - len(sums))).reshape(8, 128)  31.1 us
    reduce_sum x2, other arithmetic, norm_stats(): mean = jnp.mean(values, axis=-1, keepdims=True)  26.1 us
  transfers between devices with their start and end apart: 4, of which 1 were waited for; matrix products, arithmetic and copies ran while one was open for 13% of the time, Pallas kernels for 43%

profile of v2, /device:TPU:14, one launch (start us, length us, event | category | flops | bytes accessed | tf_op | source)
XLA Modules:
  0.0 1019.6 jit_solution(11013765468315187441)
XLA Ops:
  7.2 1.6 fusion.145
  8.9 8.1 fusion.138
  17.0 5.6 fusion.70
  23.1 3.5 copy.56
  26.6 4.5 reshape.491
  31.1 6.0 all-to-all-start
  38.3 3.0 fusion.139
  41.4 5.9 fusion.136
  48.3 1.0 fusion.111.x
  49.3 171.3 %shard_map.178 = (bf16[4,2,128,2048]{3,2,1,0:T(8,128)(2,1)}, s32[8,8,128]{2,1,0:T(8,128)}, bf16[2048,768]{1,0:T(8,128)(2,1)}, bf16[256,2048]{1,0:T(8,128)(2,1)}) custom-call(bf16[128,2048]{1,0:T(8,128)(2,1)} %fusion.111.x, s32[8,128]{1,0:T(8,128)} %add_add_fusion.ids, bf16[64,6144]{1,0:T(8,128)(2,1)} %wp.1, bf16[64,2048]{1,0:T(8,128)(2,1)} %wo.1), custom_call_target="tpu_custom_call" | custom-call | tf_op jit(solution)/shard_map/pallas_call | solution.py:412
  220.6 4.6 copy.85
  225.2 0.8 slice_convert_fusion.1
  226.1 2.7 broadcast_multiply_fusion.3
  228.9 6.2 fusion.148
  235.6 1.1 copy-done.15
  237.4 0.9 fusion.4
  238.3 5.8 fusion.147
  244.1 4.5 fusion.13
  248.6 1.0 copy.86.a
  249.6 25.7 %shard_map.179 = f32[128,2048]{1,0:T(8,128)} custom-call(bf16[1024,256]{1,0:T(8,128)(2,1)} %copy.86.a, bf16[256,2048]{1,0:T(8,128)(2,1)} %get-tuple-element.19.b), custom_call_target="tpu_custom_call" | custom-call | tf_op jit(solution)/shard_map/pallas_call | solution.py:127
  276.7 20.2 %fusion.131 = (f32[128]{0:T(128)S(1)}, f32[128,2048]{1,0:T(8,128)S(1)}, f32[128,2048]{1,0:T(8,128)S(1)}, f32[128,2048]{1,0:T(8,128)}, f32[128,2048]{1,0:T(8,128)}, /*index=5*/f32[128,2048]{1,0:T(8,128)}) fusion(f32[]{:T(128)} %bitcast.52, f32[]{:T(128)} %bitcast.51, f32[]{:T(128)} %bitcast.50, f32[]{:T(128)} %bitcast.49, f32[128,2048]{1,0:T(8,128)} %shard_map.179, ...), kind=kLoop, calls=%fused_computation.285 | loop fusion | flops 12582784 | bytes 8389216 | tf_op jit(solution)/shard_map/reduce_sum | solution.py:531
  297.1 1.0 fusion.112.x
  298.1 76.7 %shard_map.180 = bf16[4,4,2,128,2048]{4,3,2,1,0:T(8,128)(2,1)} custom-call(bf16[128,2048]{1,0:T(8,128)(2,1)} %fusion.112.x), custom_call_target="tpu_custom_call" | custom-call | tf_op jit(solution)/shard_map/pallas_call | solution.py:251
  374.8 15.0 %fusion.149 = f32[4096,512]{1,0:T(8,128)} fusion(bf16[4096,2048]{1,0:T(8,128)(2,1)} %bitcast.230, bf16[2048,512]{1,0:T(8,128)(2,1)} %bitcast.55.b), kind=kOutput, calls=%fused_computation.298 | convolution fusion | flops 8589934592 | bytes 27262976 | tf_op jit(solution)/shard_map/dot_general | solution.py:527
  389.8 13.3 %multiply_convert_fusion.2 = (bf16[4096,256]{1,0:T(8,128)(2,1)}, bf16[4096,256]{1,0:T(8,128)(2,1)}, bf16[4096,256]{1,0:T(8,128)(2,1)}) fusion(f32[4096,512]{1,0:T(8,128)} %fusion.149, bf16[4096,2048]{1,0:T(8,128)(2,1)} %all-gather.2.cloned.1.call-done, bf16[256,2048]{1,0:T(8,128)(2,1)S(1)} %copy-done), kind=kOutput, calls=%fused_computation.10 | convolution fusion | flops 4311744512 | bytes 32505856 | tf_op jit(solution)/shard_map/dot_general | solution.py:527
  403.1 9.7 convolution_convert_fusion
  412.8 14.6 %convolution_convert_fusion.2 = bf16[2048,512]{1,0:T(8,128)(2,1)} fusion(bf16[4096,2048]{1,0:T(8,128)(2,1)} %bitcast.231, bf16[4096,256]{1,0:T(8,128)(2,1)} %get-tuple-element.122, bf16[4096,256]{1,0:T(8,128)(2,1)} %get-tuple-element.121), kind=kOutput, calls=%fused_computation.101 | convolution fusion | flops 8599371776 | bytes 23068672 | tf_op jit(solution)/shard_map/dot_general | solution.py:527
  427.4 22.1 %all-to-all-start.1 = ((bf16[32,64,512]{2,1,0:T(8,128)(2,1)}), bf16[32,64,512]{2,1,0:T(8,128)(2,1)}, u32[]{:S(2)}, u32[]{:S(2)}) async-start(bf16[32,64,512]{2,1,0:T(8,128)(2,1)} %bitcast.244), calls=%async_computation.2 | async-start | bytes 4194304 | tf_op jit(solution)/shard_map/all_to_all | solution.py:754
  449.5 4.5 pad_maximum_fusion.a
  454.1 167.5 %shard_map.181 = f32[128,2048]{1,0:T(8,128)} custom-call(bf16[4096,512]{1,0:T(8,128)(2,1)} %pad_maximum_fusion.a, bf16[2048,512]{1,0:T(8,128)(2,1)} %bitcast.55.b), custom_call_target="tpu_custom_call" | custom-call | tf_op jit(solution)/shard_map/pallas_call | solution.py:127
  621.6 1.5 fusion.126
  623.1 12.5 %fusion.150 = f32[256,2048]{1,0:T(8,128)} fusion(bf16[4096,256]{1,0:T(8,128)(2,1)} %get-tuple-element.123, bf16[4096,2048]{1,0:T(8,128)(2,1)} %all-gather.2.cloned.1.call-done), kind=kOutput, calls=%fused_computation.299 | convolution fusion | flops 4294967296 | bytes 20971520 | tf_op jit(solution)/shard_map/dot_general | solution.py:527
  635.6 5.8 reshape.508
  641.4 4.7 copy.71
  646.1 4.4 copy.97
  650.5 54.4 %reduce-scatter.2.cloned.1.call-done = bf16[128,2048]{1,0:T(8,128)(2,1)} async-done(((bf16[4096,2048]{1,0:T(8,128)(2,1)}), bf16[128,2048]{1,0:T(8,128)(2,1)}) %reduce-scatter.2.cloned.1.call-update) | async-done | bytes 524304 | tf_op jit(solution)/shard_map/reduce_scatter | solution.py:744
  704.9 4.9 fusion.101
  709.8 18.3 %add_convert_fusion = (bf16[128,2048]{1,0:T(8,128)(2,1)}, f32[128,2048]{1,0:T(8,128)S(1)}, f32[128,2048]{1,0:T(8,128)}, f32[128,2048]{1,0:T(8,128)}, f32[128,2048]{1,0:T(8,128)}) fusion(f32[]{:T(128)} %bitcast.46, f32[]{:T(128)} %bitcast.40, f32[]{:T(128)} %bitcast.34, f32[]{:T(128)} %bitcast.8, f32[128,2048]{1,0:T(8,128)S(1)} %get-tuple-element.97, ...), kind=kLoop, calls=%fused_computation.231 | loop fusion | flops 12582912 | bytes 7864416 | tf_op jit(solution)/shard_map/convert_element_type | solution.py:759
  728.1 23.3 %shard_map.182 = bf16[4,2,128,2048]{3,2,1,0:T(8,128)(2,1)} custom-call(bf16[128,2048]{1,0:T(8,128)(2,1)} %get-tuple-element.99.x), custom_call_target="tpu_custom_call" | custom-call | tf_op jit(solution)/shard_map/pallas_call | solution.py:251
  751.5 3.6 convolution_convert_fusion.4
  755.1 1.3 convolution_convert_fusion.3.go_
  756.4 5.1 fusion.10
  761.5 2.8 multiply_reduce_fusion
  764.3 2.5 multiply_convert_fusion
  766.8 1.5 convolution_bitcast_fusion
  768.4 0.9 broadcast_multiply_fusion.1
  769.5 0.8 copy-done.29
  770.9 1.3 maximum_convert_fusion
  772.3 2.7 copy.87.a
  774.9 28.3 %shard_map.183 = f32[128,2048]{1,0:T(8,128)} custom-call(bf16[1024,768]{1,0:T(8,128)(2,1)} %copy.87.a, bf16[2048,768]{1,0:T(8,128)(2,1)} %get-tuple-element.17.b), custom_call_target="tpu_custom_call" | custom-call | tf_op jit(solution)/shard_map/pallas_call | solution.py:127
  803.2 1.5 fusion.125
  804.8 5.5 multiply_reduce_fusion.1
  810.4 8.2 add_bitcast_fusion.2
  818.6 8.7 add_bitcast_fusion.3
  827.3 6.9 fusion.117
  834.2 7.0 fusion.119
  841.5 2.9 copy.72
  844.4 4.9 convolution_convert_fusion.1.gq
  849.4 31.1 %stack.251 = f32[48]{0:T(128)S(1)} concatenate(f32[1]{0:T(128)} %bitcast.98, f32[1]{0:T(128)} %bitcast.99, f32[1]{0:T(128)} %bitcast.100, f32[1]{0:T(128)} %bitcast.101, f32[1]{0:T(128)} %bitcast.102, f32[1]{0:T(128)} %bitcast.103, f32[1]{0:T(128)} %bitcast.104, f32[1]{0:T(128)} %bitcast.105, f32[1]{0:T(128)} %bitcast.106, f32[1]{0:T(128)} %bitcast.107, f32[1]{0:T(128)} %bitcast.108, ...), dimensions={0} | concatenate | bytes 384 | tf_op jit(solution)/shard_map/stack | solution.py:785
  880.5 121.4 %shard_map.184 = (f32[64,6144]{1,0:T(8,128)S(1)}, f32[64,2048]{1,0:T(8,128)S(1)}, f32[8,128]{1,0:T(8,128)S(1)}) custom-call(bf16[2048,768]{1,0:T(8,128)(2,1)} %convolution_convert_fusion.1.gq, bf16[256,2048]{1,0:T(8,128)(2,1)S(1)} %convolution_convert_fusion.3.go_, f32[8,128]{1,0:T(8,128)S(1)} %pad_bitcast_fusion.small), custom_call_target="tpu_custom_call" | custom-call | tf_op jit(solution)/shard_map/pallas_call | solution.py:511
  1003.3 2.4 maximum_bitcast_fusion
  1005.8 4.7 copy.73
  1010.5 1.1 copy.116
  1011.7 0.8 copy.117
  (126 shorter events, 8.3 us)
Async XLA Ops:
  7.2 382.6 %copy-start = (bf16[256,2048]{1,0:T(8,128)(2,1)S(1)}, bf16[256,2048]{1,0:T(8,128)(2,1)}, u32[]{:S(2)}) copy-start(bf16[256,2048]{1,0:T(8,128)(2,1)} %param.17) | copy-start | bytes 3145732
  7.2 382.6 %all-gather.2.cloned.1.call-start = ((), (), s32[]{:S(2)}) async-start(), calls=%async_computation.4 | async-start | bytes 17301504 | tf_op jit(solution)/shard_map/all_gather | solution.py:710
  17.0 5.6 copy-start.26
  26.6 11.0 %copy-start.34 = (f32[2,4]{1,0:T(2,128)S(1)}, f32[2,4]{1,0:T(2,128)}, u32[]{:S(2)}) copy-start(f32[2,4]{1,0:T(2,128)} %param.18) | copy-start | bytes 100
  26.6 11.7 %copy-start.13 = (bf16[1,128,4,2048]{3,2,1,0:T(4,128)(2,1)S(1)}, bf16[1,128,4,2048]{3,2,1,0:T(4,128)(2,1)}, u32[]{:S(2)}) copy-start(bf16[1,128,4,2048]{3,2,1,0:T(4,128)(2,1)} %param.11) | copy-start | bytes 6291460
  31.1 343.6 %all-to-all-start = ((bf16[32,64,512]{2,1,0:T(8,128)(2,1)}), bf16[32,64,512]{2,1,0:T(8,128)(2,1)}, u32[]{:S(2)}, u32[]{:S(2)}) async-start(bf16[32,64,512]{2,1,0:T(8,128)(2,1)} %reshape.491), calls=%async_computation | async-start | bytes 4194304 | tf_op jit(solution)/shard_map/all_to_all | solution.py:706
  37.2 667.7 %reduce-scatter.2.cloned.1.call-start = ((), (), s32[]{:S(2)}) async-start(), calls=%async_computation.3 | async-start | bytes 17301504 | tf_op jit(solution)/shard_map/reduce_scatter | solution.py:744
  41.3 6.2 copy-start.39
  41.4 6.2 copy-start.40
  47.3 1.0 copy-start.2
  47.3 1.0 copy-start.35
  47.6 0.7 copy-start.37
  235.1 1.7 copy-start.15
  237.4 6.7 copy-start.24
  237.4 6.7 copy-start.27
  244.1 31.2 %copy-start.33 = (f32[2,4,4]{2,1,0:T(4,128)S(1)}, f32[2,4,4]{2,1,0:T(4,128)}, u32[]{:S(2)}) copy-start(f32[2,4,4]{2,1,0:T(4,128)} %param.19) | copy-start | bytes 388
  248.5 28.1 %copy-start.31 = (bf16[2,128,1024]{2,1,0:T(8,128)(2,1)}, bf16[2,128,1024]{2,1,0:T(8,128)(2,1)S(1)}, u32[]{:S(2)}) copy-start(bf16[2,128,1024]{2,1,0:T(8,128)(2,1)S(1)} %fusion.13) | copy-start | bytes 1572868
  296.8 408.0 %copy-start.7 = (f32[128,2048]{1,0:T(8,128)}, f32[128,2048]{1,0:T(8,128)S(1)}, u32[]{:S(2)}) copy-start(f32[128,2048]{1,0:T(8,128)S(1)} %get-tuple-element.111) | copy-start | bytes 3145732
  427.4 208.1 %all-to-all-start.1 = ((bf16[32,64,512]{2,1,0:T(8,128)(2,1)}), bf16[32,64,512]{2,1,0:T(8,128)(2,1)}, u32[]{:S(2)}, u32[]{:S(2)}) async-start(bf16[32,64,512]{2,1,0:T(8,128)(2,1)} %bitcast.244), calls=%async_computation.2 | async-start | bytes 4194304 | tf_op jit(solution)/shard_map/all_to_all | solution.py:754
  646.1 58.8 %copy-start.9 = (f32[128,2048]{1,0:T(8,128)S(1)}, f32[128,2048]{1,0:T(8,128)}, u32[]{:S(2)}) copy-start(f32[128,2048]{1,0:T(8,128)} %get-tuple-element.112) | copy-start | bytes 3145732
  704.8 4.9 copy-start.16
  704.8 4.9 copy-start.17
  704.9 4.9 copy-start.18
  704.9 4.9 copy-start.19
  728.1 23.4 %copy-start.30 = (bf16[256,2048]{1,0:T(8,128)(2,1)S(1)}, bf16[256,2048]{1,0:T(8,128)(2,1)}, u32[]{:S(2)}) copy-start(bf16[256,2048]{1,0:T(8,128)(2,1)} %get-tuple-element.19.b) | copy-start | bytes 3145732
  751.5 3.7 copy-start.23
  751.5 3.7 copy-start.32
  755.1 6.4 slice-start
  756.4 5.1 slice-start.1
  764.3 2.5 copy-start.28
  766.8 1.6 copy-start.20
  766.8 1.6 copy-start.25
  769.3 1.0 copy-start.29
  772.3 30.9 %copy-start.3 = (f32[128,2048]{1,0:T(8,128)S(1)}, f32[128,2048]{1,0:T(8,128)}, u32[]{:S(2)}) copy-start(f32[128,2048]{1,0:T(8,128)} %copy-done.2) | copy-start | bytes 3145732
  772.3 30.9 %copy-start.36 = (f32[128]{0:T(128)S(1)}, f32[128]{0:T(128)}, u32[]{:S(2)}) copy-start(f32[128]{0:T(128)} %copy-done.35) | copy-start | bytes 1540
  772.3 31.0 %copy-start.38 = (f32[128]{0:T(128)S(1)}, f32[128]{0:T(128)}, u32[]{:S(2)}) copy-start(f32[128]{0:T(128)} %copy-done.37) | copy-start | bytes 1540
  774.9 29.8 %copy-start.21 = (bf16[128,2048]{1,0:T(8,128)(2,1)S(1)}, bf16[128,2048]{1,0:T(8,128)(2,1)}, u32[]{:S(2)}) copy-start(bf16[128,2048]{1,0:T(8,128)(2,1)} %get-tuple-element.117) | copy-start | bytes 1572868
  804.8 5.6 copy-start.4
  804.8 5.6 copy-start.5
  804.8 5.6 copy-start.6
  818.6 8.7 copy-start.8
  818.6 8.7 copy-start.10
  818.6 8.7 copy-start.11
  818.6 8.7 copy-start.12
  818.6 8.7 copy-start.22
  841.2 3.2 copy-start.14
  841.2 3.2 copy-start.41
  1005.8 6.7 copy-start.1
Sparse Core Ops, SparseCore 0:
  22.7 180.2 all-gather.1
  412.9 291.8 reduce-scatter.1

commit v3 on v2

--- a/solution.py
+++ b/solution.py
@@ -48,91 +48,6 @@
         dst[rows, :] = total.astype(dst.dtype)
         return 0
     lax.fori_loop(0, count // step, one, 0)
-
-def rs_kernel(nz, trans, a, b, out, pp, po, ra, rd, fx, fy, fz, p_s, p_r, d_s, d_r, x_s, x_r, y_s, y_r, z_s, z_r):
-    z, s, c, k, xc, yc, dc = place()
-    rows = out.shape[0]; half = rows // 2
-    partner = (z, s + 1 - 2 * k)
-    dev_x = (z, 2 * xc + k); dev_y = (z, 2 * yc + k)
-    zt = [lax.rem(z + i, nz) for i in range(1, nz)]
-    greet([partner, dev_x, dev_y] + [(t, s) for t in zt])
-    dims = (((1,), (1,)), ((), ())) if trans else (((1,), (0,)), ((), ()))
-    cx = lax.rem(c, 2); cy = c // 2
-    def produce(i, _):
-        j = lax.rem(i, 4)
-        rx = jnp.where(j < 2, 1, 0); ry = jnp.where(lax.rem(j, 2) == 0, 1, 0) * jnp.where(j < 3, 1, 0)
-        px = cx + rx - 2 * cx * rx; py = cy + ry - 2 * cy * ry
-        blk = px + 2 * py
-        if nz > 1:
-            blk = blk + lax.rem(z + 1 + i // 4, nz) * 4
-        at = pl.ds(pl.multiple_of(blk * 2 * rows, 2 * rows), 2 * rows)
-        both = lax.dot_general(a[at, :], b[...], dims, preferred_element_type=f32).astype(bf16)
-        pp[i, 0] = both[:rows]
-        pp[i, 1] = both[rows:]
-        remote(pp.at[i, 1 - k], ra.at[i], p_s.at[i], p_r.at[i], partner).start()
-        return 0
-    lo, hi = pl.ds(0, half), pl.ds(half, half)
-    def first(zi):
-        for j in range(4):
-            q = zi * 4 + j
-            remote(ra.at[q], ra.at[q], p_s.at[q], p_r.at[q], partner).wait_recv()
-            add_rows(po.at[q], [pp.at[q, k], ra.at[q]], 0, rows)
-            if j == 0:
-                remote(po.at[q, lo], rd.at[zi, lo], d_s.at[zi, 0], d_r.at[zi, 0], dev_x).start()
-                remote(po.at[q, hi], rd.at[zi, hi], d_s.at[zi, 1], d_r.at[zi, 1], dev_y).start()
-            if j == 1:
-                remote(po.at[q, lo], fx.at[zi, lo], x_s.at[zi, 0], x_r.at[zi, 0], dev_x).start()
-            if j == 2:
-                remote(po.at[q, hi], fy.at[zi, hi], y_s.at[zi, 1], y_r.at[zi, 1], dev_y).start()
-    def second(zi):
-        qx, qy = zi * 4 + 1, zi * 4 + 2
-        remote(rd.at[zi, lo], rd.at[zi, lo], d_s.at[zi, 0], d_r.at[zi, 0], dev_x).wait_recv()
-        add_rows(po.at[qy], [po.at[qy], rd.at[zi]], 0, half)
-        remote(po.at[qy, lo], fy.at[zi, lo], y_s.at[zi, 0], y_r.at[zi, 0], dev_y).start()
-        remote(rd.at[zi, hi], rd.at[zi, hi], d_s.at[zi, 1], d_r.at[zi, 1], dev_y).wait_recv()
-        add_rows(po.at[qx], [po.at[qx], rd.at[zi]], half, half)
-        remote(po.at[qx, hi], fx.at[zi, hi], x_s.at[zi, 1], x_r.at[zi, 1], dev_x).start()
-    def third(zi):
-        q = zi * 4 + 3
-        for h, part in ((0, lo), (1, hi)):
-            remote(fx.at[zi, part], fx.at[zi, part], x_s.at[zi, h], x_r.at[zi, h], dev_x).wait_recv()
-            remote(fy.at[zi, part], fy.at[zi, part], y_s.at[zi, h], y_r.at[zi, h], dev_y).wait_recv()
-        if zi < nz - 1:
-            add_rows(po.at[q], [po.at[q], fx.at[zi], fy.at[zi]], 0, rows)
-            remote(po.at[q], fz.at[zi], z_s.at[zi], z_r.at[zi], (zt[zi], s)).start()
-        else:
-            for i in range(nz - 1):
-                remote(fz.at[i], fz.at[i], z_s.at[i], z_r.at[i], (zt[i], s)).wait_recv()
-            add_rows(out, [po.at[q], fx.at[zi], fy.at[zi]] + [fz.at[i] for i in range(nz - 1)], 0, rows)
-    lax.fori_loop(0, 4, produce, 0)
-    for t in range(nz + 2):
-        if t + 1 < nz: lax.fori_loop(4 * t + 4, 4 * t + 8, produce, 0)
-        if t < nz: first(t)
-        if 0 <= t - 1 < nz: second(t - 1)
-        if 0 <= t - 2 < nz: third(t - 2)
-    for q in range(4 * nz):
-        remote(ra.at[q], ra.at[q], p_s.at[q], p_r.at[q], partner).wait_send()
-    for zi in range(nz):
-        for h, part in ((0, lo), (1, hi)):
-            remote(rd.at[zi, part], rd.at[zi, part], d_s.at[zi, h], d_r.at[zi, h], dev_x).wait_send()
-            remote(fx.at[zi, part], fx.at[zi, part], x_s.at[zi, h], x_r.at[zi, h], dev_x).wait_send()
-            remote(fy.at[zi, part], fy.at[zi, part], y_s.at[zi, h], y_r.at[zi, h], dev_y).wait_send()
-    for i in range(nz - 1):
-        remote(fz.at[i], fz.at[i], z_s.at[i], z_r.at[i], (zt[i], s)).wait_send()
-
-def dot_scatter(a, b, nz, trans, cid):
-    rows = a.shape[0] // (8 * nz); width = b.shape[0] if trans else b.shape[1]
-    m = max(nz - 1, 1)
-    blk = lambda n: pltpu.VMEM((n, rows, width), bf16)
-    return pl.pallas_call(
-        functools.partial(rs_kernel, nz, trans),
-        out_shape=jax.ShapeDtypeStruct((rows, width), f32),
-        in_specs=[VM, VM], out_specs=VM,
-        scratch_shapes=[pltpu.VMEM((4*nz, 2, rows, width), bf16), blk(4*nz), blk(4*nz), blk(nz), blk(nz), blk(nz), blk(m),
-                        DMA((4*nz,)), DMA((4*nz,)), DMA((nz,2)), DMA((nz,2)), DMA((nz,2)), DMA((nz,2)), DMA((nz,2)), DMA((nz,2)), DMA((m,)), DMA((m,))],
-        compiler_params=pltpu.CompilerParams(collective_id=cid, has_side_effects=True, vmem_limit_bytes=60*1024*1024),
-    )(a, b)
-
 
 class Gather:
     def __init__(self, nz, x, out, sems):
@@ -422,105 +337,368 @@
         compiler_params=pltpu.CompilerParams(collective_id=cid, has_side_effects=True))(x, ids, wp, wo)
 
 
-def tail_kernel(n_dp, gq, go_, small, out_q, out_o, out_s, rz, st, rq, ro, rs, z_s, z_r, q_s, q_r, o_s, o_r, m_s, m_r, l_s):
-    z, s, c, k, xc, yc, dc = place()
-    n_seq = 8
-    rows = out_q.shape[0]
-    w = out_q.shape[1] // (3 * n_seq)
-    me = z * n_seq + s
-    n = n_dp * n_seq
-    everyone = []
+class Scatter:
+    def __init__(self, nz, trans, a, b, out, bufs, sems):
+        self.nz, self.a, self.b, self.out = nz, a, b, out
+        self.pp, self.po, self.ra, self.rd, self.fx, self.fy, self.fz = bufs
+        (self.p_s, self.p_r, self.d_s, self.d_r, self.x_s, self.x_r, self.y_s, self.y_r, self.z_s, self.z_r) = sems
+        self.z, self.s, self.c, self.k, self.xc, self.yc, self.dc = place()
+        z, s, k = self.z, self.s, self.k
+        self.rows = out.shape[0]
+        self.half = self.rows // 2
+        self.parts = (pl.ds(0, self.half), pl.ds(self.half, self.half))
+        self.partner = (z, s + 1 - 2 * k)
+        self.dev_x = (z, 2 * self.xc + k)
+        self.dev_y = (z, 2 * self.yc + k)
+        self.zt = [lax.rem(z + i, nz) for i in range(1, nz)]
+        self.dims = (((1,), (1,)), ((), ())) if trans else (((1,), (0,)), ((), ()))
+
+    def peers(self):
+        return [self.partner, self.dev_x, self.dev_y] + [(t, self.s) for t in self.zt]
+
+    def produce(self, i, _):
+        cx, cy, rows, k = lax.rem(self.c, 2), self.c // 2, self.rows, self.k
+        j = lax.rem(i, 4)
+        rx = jnp.where(j < 2, 1, 0)
+        ry = jnp.where(lax.rem(j, 2) == 0, 1, 0) * jnp.where(j < 3, 1, 0)
+        blk = cx + rx - 2 * cx * rx + 2 * (cy + ry - 2 * cy * ry)
+        if self.nz > 1:
+            blk = blk + lax.rem(self.z + 1 + i // 4, self.nz) * 4
+        at = pl.ds(pl.multiple_of(blk * 2 * rows, 2 * rows), 2 * rows)
+        both = lax.dot_general(self.a[at, :], self.b[...], self.dims, preferred_element_type=f32).astype(bf16)
+        lower, upper = both[:rows], both[rows:]
+        self.pp[i] = jnp.where(k == 0, upper, lower)
+        self.po[i] = jnp.where(k == 0, lower, upper)
+        remote(self.pp.at[i], self.ra.at[i], self.p_s.at[i], self.p_r.at[i], self.partner).start()
+        return 0
+
+    def make(self, g):
+        lax.fori_loop(4 * g, 4 * g + 4, self.produce, 0)
+
+    def first(self, zi, j):
+        q = zi * 4 + j
+        po, (lo, hi) = self.po, self.parts
+        remote(self.ra.at[q], self.ra.at[q], self.p_s.at[q], self.p_r.at[q], self.partner).wait_recv()
+        add_rows(po.at[q], [po.at[q], self.ra.at[q]], 0, self.rows)
+        if j == 0:
+            remote(po.at[q, lo], self.rd.at[zi, lo], self.d_s.at[zi, 0], self.d_r.at[zi, 0], self.dev_x).start()
+            remote(po.at[q, hi], self.rd.at[zi, hi], self.d_s.at[zi, 1], self.d_r.at[zi, 1], self.dev_y).start()
+        if j == 1:
+            remote(po.at[q, lo], self.fx.at[zi, lo], self.x_s.at[zi, 0], self.x_r.at[zi, 0], self.dev_x).start()
+        if j == 2:
+            remote(po.at[q, hi], self.fy.at[zi, hi], self.y_s.at[zi, 1], self.y_r.at[zi, 1], self.dev_y).start()
+
+    def second(self, zi):
+        po, rd, (lo, hi) = self.po, self.rd, self.parts
+        qx, qy = zi * 4 + 1, zi * 4 + 2
+        remote(rd.at[zi, lo], rd.at[zi, lo], self.d_s.at[zi, 0], self.d_r.at[zi, 0], self.dev_x).wait_recv()
+        add_rows(po.at[qy], [po.at[qy], rd.at[zi]], 0, self.half)
+        remote(po.at[qy, lo], self.fy.at[zi, lo], self.y_s.at[zi, 0], self.y_r.at[zi, 0], self.dev_y).start()
+        remote(rd.at[zi, hi], rd.at[zi, hi], self.d_s.at[zi, 1], self.d_r.at[zi, 1], self.dev_y).wait_recv()
+        add_rows(po.at[qx], [po.at[qx], rd.at[zi]], self.half, self.half)
+        remote(po.at[qx, hi], self.fx.at[zi, hi], self.x_s.at[zi, 1], self.x_r.at[zi, 1], self.dev_x).start()
+
+    def third(self, zi):
+        q, nz, po, fx, fy, fz = zi * 4 + 3, self.nz, self.po, self.fx, self.fy, self.fz
+        for h, part in enumerate(self.parts):
+            remote(fx.at[zi, part], fx.at[zi, part], self.x_s.at[zi, h], self.x_r.at[zi, h], self.dev_x).wait_recv()
+            remote(fy.at[zi, part], fy.at[zi, part], self.y_s.at[zi, h], self.y_r.at[zi, h], self.dev_y).wait_recv()
+        if zi < nz - 1:
+            add_rows(po.at[q], [po.at[q], fx.at[zi], fy.at[zi]], 0, self.rows)
+            remote(po.at[q], fz.at[zi], self.z_s.at[zi], self.z_r.at[zi], (self.zt[zi], self.s)).start()
+        else:
+            for i in range(nz - 1):
+                remote(fz.at[i], fz.at[i], self.z_s.at[i], self.z_r.at[i], (self.zt[i], self.s)).wait_recv()
+            add_rows(self.out, [po.at[q], fx.at[zi], fy.at[zi]] + [fz.at[i] for i in range(nz - 1)], 0, self.rows)
+
+    def steps(self):
+        nz = self.nz
+        todo = [lambda: self.make(0)]
+        for t in range(nz + 2):
+            if t + 1 < nz:
+                todo.append(lambda t=t: self.make(t + 1))
+            if t < nz:
+                todo += [lambda t=t, j=j: self.first(t, j) for j in range(4)]
+            if 0 <= t - 1 < nz:
+                todo.append(lambda t=t: self.second(t - 1))
+            if 0 <= t - 2 < nz:
+                todo.append(lambda t=t: self.third(t - 2))
+        return todo
+
+    def finish(self):
+        for q in range(4 * self.nz):
+            remote(self.ra.at[q], self.ra.at[q], self.p_s.at[q], self.p_r.at[q], self.partner).wait_send()
+        for zi in range(self.nz):
+            for h, part in enumerate(self.parts):
+                for buf, a, b in ((self.rd, self.d_s, self.d_r), (self.fx, self.x_s, self.x_r), (self.fy, self.y_s, self.y_r)):
+                    remote(buf.at[zi, part], buf.at[zi, part], a.at[zi, h], b.at[zi, h], self.dev_x).wait_send()
+        for i in range(self.nz - 1):
+            remote(self.fz.at[i], self.fz.at[i], self.z_s.at[i], self.z_r.at[i], self.dev_x).wait_send()
+
+
+def scatter_bufs(nz, rows, width):
+    m = max(nz - 1, 1)
+    return [pltpu.VMEM((n, rows, width), bf16) for n in (4 * nz, 4 * nz, 4 * nz, nz, nz, nz, m)]
+
+
+def scatter_sems(nz):
+    m = max(nz - 1, 1)
+    return [DMA((4 * nz,)), DMA((4 * nz,))] + [DMA((nz, 2))] * 6 + [DMA((m,)), DMA((m,))]
+
+
+def params(cid, mib):
+    return pltpu.CompilerParams(collective_id=cid, has_side_effects=True, vmem_limit_bytes=mib * 1024 * 1024)
+
+
+def scatter_gather_kernel(nz, trans, a, b, x, out, xg, *rest):
+    bufs, sems, gs = rest[:7], rest[7:17], rest[17:]
+    sc = Scatter(1, trans, a, b, out, bufs, sems)
+    g = Gather(nz, x, xg, gs)
+    greet(g.peers())
+    todo = g.steps()
+    sc_todo = sc.steps()
+    sc_todo[0]()
+    g.begin()
+    rest_ = sc_todo[1:]
+    for act, _ in todo:
+        if rest_:
+            rest_.pop(0)()
+        act()
+    for act in rest_:
+        act()
+    sc.finish()
+    g.finish(todo)
+
+
+def scatter_gather(a, b, x, nz, trans, cid):
+    rows, width = x.shape
+    out, xg = pl.pallas_call(
+        functools.partial(scatter_gather_kernel, nz, trans),
+        out_shape=(jax.ShapeDtypeStruct((rows, width), f32), jax.ShapeDtypeStruct((nz, 4, 2, rows, width), x.dtype)),
+        in_specs=[VM, VM, ANY], out_specs=(VM, ANY),
+        scratch_shapes=scatter_bufs(1, rows, width) + scatter_sems(1) + gather_sems(nz),
+        compiler_params=params(cid, 48))(a, b, x)
+    return out, xg.reshape(nz * 8 * rows, width)
+
+
+class Owners:
+    def __init__(self, n_dp, gq, go, out_q, out_o, bufs, sems):
+        self.n_dp, self.gq, self.go, self.out_q, self.out_o = n_dp, gq, go, out_q, out_o
+        self.dn, self.up, self.st, self.rq, self.ro = bufs
+        (self.dn_s, self.dn_r, self.up_s, self.up_r, self.q_s, self.q_r, self.o_s, self.o_r, self.l_s) = sems
+        self.z, self.s = lax.axis_index("dp"), lax.axis_index("seq")
+        self.rows = out_q.shape[0]
+        self.w = out_q.shape[1] // 24
+        self.me = self.z * 8 + self.s
+
+    def part(self, plane, t):
+        return self.gq.at[pl.ds(pl.multiple_of((plane * 8 + t) * self.rows, self.rows), self.rows)]
+
+    def piece(self, i):
+        return lax.rem(self.s + i, 8)
+
+    def down(self, h, i):
+        z = self.z
+        own = self.part(z - h, self.piece(i))
+        if h < self.n_dp - 1:
+            @pl.when((z >= h) & (z < self.n_dp - 1))
+            def _():
+                buf = self.dn.at[h, i]
+                remote(buf, buf, self.dn_s.at[h, i], self.dn_r.at[h, i], (z + 1, self.s)).wait_recv()
+                add_rows(buf, [own, buf], 0, self.rows)
+                remote(buf, self.dn.at[h - 1, i], self.dn_s.at[h - 1, i], self.dn_r.at[h - 1, i], (z - 1, self.s)).start()
+
+        @pl.when((z >= h) & (z == self.n_dp - 1))
+        def _():
+            remote(own, self.dn.at[h - 1, i], self.dn_s.at[h - 1, i], self.dn_r.at[h - 1, i], (z - 1, self.s)).start()
+
+    def rise(self, h, i):
+        z = self.z
+        own = self.part(z + h, self.piece(i))
+        if h < self.n_dp - 1:
+            @pl.when((z + h < self.n_dp) & (z > 0))
+            def _():
+                buf = self.up.at[h, i]
+                remote(buf, buf, self.up_s.at[h, i], self.up_r.at[h, i], (z - 1, self.s)).wait_recv()
+                add_rows(buf, [own, buf], 0, self.rows)
+                remote(buf, self.up.at[h - 1, i], self.up_s.at[h - 1, i], self.up_r.at[h - 1, i], (z + 1, self.s)).start()
+
+        @pl.when((z + h < self.n_dp) & (z == 0))
+        def _():
+            remote(own, self.up.at[h - 1, i], self.up_s.at[h - 1, i], self.up_r.at[h - 1, i], (z + 1, self.s)).start()
+
+    def target(self, t):
+        d = self.s * 4 + t
+        return d, (d // 8, lax.rem(d, 8))
+
+    def begin(self):
+        for t in range(4):
+            d, dev = self.target(t)
+            src = self.go.at[pl.ds(t * self.rows, self.rows)]
+
+            @pl.when(d != self.me)
+            def _():
+                remote(src, self.ro.at[self.z], self.o_s.at[t], self.o_r.at[self.z], dev).start()
+
+            @pl.when(d == self.me)
+            def _():
+                pltpu.make_async_copy(src, self.ro.at[self.z], self.l_s).start()
+
+    def last(self, i):
+        z, s = self.z, self.s
+        dst = self.rq.at[0] if i == 0 else self.st.at[i]
+        own = self.part(z, self.piece(i))
+        dn, up = self.dn.at[0, i], self.up.at[0, i]
+
+        @pl.when(z < self.n_dp - 1)
+        def _():
+            remote(dn, dn, self.dn_s.at[0, i], self.dn_r.at[0, i], (z + 1, s)).wait_recv()
+
+        @pl.when(z > 0)
+        def _():
+            remote(up, up, self.up_s.at[0, i], self.up_r.at[0, i], (z - 1, s)).wait_recv()
+
+        @pl.when((z > 0) & (z < self.n_dp - 1))
+        def _():
+            add_rows(dst, [own, dn, up], 0, self.rows)
+
+        @pl.when(z == 0)
+        def _():
+            add_rows(dst, [own, dn], 0, self.rows)
+
+        @pl.when(z == self.n_dp - 1)
+        def _():
+            add_rows(dst, [own, up], 0, self.rows)
+        if i:
+            remote(dst, self.rq.at[i], self.q_s.at[i], self.q_r.at[i], (z, self.piece(i))).start()
+
+    def steps(self):
+        order = list(range(1, 8)) + [0]
+        todo = []
+        for h in range(self.n_dp - 1, 0, -1):
+            for i in order:
+                todo.append(lambda h=h, i=i: (self.down(h, i), self.rise(h, i)))
+        todo += [lambda i=i: self.last(i) for i in order]
+        return todo
+
+    def finish(self):
+        z, s, me, w = self.z, self.s, self.me, self.w
+        for t in range(self.n_dp):
+            from_s = me // 4
+
+            @pl.when((z != t) | (s != from_s))
+            def _():
+                remote(self.ro.at[t], self.ro.at[t], self.o_s.at[0], self.o_r.at[t], (t, from_s)).wait_recv()
+
+            @pl.when((z == t) & (s == from_s))
+            def _():
+                pltpu.make_async_copy(self.ro.at[t], self.ro.at[t], self.l_s).wait()
+        add_rows(self.out_o, [self.ro.at[t] for t in range(self.n_dp)], 0, self.rows)
+        for i in range(8):
+            src = lax.rem(s + 8 - i, 8)
+            if i:
+                remote(self.rq.at[i], self.rq.at[i], self.q_s.at[i], self.q_r.at[i], (z, src)).wait_recv()
+            for j in range(3):
+                at = pl.ds(pl.multiple_of(j * 8 * w + src * w, w), w)
+                self.out_q[:, at] = self.rq[i, :, j * w:(j + 1) * w].astype(f32)
+        for i in range(1, 8):
+            remote(self.rq.at[i], self.rq.at[i], self.q_s.at[i], self.q_r.at[i], (z, s + 1 - 2 * lax.rem(s, 2))).wait_send()
+        for t in range(4):
+            d, dev = self.target(t)
+
+            @pl.when(d != me)
+            def _():
+                remote(self.ro.at[0], self.ro.at[0], self.o_s.at[t], self.o_r.at[0], dev).wait_send()
+        for h in range(1, self.n_dp):
+            for i in range(8):
+                @pl.when(z >= h)
+                def _():
+                    buf = self.dn.at[h - 1, i]
+                    remote(buf, buf, self.dn_s.at[h - 1, i], self.dn_r.at[h - 1, i], (z - 1, s)).wait_send()
+
+                @pl.when(z + h < self.n_dp)
+                def _():
+                    buf = self.up.at[h - 1, i]
+                    remote(buf, buf, self.up_s.at[h - 1, i], self.up_r.at[h - 1, i], (z + 1, s)).wait_send()
+
+
+def everyone():
+    z, s = lax.axis_index("dp"), lax.axis_index("seq")
+    n = lax.axis_size("dp") * 8
+    found = []
     for i in range(1, n):
-        t = lax.rem(me + i, n)
-        everyone.append((t // n_seq, lax.rem(t, n_seq)))
-    greet(everyone)
+        t = lax.rem(z * 8 + s + i, n)
+        found.append((t // 8, lax.rem(t, 8)))
+    return found
+
+
+def final_kernel(n_dp, hid, wo, dp_, wq, gq, go, bf, dua, out_q, out_o, *rest):
+    s4, s1, own = rest[:17], rest[17:34], rest[34:]
+    big = Scatter(n_dp, False, hid, wo, bf, s4[:7], s4[7:])
+    near = Scatter(1, True, dp_, wq, dua, s1[:7], s1[7:])
+    grads = Owners(n_dp, gq, go, out_q, out_o, own[:5], own[5:])
+    greet(everyone())
+    lists = [grads.steps(), big.steps(), near.steps()]
+    lists[1].pop(0)()
+    for act in lists[0][:8]:
+        act()
+    grads.begin()
+    lists[0] = lists[0][8:]
+    lists[2].pop(0)()
+    while any(lists):
+        if lists[1]:
+            lists[1].pop(0)()
+        if lists[2] and len(lists[1]) < 20:
+            lists[2].pop(0)()
+        if lists[0]:
+            lists[0].pop(0)()
+    big.finish()
+    near.finish()
+    grads.finish()
+
+
+def final_exchange(hid, wo, d_proj, wq, gq, gwo, n_dp, cid):
+    n = n_dp * 8
+    width = wo.shape[1]
+    rows, w3 = gq.shape[0] // n, gq.shape[1]
+    toks = hid.shape[0] // n
+    blk = lambda *k: pltpu.VMEM(k + (rows, w3), bf16)
+    h = n_dp - 1
+    return pl.pallas_call(
+        functools.partial(final_kernel, n_dp),
+        out_shape=(jax.ShapeDtypeStruct((toks, width), f32), jax.ShapeDtypeStruct((toks, width), f32),
+                   jax.ShapeDtypeStruct((rows, w3 * 8), f32), jax.ShapeDtypeStruct((rows, width), f32)),
+        in_specs=[VM] * 6, out_specs=(VM,) * 4,
+        scratch_shapes=scatter_bufs(n_dp, toks, width) + scatter_sems(n_dp) + scatter_bufs(1, toks, width) + scatter_sems(1)
+        + [blk(h, 8), blk(h, 8), blk(8), blk(8), pltpu.VMEM((n_dp, rows, width), bf16)]
+        + [DMA((h, 8))] * 4 + [DMA((8,)), DMA((8,)), DMA((4,)), DMA((n_dp,)), DMA],
+        compiler_params=params(cid, 63))(hid, wo, d_proj, wq, gq, gwo)
+
+
+def total_kernel(n_dp, x, out, rs, m_s, m_r):
+    devs = everyone()
+    greet(devs)
     sends = []
-
-    def go(*args):
-        d = remote(*args)
+    for i, dev in enumerate(devs):
+        d = remote(x, rs.at[i], m_s.at[i], m_r.at[i], dev)
         d.start()
         sends.append(d)
-    for i in range(1, n):
-        go(small, rs.at[i], m_s.at[i], m_r.at[i], everyone[i - 1])
-    seqs = [lax.rem(s + i, n_seq) for i in range(n_seq)]
-    order = list(range(1, n_seq)) + [0]
-
-    def part(plane, t):
-        return pl.ds(pl.multiple_of((plane * n_seq + t) * rows, rows), rows)
-    for i in order:
-        for h in range(1, n_dp):
-            zt = lax.rem(z + h, n_dp)
-            go(gq.at[part(zt, seqs[i])], rz.at[h, i], z_s.at[h, i], z_r.at[h, i], (zt, s))
-    for t in range(4):
-        d = s * 4 + t
-        src = go_.at[pl.ds(t * rows, rows)]
-
-        @pl.when(d != me)
-        def _():
-            remote(src, ro.at[z], o_s.at[t], o_r.at[z], (d // n_seq, lax.rem(d, n_seq))).start()
-
-        @pl.when(d == me)
-        def _():
-            pltpu.make_async_copy(src, ro.at[z], l_s).start()
-    for i in order:
-        for h in range(1, n_dp):
-            remote(rz.at[h, i], rz.at[h, i], z_s.at[h, i], z_r.at[h, i], (z, s + 1 - 2 * k)).wait_recv()
-        own = gq.at[part(z, seqs[i])]
-        if i == 0:
-            add_rows(rq.at[0], [own] + [rz.at[h, i] for h in range(1, n_dp)], 0, rows)
-        else:
-            add_rows(st.at[i], [own] + [rz.at[h, i] for h in range(1, n_dp)], 0, rows)
-            go(st.at[i], rq.at[i], q_s.at[i], q_r.at[i], (z, seqs[i]))
-    total = small[...]
-    for i in range(1, n):
-        remote(rs.at[i], rs.at[i], m_s.at[i], m_r.at[i], everyone[0]).wait_recv()
+    total = x[...]
+    for i in range(len(devs)):
+        remote(rs.at[i], rs.at[i], m_s.at[i], m_r.at[i], devs[0]).wait_recv()
         total = total + rs[i]
-    out_s[...] = total
-    for t in range(n_dp):
-        from_s = me // 4
-
-        @pl.when((z != t) | (s != from_s))
-        def _():
-            remote(ro.at[t], ro.at[t], o_s.at[0], o_r.at[t], (t, from_s)).wait_recv()
-
-        @pl.when((z == t) & (s == from_s))
-        def _():
-            pltpu.make_async_copy(ro.at[t], ro.at[t], l_s).wait()
-    add_rows(out_o, [ro.at[t] for t in range(n_dp)], 0, rows)
-    for i in range(n_seq):
-        src = lax.rem(s + n_seq - i, n_seq)
-        if i:
-            remote(rq.at[i], rq.at[i], q_s.at[i], q_r.at[i], (z, src)).wait_recv()
-        for j in range(3):
-            at = pl.ds(pl.multiple_of(j * n_seq * w + src * w, w), w)
-            out_q[:, at] = rq[i, :, j * w:(j + 1) * w].astype(f32)
+    out[...] = total
     for d in sends:
         d.wait_send()
-    for t in range(4):
-        d = s * 4 + t
-        src = go_.at[pl.ds(t * rows, rows)]
-
-        @pl.when(d != me)
-        def _():
-            remote(src, ro.at[z], o_s.at[t], o_r.at[z], (d // n_seq, lax.rem(d, n_seq))).wait_send()
-
-
-def tail_exchange(gq, gwo, small, n_dp, cid):
-    n = n_dp * 8
-    rows, w3 = gq.shape[0] // n, gq.shape[1]
+
+
+def total_all(x, n_dp, cid):
+    n = n_dp * 8 - 1
     return pl.pallas_call(
-        functools.partial(tail_kernel, n_dp),
-        out_shape=(jax.ShapeDtypeStruct((rows, w3 * 8), f32),
-                   jax.ShapeDtypeStruct((rows, gwo.shape[1]), f32),
-                   jax.ShapeDtypeStruct(small.shape, f32)),
-        in_specs=[VM] * 3, out_specs=(VM,) * 3,
-        scratch_shapes=[pltpu.VMEM((n_dp, 8, rows, w3), bf16), pltpu.VMEM((8, rows, w3), bf16),
-                        pltpu.VMEM((8, rows, w3), bf16), pltpu.VMEM((n_dp, rows, gwo.shape[1]), bf16),
-                        pltpu.VMEM((n,) + small.shape, f32),
-                        DMA((n_dp, 8)), DMA((n_dp, 8)), DMA((8,)), DMA((8,)), DMA((4,)), DMA((n_dp,)),
-                        DMA((n,)), DMA((n,)), DMA],
-        compiler_params=pltpu.CompilerParams(collective_id=cid, has_side_effects=True,
-                                             vmem_limit_bytes=48 * 1024 * 1024))(gq, gwo, small)
+        functools.partial(total_kernel, n_dp), out_shape=jax.ShapeDtypeStruct(x.shape, f32),
+        in_specs=[VM], out_specs=VM,
+        scratch_shapes=[pltpu.VMEM((n,) + x.shape, f32), DMA((n,)), DMA((n,))],
+        compiler_params=pltpu.CompilerParams(collective_id=cid, has_side_effects=True))(x)
 
 
 def dot(a, b, dims):
@@ -556,6 +734,328 @@
 def turn_back(values):
     half = HEAD_DIM // 2
     return jnp.concatenate([values[..., half:], -values[..., :half]], axis=-1)
+
+
+def ff_kernel(nz, x, dbf, wf, wo, xf, out, hid, dug, xb, gb, pp, po, ra, rd, fx, fy, fz, *sems):
+    ag, rs = sems[:9], sems[9:]
+    zs, zr, cs, cr, ds, dr, ps, pr, ls = ag
+    p_s, p_r, d_s, d_r, x_s, x_r, y_s, y_r, z_s, z_r, l_s = rs
+    z, s, c, k, xc, yc, dc = place()
+    rows = x.shape[0]
+    half = rows // 2
+    ffl = wo.shape[0]
+    partner = (z, s + 1 - 2 * k)
+    dev = [(z, 2 * xc + k), (z, 2 * yc + k)]
+    zt = [lax.rem(z + i, nz) for i in range(1, nz)]
+    greet([partner] + dev + [(t, s) for t in zt])
+    lo, hi = pl.ds(0, half), pl.ds(half, half)
+    parts = (lo, hi)
+    cx, cy = lax.rem(c, 2), c // 2
+
+    def plane_of(g):
+        return lax.rem(z + nz - g, nz)
+
+    def chip_of(j):
+        rx = jnp.where(j < 2, 1, 0)
+        ry = jnp.where(lax.rem(j, 2) == 0, 1, 0) * jnp.where(j < 3, 1, 0)
+        return cx + rx - 2 * cx * rx + 2 * (cy + ry - 2 * cy * ry)
+
+    def pair(g, slot, blk):
+        remote(blk, blk, ps.at[g, slot], pr.at[g, slot], partner).start()
+
+    own = xf.at[z, c, k]
+    local = pltpu.make_async_copy(x, own, ls)
+    local.start()
+    for j in range(2):
+        remote(x, own, cs.at[0, j], cr.at[0, j], dev[j]).start()
+    for i in range(1, nz):
+        remote(x, own, zs.at[i - 1], zr.at[i - 1], (zt[i - 1], s)).start()
+    remote(x, own, ps.at[0, 0], pr.at[0, 0], partner).start()
+    local.wait()
+
+    def line(g):
+        blk = xf.at[plane_of(g), c, k]
+        remote(blk, blk, zs.at[g - 1], zr.at[g - 1], dev[0]).wait_recv()
+        for j in range(2):
+            remote(blk, blk, cs.at[g, j], cr.at[g, j], dev[j]).start()
+        pair(g, 0, blk)
+
+    def near(g, j):
+        blk = xf.at[plane_of(g), (xc, yc)[j], k]
+        remote(blk, blk, cs.at[g, j], cr.at[g, j], dev[j]).wait_recv()
+        part = xf.at[plane_of(g), (xc, yc)[j], k, parts[j]]
+        remote(part, part, ds.at[g, j], dr.at[g, j], dev[1 - j]).start()
+        pair(g, 1 + j, blk)
+
+    def far(g, h):
+        part = xf.at[plane_of(g), dc, k, parts[h]]
+        remote(part, part, ds.at[g, h], dr.at[g, h], dev[1 - h]).wait_recv()
+        pair(g, 3 + h, part)
+
+    def compute(g, j):
+        plane, chip = plane_of(g), chip_of(j)
+        blk = xf.at[plane, chip, 1 - k]
+
+        @pl.when(j == 0)
+        def _():
+            for h in range(2):
+                part = xf.at[plane, chip, 1 - k, parts[h]]
+                remote(part, part, ps.at[g, 3 + h], pr.at[g, 3 + h], partner).wait_recv()
+
+        @pl.when(j > 0)
+        def _():
+            slot = jnp.where(j == 3, 0, j)
+            remote(blk, blk, ps.at[g, slot], pr.at[g, slot], partner).wait_recv()
+        load = pltpu.make_async_copy(xf.at[plane, chip], xb, l_s.at[0])
+        load.start()
+        grads = pltpu.make_async_copy(dbf.at[plane, chip], gb, l_s.at[1])
+        grads.start()
+        load.wait()
+        rows2 = 2 * rows
+        upgate = jnp.dot(xb[...].reshape(rows2, x.shape[1]), wf[...], preferred_element_type=f32)
+        up, gate = upgate[:, :ffl], upgate[:, ffl:]
+        sig = 1.0 / (1.0 + jnp.exp(-gate))
+        act = gate * sig
+        grads.wait()
+        d_h = lax.dot_general(gb[...].reshape(rows2, x.shape[1]), wo[...], (((1,), (1,)), ((), ())),
+                              preferred_element_type=f32)
+        at = pl.ds(pl.multiple_of((plane * 4 + chip) * rows2, rows2), rows2)
+        hid[at, :] = (act * up).astype(bf16)
+        d_up = (d_h * act).astype(bf16)
+        d_gate = (d_h * up * (sig * (1.0 + gate * (1.0 - sig)))).astype(bf16)
+        both = jnp.concatenate([d_up, d_gate], axis=1)
+        dug[at, :] = both
+        back = lax.dot_general(both, wf[...], (((1,), (1,)), ((), ())), preferred_element_type=f32).astype(bf16)
+        pp[g, j, 0] = back[:rows]
+        pp[g, j, 1] = back[rows:]
+        remote(pp.at[g, j, 1 - k], ra.at[g, j], p_s.at[g, j], p_r.at[g, j], partner).start()
+
+    def first(g, j):
+        remote(ra.at[g, j], ra.at[g, j], p_s.at[g, j], p_r.at[g, j], partner).wait_recv()
+        mine = po.at[g, j]
+        add_rows(mine, [pp.at[g, j, k], ra.at[g, j]], 0, rows)
+        if j == 0:
+            remote(mine.at[lo], rd.at[g, lo], d_s.at[g, 0], d_r.at[g, 0], dev[0]).start()
+            remote(mine.at[hi], rd.at[g, hi], d_s.at[g, 1], d_r.at[g, 1], dev[1]).start()
+        if j == 1:
+            remote(mine.at[lo], fx.at[g, lo], x_s.at[g, 0], x_r.at[g, 0], dev[0]).start()
+        if j == 2:
+            remote(mine.at[hi], fy.at[g, hi], y_s.at[g, 1], y_r.at[g, 1], dev[1]).start()
+
+    def second(g):
+        remote(rd.at[g, lo], rd.at[g, lo], d_s.at[g, 0], d_r.at[g, 0], dev[0]).wait_recv()
+        add_rows(po.at[g, 2], [po.at[g, 2], rd.at[g]], 0, half)
+        remote(po.at[g, 2, lo], fy.at[g, lo], y_s.at[g, 0], y_r.at[g, 0], dev[1]).start()
+        remote(rd.at[g, hi], rd.at[g, hi], d_s.at[g, 1], d_r.at[g, 1], dev[1]).wait_recv()
+        add_rows(po.at[g, 1], [po.at[g, 1], rd.at[g]], half, half)
+        remote(po.at[g, 1, hi], fx.at[g, hi], x_s.at[g, 1], x_r.at[g, 1], dev[0]).start()
+
+    def third(g):
+        for h, part in enumerate(parts):
+            remote(fx.at[g, part], fx.at[g, part], x_s.at[g, h], x_r.at[g, h], dev[0]).wait_recv()
+            remote(fy.at[g, part], fy.at[g, part], y_s.at[g, h], y_r.at[g, h], dev[1]).wait_recv()
+        add_rows(po.at[g, 3], [po.at[g, 3], fx.at[g], fy.at[g]], 0, rows)
+
+        @pl.when(g > 0)
+        def _():
+            remote(po.at[g, 3], fz.at[g - 1], z_s.at[g - 1], z_r.at[g - 1], (plane_of(g), s)).start()
+
+    def turn_(t, _):
+        @pl.when((t >= 1) & (t < nz))
+        def _():
+            line(t)
+
+        @pl.when((t >= 1) & (t <= nz))
+        def _():
+            near(t - 1, 0)
+            near(t - 1, 1)
+
+        @pl.when((t >= 2) & (t <= nz + 1))
+        def _():
+            far(t - 2, 0)
+            far(t - 2, 1)
+
+        def some(j, _):
+            g = jnp.where(j == 0, t - 2, t - 1)
+
+            @pl.when((g >= 0) & (g < nz))
+            def _():
+                compute(g, j)
+            return 0
+        lax.fori_loop(0, 4, some, 0)
+
+        @pl.when((t >= 1) & (t <= nz))
+        def _():
+            first(t - 1, 1)
+            first(t - 1, 2)
+            first(t - 1, 3)
+
+        @pl.when((t >= 2) & (t <= nz + 1))
+        def _():
+            first(t - 2, 0)
+
+        @pl.when((t >= 3) & (t <= nz + 2))
+        def _():
+            second(t - 3)
+
+        @pl.when((t >= 4) & (t <= nz + 3))
+        def _():
+            third(t - 4)
+        return 0
+    lax.fori_loop(1, nz + 4, turn_, 0)
+    for i in range(nz - 1):
+        remote(fz.at[i], fz.at[i], z_s.at[i], z_r.at[i], (zt[i], s)).wait_recv()
+    add_rows(out, [po.at[0, 3]] + [fz.at[i] for i in range(nz - 1)], 0, rows)
+    for i in range(nz - 1):
+        remote(x, x, zs.at[i], zr.at[i], partner).wait_send()
+        remote(fz.at[i], fz.at[i], z_s.at[i], z_r.at[i], partner).wait_send()
+
+    def drain(g, _):
+        for j in range(2):
+            remote(x, x, cs.at[g, j], cr.at[g, j], partner).wait_send()
+            remote(x.at[lo], x.at[lo], ds.at[g, j], dr.at[g, j], partner).wait_send()
+            for a, b in ((d_s, d_r), (x_s, x_r), (y_s, y_r)):
+                remote(rd.at[g, lo], rd.at[g, lo], a.at[g, j], b.at[g, j], partner).wait_send()
+            remote(x.at[lo], x.at[lo], ps.at[g, 3 + j], pr.at[g, 3 + j], partner).wait_send()
+        for j in range(3):
+            remote(x, x, ps.at[g, j], pr.at[g, j], partner).wait_send()
+        for j in range(4):
+            remote(ra.at[g, j], ra.at[g, j], p_s.at[g, j], p_r.at[g, j], partner).wait_send()
+        return 0
+    lax.fori_loop(0, nz, drain, 0)
+
+
+def feed_forward(x, dbf, wf, wo, nz, cid):
+    rows, width = x.shape
+    ffl = wo.shape[0]
+    toks = rows * 8 * nz
+    blk = lambda *n: pltpu.VMEM(n + (rows, width), bf16)
+    sem = lambda *n: DMA(n)
+    xf, d_unit, hidden, d_ug = pl.pallas_call(
+        functools.partial(ff_kernel, nz),
+        out_shape=(jax.ShapeDtypeStruct((nz, 4, 2, rows, width), bf16), jax.ShapeDtypeStruct((rows, width), f32),
+                   jax.ShapeDtypeStruct((toks, ffl), bf16), jax.ShapeDtypeStruct((toks, 2 * ffl), bf16)),
+        in_specs=[ANY, ANY, VM, VM], out_specs=(ANY, VM, VM, VM),
+        scratch_shapes=[blk(2), blk(2), blk(nz, 4, 2), blk(nz, 4), blk(nz, 4), blk(nz), blk(nz), blk(nz), blk(nz - 1),
+                        sem(nz - 1), sem(nz - 1), sem(nz, 2), sem(nz, 2), sem(nz, 2), sem(nz, 2), sem(nz, 5), sem(nz, 5), DMA,
+                        sem(nz, 4), sem(nz, 4), sem(nz, 2), sem(nz, 2), sem(nz, 2), sem(nz, 2), sem(nz, 2), sem(nz, 2),
+                        sem(nz - 1), sem(nz - 1), sem(2)],
+        compiler_params=pltpu.CompilerParams(collective_id=cid, has_side_effects=True,
+                                             vmem_limit_bytes=62 * 1024 * 1024),
+    )(x, dbf.reshape(nz, 4, 2, rows, width), wf, wo)
+    return xf.reshape(toks, width), d_unit, hidden, d_ug
+
+
+SM = pl.BlockSpec(memory_space=pltpu.SMEM)
+
+
+def combine(parts, weights):
+    total = parts[0] * weights[0]
+    for part, weight in zip(parts[1:], weights[1:]):
+        total = total + part * weight
+    return total
+
+
+def row(ref, i):
+    return [ref[i, j] for j in range(4)]
+
+
+def planes(ref):
+    return [ref[i].astype(f32) for i in range(4)]
+
+
+def scalar_table(mix_in, mix_res, depth):
+    through_in = jnp.sum(mix_res[0] * mix_in[1][None, :], axis=1)
+    through_depth = jnp.sum(mix_res[1] * depth[0][:, None], axis=0)
+    cross = jnp.sum(mix_res[0][:, :, None] * mix_res[1][None], axis=1)
+    dot_ = jnp.sum(depth[0] * mix_in[1])
+    return jnp.concatenate([mix_in[:1], through_in[None], through_depth[None], depth[1:],
+                            jnp.broadcast_to(dot_, (1, 4)), cross], axis=0)
+
+
+def pre_kernel(tab, st, ct, xn, db, so, co):
+    s_in = [st[0, :, i, :] for i in range(4)]
+    cot = [ct[0, :, i, :] for i in range(4)]
+    for i in range(4):
+        so[i] = s_in[i]
+        co[i] = cot[i]
+    unit, _ = norm_stats(combine([v.astype(f32) for v in s_in], row(tab, 0)))
+    xn[...] = unit.astype(bf16)
+    db[...] = combine([v.astype(f32) for v in cot], row(tab, 3)).astype(bf16)
+
+
+def mixed_ff(tab, s_in, branch):
+    return norm_stats(combine(s_in, row(tab, 1)) + tab[4, 0] * branch)
+
+
+def mid_kernel(tab, st, ba, xn):
+    unit, _ = mixed_ff(tab, planes(st), ba[...])
+    xn[...] = unit.astype(bf16)
+
+
+def back_kernel(tab, st, ct, ba, du, dba):
+    unit, inv = mixed_ff(tab, planes(st), ba[...])
+    d_mix = norm_back(du[...], unit, inv)
+    dba[...] = (combine(planes(ct), row(tab, 2)) + tab[4, 0] * d_mix).astype(bf16)
+
+
+def end_kernel(tab, mi, dep, st, ct, ba, bf, duf, dua, out, gs, small, acc):
+    s_in, cot = planes(st), planes(ct)
+    b_att, b_ff = ba[...], bf[...]
+    unit, inv = mixed_ff(tab, s_in, b_att)
+    d_ff = norm_back(duf[...], unit, inv)
+    unit, inv = norm_stats(combine(s_in, row(tab, 0)))
+    d_att = norm_back(dua[...], unit, inv)
+    for i in range(4):
+        gs[0, :, i, :] = combine(cot, row(tab, 5 + i)) + tab[1, i] * d_ff + tab[0, i] * d_att
+        out[0, :, i, :] = (combine(s_in, [tab[5 + k, i] for k in range(4)]) + tab[2, i] * b_att
+                           + tab[3, i] * b_ff).astype(bf16)
+    pairs = [(s, c) for s in s_in for c in cot] + [(s, d_ff) for s in s_in] + [(s, d_att) for s in s_in]
+    pairs += [(b_att, c) for c in cot] + [(b_ff, c) for c in cot] + [(b_att, d_ff)]
+
+    @pl.when(pl.program_id(0) == 0)
+    def _():
+        acc[...] = jnp.zeros_like(acc)
+    for q, (a, b) in enumerate(pairs):
+        product = a * b
+        total = product[:, :128]
+        for j in range(1, product.shape[1] // 128):
+            total = total + product[:, j * 128:(j + 1) * 128]
+        acc[q] += total
+
+    @pl.when(pl.program_id(0) == pl.num_programs(0) - 1)
+    def _():
+        small[...] = jnp.sum(acc[...], axis=1)
+
+
+def small_grads(sums, mix_in, mix_res, depth):
+    s_c, s_f, s_a = sums[:16].reshape(4, 4), sums[16:20], sums[20:24]
+    b_c, bf_c, b_f = sums[24:28], sums[28:32], sums[32]
+    mm = lambda a, b: jnp.sum(a[:, :, None] * b[None], axis=1)
+    in_ff = jnp.sum(mix_res[0] * s_f[:, None], axis=0) + depth[0] * b_f
+    res_ff = mm(mix_res[0].T, s_c) + depth[0][:, None] * b_c[None]
+    res_att = mm(s_c, mix_res[1].T) + s_f[:, None] * mix_in[1][None]
+    depth_att = jnp.sum(mix_res[1] * b_c[None], axis=1) + mix_in[1] * b_f
+    return jnp.stack([s_a, in_ff]), jnp.stack([res_att, res_ff]), jnp.stack([depth_att, bf_c])
+
+
+def token_call(kernel, scalars, arrays, outs, scratch=(), step=16):
+    toks, width = [a for a in arrays if a.ndim == 2 or a.ndim == 4][0].shape[-2:] if arrays[0].ndim != 4 else (
+        arrays[0].shape[1], arrays[0].shape[3])
+    specs_of = {
+        "tok": ((1, toks, 4, width), pl.BlockSpec((1, step, 4, width), lambda i: (0, i, 0, 0))),
+        "mat": ((toks, width), pl.BlockSpec((step, width), lambda i: (i, 0))),
+        "pla": ((4, toks, width), pl.BlockSpec((4, step, width), lambda i: (0, i, 0))),
+        "sum": ((40, 128), pl.BlockSpec((40, 128), lambda i: (0, 0)))}
+    kind_of = {4: "tok", 3: "pla", 2: "mat"}
+    return pl.pallas_call(
+        kernel, grid=(toks // step,),
+        out_shape=tuple(jax.ShapeDtypeStruct(specs_of[kind][0], dtype) for kind, dtype in outs),
+        out_specs=tuple(specs_of[kind][1] for kind, _ in outs),
+        in_specs=[SM] * len(scalars) + [specs_of[kind_of[a.ndim]][1] for a in arrays],
+        scratch_shapes=list(scratch),
+        compiler_params=pltpu.CompilerParams(vmem_limit_bytes=48 * 1024 * 1024),
+    )(*scalars, *arrays)
 
 
 def plain_body(n_dp, n_seq, streams, segments, positions, att_proj, attn_out, ff_proj, ff_out,
@@ -683,9 +1183,8 @@
 
 
 def fast_body(n_dp, n_seq, streams, segments, positions, att_proj, attn_out, ff_proj, ff_out,
-         mix_in, mix_res, depth, cotangent):
-    seq_count, toks, n_str, width = streams.shape
-    assert seq_count == 1
+              mix_in, mix_res, depth, cotangent):
+    _, toks, _, width = streams.shape
     n_all = n_dp * n_seq
     both = ("dp", "seq")
     rows = att_proj.shape[0]
@@ -694,24 +1193,16 @@
     hw = hp * HEAD_DIM
     length = toks * n_seq
     scale = HEAD_DIM ** -0.5
-    seq_id = lax.axis_index("seq")
-
-    def mix(parts, weights):
-        total = parts[0] * weights[0]
-        for i in range(1, n_str):
-            total = total + parts[i] * weights[i]
-        return total
-
+    tab = scalar_table(mix_in, mix_res, depth)
+
+    xn, d_branch_ff, s_low, c_low = token_call(
+        pre_kernel, (tab,), (streams, cotangent), [("mat", bf16), ("mat", bf16), ("pla", bf16), ("pla", bf16)])
+
+    ids = jnp.concatenate([segments, positions, jnp.zeros((6, toks), jnp.int32)], axis=0)
     wf = ff_proj.reshape(rows, 2, n_all, ffl).transpose(2, 0, 1, 3).reshape(n_all, rows, 2 * ffl)
+    xa, ids_all, wq, wo = head_exchange(xn, ids, att_proj, attn_out, n_dp, 0)
+    xa, ids_all, wq, wo, wf = lax.optimization_barrier((xa, ids_all, wq, wo, wf))
     wf = lax.all_to_all(wf, both, 0, 0, tiled=True).reshape(n_all * rows, 2 * ffl)
-    s_in = [streams[0, :, i].astype(f32) for i in range(n_str)]
-    cot = [cotangent[0, :, i].astype(f32) for i in range(n_str)]
-    d_branch_ff = mix(cot, depth[1]).astype(bf16)
-    dbf = lax.all_gather(d_branch_ff, both, axis=0, tiled=True)
-
-    unit_att, inv_att = norm_stats(mix(s_in, mix_in[0]))
-    ids = jnp.concatenate([segments, positions, jnp.zeros((6, toks), jnp.int32)], axis=0)
-    xa, ids_all, wq, wo = head_exchange(unit_att.astype(bf16), ids, att_proj, attn_out, n_dp, 0)
     xa = xa.reshape(length, width)
     seg_all = ids_all[:, 0].reshape(length)
     pos_all = ids_all[:, 1].reshape(length)
@@ -732,31 +1223,13 @@
     p_low = p.astype(bf16)
     att = jnp.einsum("hqk,khd->qhd", p_low, v, preferred_element_type=f32)
     att = att.reshape(length, hw).astype(bf16)
-    branch_att = dot_scatter(att, wo, 1, False, 1)
-
-    mid = [mix(s_in, mix_res[0, :, j]) + depth[0, j] * branch_att for j in range(n_str)]
-    unit_ff, inv_ff = norm_stats(mix(mid, mix_in[1]))
-    xf = all_gather(unit_ff.astype(bf16), n_dp, 2)
-    upgate = dot(xf, wf, ((1,), (0,)))
-    up, gate = upgate[:, :ffl], upgate[:, ffl:]
-    sig = 1.0 / (1.0 + jnp.exp(-gate))
-    hidden = (gate * sig * up).astype(bf16)
-    branch_ff = lax.psum_scatter(dot(hidden, ff_out, ((1,), (0,))).astype(bf16), both,
-                                 scatter_dimension=0, tiled=True).astype(f32)
-
-    d_hidden = dot(dbf, ff_out, ((1,), (1,)))
-    g_ff_out = dot(hidden, dbf, ((0,), (0,)))
-    d_up = d_hidden * gate * sig
-    d_gate = d_hidden * up * (sig * (1.0 + gate * (1.0 - sig)))
-    d_ug = jnp.concatenate([d_up, d_gate], axis=1).astype(bf16)
-    d_unit = dot_scatter(d_ug, wf, n_dp, True, 3)
+    branch_att, dbf = scatter_gather(att, wo, d_branch_ff, n_dp, False, 1)
+
+    xn_ff, = token_call(mid_kernel, (tab,), (s_low, branch_att), [("mat", bf16)])
+    xf, d_unit, hidden, d_ug = feed_forward(xn_ff, dbf, wf, ff_out, n_dp, 2)
     g_wf = dot(xf, d_ug, ((0,), (0,))).astype(bf16).reshape(n_all, rows, 2 * ffl)
     g_wf = lax.all_to_all(g_wf, both, 0, 0, tiled=True)
-    g_ff_proj = g_wf.reshape(n_all, rows, 2, ffl).transpose(1, 2, 0, 3).reshape(ff_proj.shape).astype(f32)
-    d_mix_ff = norm_back(d_unit, unit_ff, inv_ff)
-
-    d_mid = [mix(cot, mix_res[1, i]) + mix_in[1, i] * d_mix_ff for i in range(n_str)]
-    d_branch_att = mix(d_mid, depth[0]).astype(bf16)
+    d_branch_att, = token_call(back_kernel, (tab,), (s_low, c_low, branch_att, d_unit), [("mat", bf16)])
     dba = all_gather(d_branch_att, 1, 4)
     d_att = dot(dba, wo, ((1,), (1,))).astype(bf16).reshape(length, hp, HEAD_DIM)
     g_wo = dot(att, dba, ((0,), (0,))).astype(bf16)
@@ -769,27 +1242,16 @@
     d_q = d_q * cosine + turn_back(d_q * sine)
     d_k = d_k * cosine + turn_back(d_k * sine)
     d_proj = jnp.stack([d_q, d_k, d_v], axis=1).reshape(length, 3 * hw).astype(bf16)
-    d_unit_att = dot_scatter(d_proj, wq, 1, True, 5)
     g_wq = dot(xa, d_proj, ((0,), (0,))).astype(bf16)
-    d_mix_att = norm_back(d_unit_att, unit_att, inv_att)
-
-    g_in = [mix(d_mid, mix_res[0, i]) + mix_in[0, i] * d_mix_att for i in range(n_str)]
-    out = [mix(mid, mix_res[1, :, j]) + depth[1, j] * branch_ff for j in range(n_str)]
-
-    def inner(a, b):
-        return jnp.sum(a * b)
-
-    sums = [inner(s, d_mix_att) for s in s_in] + [inner(m, d_mix_ff) for m in mid]
-    sums += [inner(s, d) for s in s_in for d in d_mid] + [inner(m, c) for m in mid for c in cot]
-    sums += [inner(branch_att, d) for d in d_mid] + [inner(branch_ff, c) for c in cot]
-    small = jnp.pad(jnp.stack(sums), (0, 1024 - len(sums))).reshape(8, 128)
-    g_att_proj, g_attn_out, small = tail_exchange(g_wq, g_wo, small, n_dp, 6)
-    small = small.reshape(-1)
-    g_mix_in = small[:8].reshape(2, 4)
-    g_mix_res = small[8:40].reshape(2, 4, 4)
-    g_depth = small[40:48].reshape(2, 4)
-    return (jnp.stack(out, axis=1).astype(bf16)[None], jnp.stack(g_in, axis=1)[None],
-            g_att_proj, g_attn_out, g_ff_proj, g_ff_out, g_mix_in, g_mix_res, g_depth)
+    branch_ff, d_unit_att, g_att_proj, g_attn_out = final_exchange(hidden, ff_out, d_proj, wq, g_wq, g_wo, n_dp, 3)
+    out, g_in, small = token_call(
+        end_kernel, (tab, mix_in, depth), (s_low, c_low, branch_att, branch_ff, d_unit, d_unit_att),
+        [("tok", bf16), ("tok", f32), ("sum", f32)], [pltpu.VMEM((40, 16, 128), f32)])
+    sums = jnp.sum(total_all(small, n_dp, 5), axis=1)
+    g_mix_in, g_mix_res, g_depth = small_grads(sums, mix_in, mix_res, depth)
+    g_ff_out = dot(hidden, dbf, ((0,), (0,)))
+    g_ff_proj = g_wf.reshape(n_all, rows, 2, ffl).transpose(1, 2, 0, 3).reshape(ff_proj.shape).astype(f32)
+    return out, g_in, g_att_proj, g_attn_out, g_ff_proj, g_ff_out, g_mix_in, g_mix_res, g_depth
 
 
 def solution(mesh):

time: 1040 us -> 800 us (0.77); the launches traced: 1020 us -> 793 us
  other arithmetic: 115 us -> 21.7 us
  waiting for transfers between devices: 54.4 us -> 0.01 us
  local copies, waits for them, and re-layouts: 91.2 us -> 53.5 us
  matrix products: 102 us -> 66.5 us
  Pallas kernels: 614 us -> 633 us
  between operations: 15.1 us -> 1.71 us
  starting transfers between devices: 28.5 us -> 16.5 us
    pallas_call x4 -> x8, Pallas kernels: 343 us -> 530 us  [the longest x1 201 us: feed_forward(): pl.pallas_call(functools.partial(ff_kernel, nz), out_shape=(jax.ShapeDtyp...]
    pallas_call x1, Pallas kernels: 171 us -> 78.5 us  [head_exchange(): pl.pallas_call(functools.partial(head_kernel, n_dp), out_shape=(jax.Shape...]
    pallas_call x2 -> x1, Pallas kernels: 100 us -> 24.2 us  [all_gather(): pl.pallas_call(functools.partial(gather_kernel, nz), out_shape=jax.ShapeD...]
    reduce_scatter x1 -> x0, waiting for transfers between devices: 54.4 us -> none  [fast_body(): lax.psum_scatter(dot(hidden, ff_out, ((1,), (0,))).astype(bf16), both, sc...]
    dot_general x9 -> x6, matrix products: 81.1 us -> 38.8 us  [dot(): return lax.dot_general(a, b, (dims, ((), ())), preferred_element_type=f32)]
    reduce_sum x8 -> x6, other arithmetic: 40.1 us -> 2.58 us  [the longest x1 1.3 us: scalar_table(): dot_ = jnp.sum(depth[0] * mix_in[1])]
    another operation x1, local copies, waits for them, and re-layouts: 31.1 us -> 0.07 us  [small_grads(): jnp.stack([depth_att, bf_c])]
    another operation x5 -> x3, other arithmetic: 31 us -> 1.74 us  [the longest x1 0.6 us: small_grads(): jnp.stack([res_att, res_ff])]
  transfers between devices with their start and end apart: 4 -> 2, of which waited for: 1 -> 0; matrix products, arithmetic and copies ran while one was open for 13% -> 9% of each run, Pallas kernels for 43% -> 39%
where the time goes in v3:
time: 800 us; the launch traced here: 793 us
  Pallas kernels  633 us (79%)
  matrix products  66.5 us (8%)
  local copies, waits for them, and re-layouts  53.5 us (7%)
  other arithmetic  21.7 us (3%)
  starting transfers between devices  16.5 us (2%)
    pallas_call x1, Pallas kernels, feed_forward(): pl.pallas_call(functools.partial(ff_kernel, nz), out_shape=(jax.ShapeDtyp...  201 us
    pallas_call x1, Pallas kernels, final_exchange(): pl.pallas_call(functools.partial(final_kernel, n_dp), out_shape=(jax.Shap...  164 us
    pallas_call x1, Pallas kernels, scatter_gather(): pl.pallas_call(functools.partial(scatter_gather_kernel, nz, trans), out_s...  96.3 us
    pallas_call x1, Pallas kernels, head_exchange(): pl.pallas_call(functools.partial(head_kernel, n_dp), out_shape=(jax.Shape...  78.5 us
    pallas_call x4, Pallas kernels, token_call(): pl.pallas_call(kernel, grid=(toks // step,), out_shape=tuple((jax.ShapeDt...  40.2 us
    dot_general x6, matrix products, dot(): return lax.dot_general(a, b, (dims, ((), ())), preferred_element_type=f32)  38.8 us
    pallas_call x1, Pallas kernels, total_all(): pl.pallas_call(functools.partial(total_kernel, n_dp), out_shape=jax.Shape...  28.4 us
    unnamed x90, local copies, waits for them, and re-layouts  28 us
  transfers between devices with their start and end apart: 2, of which 0 were waited for; matrix products, arithmetic and copies ran while one was open for 9% of the time, Pallas kernels for 39%

profile of v3, /device:TPU:14, one launch (start us, length us, event | category | flops | bytes accessed | tf_op | source)
XLA Modules:
  0.0 792.6 jit_solution(18146508952711700541)
XLA Ops:
  0.6 1.3 multiply_reduce_fusion.8
  1.9 0.8 slice_bitcast_fusion.9
  2.8 0.7 slice_bitcast_fusion.4
  3.5 2.1 copy.85
  5.7 2.2 copy.58
  7.8 2.6 reshape.321
  10.7 0.7 add_add_fusion.ids
  12.1 17.6 %shard_map.178 = (bf16[128,2048]{1,0:T(8,128)(2,1)S(1)}, bf16[128,2048]{1,0:T(8,128)(2,1)S(1)}, bf16[4,128,2048]{2,1,0:T(8,128)(2,1)S(1)}, bf16[4,128,2048]{2,1,0:T(8,128)(2,1)S(1)}) custom-call(f32[9,4]{1,0:T(8,128)S(1)} %concatenate.29.tab, bf16[1,128,4,2048]{3,2,1,0:T(4,128)(2,1)} %st.1, bf16[1,128,4,2048]{3,2,1,0:T(4,128)(2,1)} %ct.1), custom_call_target="tpu_custom_call" | custom-call | tf_op jit(solution)/shard_map/pallas_call | solution.py:1051
  29.7 1.3 copy-done.4
  31.0 0.8 copy-done.14
  31.8 0.8 copy-done.15
  32.6 78.5 %shard_map.179 = (bf16[4,2,128,2048]{3,2,1,0:T(8,128)(2,1)}, s32[8,8,128]{2,1,0:T(8,128)}, bf16[2048,768]{1,0:T(8,128)(2,1)}, bf16[256,2048]{1,0:T(8,128)(2,1)}) custom-call(bf16[128,2048]{1,0:T(8,128)(2,1)} %copy-done.14, s32[8,128]{1,0:T(8,128)} %add_add_fusion.ids, bf16[64,6144]{1,0:T(8,128)(2,1)} %wp.1, bf16[64,2048]{1,0:T(8,128)(2,1)} %wo.3), custom_call_target="tpu_custom_call" | custom-call | tf_op jit(solution)/shard_map/pallas_call | solution.py:327
  111.1 9.9 %all-to-all-start = ((bf16[32,64,512]{2,1,0:T(8,128)(2,1)}), bf16[32,64,512]{2,1,0:T(8,128)(2,1)}, u32[]{:S(2)}, u32[]{:S(2)}) async-start(bf16[32,64,512]{2,1,0:T(8,128)(2,1)} %reshape.321), calls=%async_computation | async-start | bytes 4194304 | tf_op jit(solution)/shard_map/all_to_all | solution.py:1205
  121.2 0.8 slice_convert_fusion.1
  122.2 2.8 broadcast_multiply_fusion.3
  125.0 4.6 copy.82
  129.6 6.2 fusion.36
  136.3 1.2 copy-done.21
  137.5 1.4 fusion.19
  138.9 1.8 fusion.4
  140.7 8.0 %fusion.35 = (f32[2,1024]{1,0:T(2,128)S(1)}, f32[2,1024,1024]{1,2,0:T(8,128)}) fusion(pred[1024,1024]{0,1:T(8,128)(4,1)} %fusion.4, bf16[1024,2,128]{0,2,1:T(8,128)(2,1)} %get-tuple-element.68, bf16[1024,2,128]{0,2,1:T(8,128)(2,1)S(1)} %get-tuple-element.67), kind=kOutput, calls=%fused_computation.85 | convolution fusion | flops 545260544 | bytes 10493952 | tf_op jit(solution)/shard_map/sub | solution.py:1221
  148.8 4.4 fusion.13
  153.3 1.0 copy.83.a
  154.3 1.0 copy-done.8
  155.3 1.2 copy-done.10
  156.5 1.0 copy-done.16
  157.6 96.3 %shard_map.180 = (f32[128,2048]{1,0:T(8,128)S(1)}, bf16[4,4,2,128,2048]{4,3,2,1,0:T(8,128)(2,1)}) custom-call(bf16[1024,256]{1,0:T(8,128)(2,1)S(1)} %copy-done.8, bf16[256,2048]{1,0:T(8,128)(2,1)S(1)} %copy-done.10, bf16[128,2048]{1,0:T(8,128)(2,1)S(1)} %copy-done.16), custom_call_target="tpu_custom_call" | custom-call | tf_op jit(solution)/shard_map/pallas_call | solution.py:475
  253.9 3.0 shard_map.181.x
  256.9 0.8 copy-done.7
  257.7 200.7 %shard_map.182 = (bf16[4,4,2,128,2048]{4,3,2,1,0:T(8,128)(2,1)}, f32[128,2048]{1,0:T(8,128)}, bf16[4096,256]{1,0:T(8,128)(2,1)}, bf16[4096,512]{1,0:T(8,128)(2,1)}) custom-call(bf16[128,2048]{1,0:T(8,128)(2,1)} %copy-done.7, bf16[4,4,2,128,2048]{4,3,2,1,0:T(8,128)(2,1)} %get-tuple-element.48.dbf, bf16[2048,512]{1,0:T(8,128)(2,1)} %bitcast.19.wf, ...), custom_call_target="tpu_custom_call" | custom-call | tf_op jit(solution)/shard_map/pallas_call | solution.py:934
  458.4 1.6 copy-done.1
  460.0 1.2 copy-done.5
  461.2 6.0 shard_map.183.x
  467.2 0.8 copy-done.9
  468.0 24.2 %shard_map.184 = bf16[4,2,128,2048]{3,2,1,0:T(8,128)(2,1)} custom-call(bf16[128,2048]{1,0:T(8,128)(2,1)} %copy-done.9), custom_call_target="tpu_custom_call" | custom-call | tf_op jit(solution)/shard_map/pallas_call | solution.py:166
  492.3 3.6 convolution_convert_fusion.3
  495.9 5.1 fusion.10
  501.1 7.6 multiply_reduce_fusion
  508.7 1.4 copy-done.36
  510.1 10.0 %convolution_convert_fusion.1 = bf16[2048,512]{1,0:T(8,128)(2,1)} fusion(bf16[4096,2048]{1,0:T(8,128)(2,1)S(1)} %bitcast.141, bf16[4096,512]{1,0:T(8,128)(2,1)S(1)} %copy-done.36), kind=kOutput, calls=%fused_computation.14 | convolution fusion | flops 8590983168 | bytes 23068672 | tf_op jit(solution)/shard_map/dot_general | solution.py:705
  520.2 6.7 all-to-all-start.1
  526.8 7.0 multiply_convert_fusion
  533.9 1.5 convolution_bitcast_fusion
  535.5 0.9 broadcast_multiply_fusion.1
  536.6 0.8 copy-done.27
  538.2 1.6 copy.84.dp_
  539.8 4.6 convolution_convert_fusion.2.go
  544.4 4.9 convolution_convert_fusion.gq
  549.3 164.4 %shard_map.185 = (f32[128,2048]{1,0:T(8,128)}, f32[128,2048]{1,0:T(8,128)}, f32[64,6144]{1,0:T(8,128)}, f32[64,2048]{1,0:T(8,128)}) custom-call(bf16[4096,256]{1,0:T(8,128)(2,1)} %get-tuple-element.50.hid, bf16[256,2048]{1,0:T(8,128)(2,1)} %wo.5, bf16[1024,768]{1,0:T(8,128)(2,1)} %copy.84.dp_, bf16[2048,768]{1,0:T(8,128)(2,1)} %get-tuple-element.43.wq, ...), custom_call_target="tpu_custom_call" | custom-call | tf_op jit(solution)/shard_map/pallas_call | solution.py:667
  713.7 1.2 copy-done.3
  714.9 1.2 copy-done.6
  716.1 1.2 copy-done.12
  717.4 1.2 copy-done.13
  718.6 13.7 %shard_map.186 = (bf16[1,128,4,2048]{3,2,1,0:T(4,128)(2,1)}, f32[1,128,4,2048]{3,2,1,0:T(4,128)}, f32[40,128]{1,0:T(8,128)S(1)}) custom-call(f32[9,4]{1,0:T(8,128)S(1)} %concatenate.29.tab, f32[2,4]{1,0:T(2,128)S(1)} %copy-done.19, f32[2,4]{1,0:T(2,128)S(1)} %copy-done.18, bf16[4,128,2048]{2,1,0:T(8,128)(2,1)} %copy-done, bf16[4,128,2048]{2,1,0:T(8,128)(2,1)} %copy-done.4, ...), custom_call_target="tpu_custom_call" | custom-call | tf_op jit(solution)/shard_map/pallas_call | solution.py:1051
  732.9 28.4 %shard_map.187 = f32[40,128]{1,0:T(8,128)} custom-call(f32[40,128]{1,0:T(8,128)} %copy-done.17), custom_call_target="tpu_custom_call" | custom-call | tf_op jit(solution)/shard_map/pallas_call | solution.py:697
  761.3 0.8 reduce_sum.113
  763.0 0.7 bitcast_add_fusion.3
  764.3 0.6 bitcast_add_fusion.2
  766.3 9.5 %fusion.37 = f32[256,2048]{1,0:T(8,128)} fusion(bf16[4096,256]{1,0:T(8,128)(2,1)S(1)} %copy-done.20, bf16[4096,2048]{1,0:T(8,128)(2,1)} %bitcast.118), kind=kOutput, calls=%fused_computation.87 | convolution fusion | flops 4294967296 | bytes 20971520 | tf_op jit(solution)/shard_map/dot_general | solution.py:705
  775.8 5.4 reshape.330
  781.2 4.6 copy.70
  785.8 4.4 copy.86
  790.2 1.1 copy.89
  791.4 0.8 copy.90
  (101 shorter events, 6.4 us)
Async XLA Ops:
  5.6 4.8 copy-start.32
  5.6 5.0 copy-start.33
  5.6 5.0 copy-start.34
  29.7 1.4 copy-start.4
  31.0 0.8 copy-start.14
  31.8 0.8 copy-start.15
  32.6 221.3 %copy-start = (bf16[4,128,2048]{2,1,0:T(8,128)(2,1)}, bf16[4,128,2048]{2,1,0:T(8,128)(2,1)S(1)}, u32[]{:S(2)}) copy-start(bf16[4,128,2048]{2,1,0:T(8,128)(2,1)S(1)} %get-tuple-element.35.st) | copy-start | bytes 6291460
  111.1 146.5 %all-to-all-start = ((bf16[32,64,512]{2,1,0:T(8,128)(2,1)}), bf16[32,64,512]{2,1,0:T(8,128)(2,1)}, u32[]{:S(2)}, u32[]{:S(2)}) async-start(bf16[32,64,512]{2,1,0:T(8,128)(2,1)} %reshape.321), calls=%async_computation | async-start | bytes 4194304 | tf_op jit(solution)/shard_map/all_to_all | solution.py:1205
  135.8 1.7 copy-start.21
  135.8 1.7 copy-start.25
  138.9 9.9 %copy-start.23 = (bf16[1024,2,128]{0,2,1:T(8,128)(2,1)}, bf16[1024,2,128]{0,2,1:T(8,128)(2,1)S(1)}, u32[]{:S(2)}) copy-start(bf16[1024,2,128]{0,2,1:T(8,128)(2,1)S(1)} %get-tuple-element.67) | copy-start | bytes 1572868
  153.2 1.0 copy-start.29
  154.3 1.0 copy-start.8
  155.3 1.2 copy-start.10
  156.5 1.0 copy-start.16
  253.9 204.5 %copy-start.2 = (f32[128,2048]{1,0:T(8,128)}, f32[128,2048]{1,0:T(8,128)S(1)}, u32[]{:S(2)}) copy-start(f32[128,2048]{1,0:T(8,128)S(1)} %get-tuple-element.47.ba) | copy-start | bytes 3145732
  256.9 0.8 copy-start.7
  458.4 1.6 copy-start.1
  460.0 1.2 copy-start.5
  461.2 31.0 %copy-start.11 = (bf16[256,2048]{1,0:T(8,128)(2,1)S(1)}, bf16[256,2048]{1,0:T(8,128)(2,1)}, u32[]{:S(2)}) copy-start(bf16[256,2048]{1,0:T(8,128)(2,1)} %get-tuple-element.45.b) | copy-start | bytes 3145732
  467.2 0.8 copy-start.9
  492.3 8.7 %slice-start = ((s8[8388608]{0:T(1024)(128)(4,1)}), s8[4194304]{0:T(1024)(128)(4,1)S(1)}, s32[]{:S(2)}) async-start(s8[8388608]{0:T(1024)(128)(4,1)} %bitcast.121), calls=%async_computation.2 | async-start | bytes 8388608
  495.9 5.1 slice-start.1
  495.9 12.8 %slice-start.2 = ((s8[16777216]{0:T(1024)(128)(4,1)}), s8[4194304]{0:T(1024)(128)(4,1)S(1)}, s32[]{:S(2)}) async-start(s8[16777216]{0:T(1024)(128)(4,1)} %bitcast.139), calls=%async_computation.4 | async-start | bytes 8388608
  495.9 12.8 %slice-start.3 = ((s8[16777216]{0:T(1024)(128)(4,1)}), s8[4194304]{0:T(1024)(128)(4,1)S(1)}, s32[]{:S(2)}) async-start(s8[16777216]{0:T(1024)(128)(4,1)} %bitcast.139), calls=%async_computation.5 | async-start | bytes 8388608
  501.0 7.7 slice-start.4
  501.1 7.7 slice-start.5
  501.1 9.0 %copy-start.36 = (bf16[4096,512]{1,0:T(8,128)(2,1)S(1)}, bf16[4096,512]{1,0:T(8,128)(2,1)}, u32[]{:S(2)}) copy-start(bf16[4096,512]{1,0:T(8,128)(2,1)} %get-tuple-element.59) | copy-start | bytes 12582916
  520.2 255.6 %all-to-all-start.1 = ((bf16[32,64,512]{2,1,0:T(8,128)(2,1)}), bf16[32,64,512]{2,1,0:T(8,128)(2,1)}, u32[]{:S(2)}, u32[]{:S(2)}) async-start(bf16[32,64,512]{2,1,0:T(8,128)(2,1)} %bitcast.31), calls=%async_computation.1 | async-start | bytes 4194304 | tf_op jit(solution)/shard_map/all_to_all | solution.py:1231
  526.8 7.1 copy-start.26
  533.9 1.6 copy-start.22
  533.9 1.6 copy-start.24
  536.4 1.0 copy-start.27
  538.0 1.8 copy-start.30
  539.8 4.6 copy-start.35
  549.3 164.4 %copy-start.18 = (f32[2,4]{1,0:T(2,128)S(1)}, f32[2,4]{1,0:T(2,128)}, u32[]{:S(2)}) copy-start(f32[2,4]{1,0:T(2,128)} %dep.1) | copy-start | bytes 100
  549.3 164.4 %copy-start.19 = (f32[2,4]{1,0:T(2,128)S(1)}, f32[2,4]{1,0:T(2,128)}, u32[]{:S(2)}) copy-start(f32[2,4]{1,0:T(2,128)} %mi.1) | copy-start | bytes 100
  713.7 1.2 copy-start.3
  714.9 1.2 copy-start.6
  716.1 1.2 copy-start.12
  717.4 1.2 copy-start.13
  718.6 47.7 %copy-start.20 = (bf16[4096,256]{1,0:T(8,128)(2,1)S(1)}, bf16[4096,256]{1,0:T(8,128)(2,1)}, u32[]{:S(2)}) copy-start(bf16[4096,256]{1,0:T(8,128)(2,1)} %get-tuple-element.50.hid) | copy-start | bytes 6291460
  732.3 0.6 copy-start.17
  785.8 4.4 copy-start.28
  785.8 5.5 copy-start.31
